TPU v7x, 256 devices: a whole 4x4x8 slice. The times are simulated.
256 devices in a mesh: ctx: 8 (over z), tp: 4 (over y_lo, core), dp: 8 (over x, y_hi).
Axes of the slice: x: 4, y: 4 (y_hi: 2, y_lo: 2; y = y_hi * 2 + y_lo), z: 8, core: 2. Of those that a mesh axis runs over, the one named last changes fastest.
Arguments:
- tokens: bfloat16 [8, 2, 2048, 4096], P('dp', None, 'ctx')
- norm_gain: float32 [4096], replicated, as said below
- query_weight: bfloat16 [4096, 2048], P(('ctx', 'dp'), 'tp'), may hold values from -0.09375 to 0.09375
- key_weight: bfloat16 [4096, 512], P(('ctx', 'dp'), 'tp'), may hold values from -0.09375 to 0.09375
- value_weight: bfloat16 [4096, 512], P(('ctx', 'dp'), 'tp'), may hold values from -0.09375 to 0.09375
- output_weight: bfloat16 [2048, 4096], P(None, ('tp', 'ctx', 'dp')), may hold values from -0.125 to 0.125
- query_noise: bfloat16 [4096, 2048], P(('ctx', 'dp'), 'tp'), may hold values from -6 to 6
- key_noise: bfloat16 [4096, 512], P(('ctx', 'dp'), 'tp'), may hold values from -6 to 6
- value_noise: bfloat16 [4096, 512], P(('ctx', 'dp'), 'tp'), may hold values from -6 to 6
- output_noise: bfloat16 [2048, 4096], P(None, ('tp', 'ctx', 'dp')), may hold values from -6 to 6
- sign: int32 [2], replicated, may hold values from -1 to 1, as said below
- segment_ids: int32 [8, 2, 2048], P('dp', None, 'ctx'), may hold values from 0 to 3, as said below
- doc_weight: float32 [8], P('dp'), may hold values from 0.5 to 8
Outputs:
- branch: bfloat16 [8, 2, 2048, 4096], P('dp', None, 'ctx', 'tp')
- loss: float32 [1], replicated
Inputs may be any that keep to these rules, and one draw needn't show every extreme that they name: `segment_ids`: read in natural position order, each sequence's ids never fall, begin at 0 and end at 3. `sign`: the two entries are opposite, each -1 or 1. `norm_gain`: Positive.
All inputs are finite; a program needn't handle non-finite values.
Results may differ from a plain program's by a relative error of at most 0.017.
The roundings to bfloat16 on the way count: a program that leaves them out, or rounds other values in their place, can miss the bound.
Values may be sent and summed in bfloat16 or wider, within the bound.
No kernel may reach another device: no remote copies, remote signals or barrier semaphores. Data moves between devices by JAX's collectives and lax.ppermute only.
A program may use at most 128 MiB of HBM per device.

v0:
```python
import jax
import jax.numpy as jnp
from jax import lax
from jax.sharding import PartitionSpec as P

D = 4096
HD = 128


perturb_step = 0.004
rope_base = 500000.0
norm_epsilon = 1e-05
masked_score = -1e30


def perturbed(weight, noise, factor):
    return (weight.astype(jnp.float32) + factor * noise.astype(jnp.float32)).astype(jnp.bfloat16)


def rotate(values, positions):
    head_size = values.shape[-1]
    half_size = head_size // 2
    inverse = rope_base ** (-jnp.arange(half_size, dtype=jnp.float32) * 2.0 / head_size)
    angles = positions.astype(jnp.float32)[:, None] * inverse[None, :]
    extra = (1,) * (values.ndim - 2)
    cosine = jnp.cos(angles).reshape(angles.shape[:1] + extra + angles.shape[1:])
    sine = jnp.sin(angles).reshape(angles.shape[:1] + extra + angles.shape[1:])
    first_half = values[..., :half_size]
    second_half = values[..., half_size:]
    return jnp.concatenate(
        [first_half * cosine - second_half * sine, second_half * cosine + first_half * sine],
        axis=-1,
    )


def shards(
    tokens,
    norm_gain,
    query_weight,
    key_weight,
    value_weight,
    output_weight,
    query_noise,
    key_noise,
    value_noise,
    output_noise,
    sign,
    segment_ids,
    doc_weight,
):
    factor = sign[0].astype(jnp.float32) * perturb_step
    half_rows = tokens.shape[2]
    model_width = tokens.shape[3]
    local_rows = 2 * half_rows
    ctx_index = lax.axis_index("ctx")
    seq_len = 2 * half_rows * lax.axis_size("ctx")
    tp_count = lax.axis_size("tp")
    head_size = HD
    kv_heads = key_weight.shape[1] // head_size
    query_heads = query_weight.shape[1] // head_size
    group = query_heads // kv_heads
    scale = 1.0 / HD**0.5
    offsets = jnp.arange(half_rows, dtype=jnp.int32)
    local_pos = jnp.concatenate(
        [ctx_index * half_rows + offsets, seq_len - (ctx_index + 1) * half_rows + offsets]
    )
    local_seg = segment_ids[0].reshape(local_rows)
    rows_f = tokens[0].reshape(local_rows, model_width).astype(jnp.float32)
    normed = (
        rows_f
        * lax.rsqrt(jnp.mean(rows_f * rows_f, axis=-1, keepdims=True) + norm_epsilon)
        * norm_gain
    ).astype(jnp.bfloat16)
    formed = (
        perturbed(
            lax.all_gather(query_weight, ("ctx", "dp"), axis=0, tiled=True),
            lax.all_gather(query_noise, ("ctx", "dp"), axis=0, tiled=True),
            factor,
        ),
        perturbed(
            lax.all_gather(key_weight, ("ctx", "dp"), axis=0, tiled=True),
            lax.all_gather(key_noise, ("ctx", "dp"), axis=0, tiled=True),
            factor,
        ),
        perturbed(
            lax.all_gather(value_weight, ("ctx", "dp"), axis=0, tiled=True),
            lax.all_gather(value_noise, ("ctx", "dp"), axis=0, tiled=True),
            factor,
        ),
    )
    query_sum, key_sum, value_sum = tuple(
        (jnp.dot(normed, weight_rows, preferred_element_type=jnp.float32) for weight_rows in formed)
    )
    queries = rotate(query_sum.reshape(local_rows, kv_heads, group, head_size), local_pos).astype(
        jnp.bfloat16
    )
    keys_local = rotate(key_sum.reshape(local_rows, kv_heads, head_size), local_pos).astype(
        jnp.bfloat16
    )
    values_local = value_sum.astype(jnp.bfloat16)
    key_fold = keys_local.reshape(2, half_rows, kv_heads * head_size)
    value_fold = values_local.reshape(2, half_rows, kv_heads * head_size)
    seg_fold = segment_ids[0].astype(jnp.bfloat16)

    def attend(state, block):
        block_keys, block_values, block_pos, block_seg = block
        allowed = (block_pos[None, :] <= local_pos[:, None]) & (
            block_seg[None, :] == local_seg[:, None]
        )
        highest, totals, accum = state
        scores = (
            jnp.einsum("rhgd,khd->hgrk", queries, block_keys, preferred_element_type=jnp.float32)
            * scale
        )
        limited = jnp.where(allowed, scores, masked_score)
        new_high = jnp.maximum(highest, jnp.max(limited, axis=-1))
        shrink = jnp.exp(highest - new_high)
        weights = jnp.where(allowed, jnp.exp(scores - new_high[..., None]), 0.0)
        new_totals = totals * shrink + jnp.sum(weights, axis=-1)
        added = jnp.einsum(
            "hgrk,khd->hgrd",
            weights.astype(jnp.bfloat16),
            block_values,
            preferred_element_type=jnp.float32,
        )
        return (new_high, new_totals, accum * shrink[..., None] + added)

    start_state = (
        jnp.full((kv_heads, group, local_rows), masked_score, jnp.float32),
        jnp.zeros((kv_heads, group, local_rows), jnp.float32),
        jnp.zeros((kv_heads, group, local_rows, head_size), jnp.float32),
    )
    key_part = lax.all_gather(key_fold, "ctx", axis=1, tiled=True)
    value_part = lax.all_gather(value_fold, "ctx", axis=1, tiled=True)
    seg_part = lax.all_gather(seg_fold, "ctx", axis=1, tiled=True)
    count = key_part.shape[1]
    positions = jnp.arange(count, dtype=jnp.int32)
    inner = positions % half_rows
    later = seq_len - half_rows - positions + 2 * inner
    key_pos = jnp.concatenate([positions, later])
    blocks_count = 2 * count // half_rows
    stacked = (
        key_part.reshape(blocks_count, half_rows, kv_heads, head_size),
        value_part.reshape(blocks_count, half_rows, kv_heads, head_size),
        key_pos.reshape(blocks_count, half_rows),
        seg_part.reshape(blocks_count, half_rows).astype(jnp.int32),
    )

    def scan_step(current, block):
        return (attend(current, block), None)

    result, _ = lax.scan(scan_step, start_state, stacked)
    highest, totals, accum = result
    mixed = accum / totals[..., None]
    attention = (
        jnp.transpose(mixed, (2, 0, 1, 3))
        .reshape(local_rows, query_heads * head_size)
        .astype(jnp.bfloat16)
    )
    out_stack = jnp.stack([output_weight, output_noise])
    own_rows = lax.all_to_all(out_stack, "tp", split_axis=1, concat_axis=2, tiled=True)
    piece = lax.all_gather(own_rows, ("ctx", "dp"), axis=2, tiled=True)
    terms = jnp.dot(
        attention, perturbed(piece[0], piece[1], factor), preferred_element_type=jnp.float32
    )
    shard_count = terms.shape[1] // model_width * 0 + model_width // (
        tp_count * output_weight.shape[1]
    )
    terms = terms.reshape(local_rows, shard_count, tp_count, output_weight.shape[1])
    terms = jnp.transpose(terms, (0, 2, 1, 3)).reshape(local_rows, model_width)
    summed = lax.psum_scatter(terms.astype(jnp.bfloat16), "tp", scatter_dimension=1, tiled=True)
    local_total = jnp.sum(jnp.square(summed.astype(jnp.float32))) * doc_weight[0]
    loss = lax.psum(local_total, ("ctx", "tp", "dp")) / (seq_len * D)
    return (summed.reshape(1, 2, half_rows, summed.shape[1]), loss.reshape(1))


def solution(mesh):
    return jax.shard_map(
        shards,
        mesh=mesh,
        in_specs=(
            P("dp", None, "ctx", None),
            P(),
            P(("ctx", "dp"), "tp"),
            P(("ctx", "dp"), "tp"),
            P(("ctx", "dp"), "tp"),
            P(None, ("tp", "ctx", "dp")),
            P(("ctx", "dp"), "tp"),
            P(("ctx", "dp"), "tp"),
            P(("ctx", "dp"), "tp"),
            P(None, ("tp", "ctx", "dp")),
            P(),
            P("dp", None, "ctx"),
            P("dp"),
        ),
        out_specs=(P("dp", None, "ctx", "tp"), P()),
        check_vma=False,
    )
```

profile of v0, /device:TPU:1, one launch (start us, length us, event | category | flops | bytes accessed | tf_op | source)
XLA Modules:
  0.0 1103.1 jit_solution(1531369920302911167)
XLA Ops:
  13.8 5.8 fusion.24
  19.6 105.2 %all-gather.11.cloned.1.call-done = bf16[4096,128]{1,0:T(8,128)(2,1)} async-done(((bf16[64,128]{1,0:T(8,128)(2,1)}), bf16[4096,128]{1,0:T(8,128)(2,1)}) %all-gather.11.cloned.1.call-update) | async-done | bytes 1048592 | tf_op jit(solution)/shard_map/all_gather | solution.py:81
  124.8 114.2 %all-gather.13.cloned.1.call-done = bf16[4096,128]{1,0:T(8,128)(2,1)} async-done(((bf16[64,128]{1,0:T(8,128)(2,1)}), bf16[4096,128]{1,0:T(8,128)(2,1)}) %all-gather.13.cloned.1.call-update) | async-done | bytes 1048592 | tf_op jit(solution)/shard_map/all_gather | solution.py:82
  238.9 4.3 convolution_bitcast_fusion.2
  246.1 107.0 %all-gather.21.cloned.1.call-done = bf16[4096,128]{1,0:T(8,128)(2,1)} async-done(((bf16[64,128]{1,0:T(8,128)(2,1)}), bf16[4096,128]{1,0:T(8,128)(2,1)}) %all-gather.21.cloned.1.call-update) | async-done | bytes 1048592 | tf_op jit(solution)/shard_map/all_gather | solution.py:86
  353.1 114.0 %all-gather.23.cloned.1.call-done = bf16[4096,128]{1,0:T(8,128)(2,1)} async-done(((bf16[64,128]{1,0:T(8,128)(2,1)}), bf16[4096,128]{1,0:T(8,128)(2,1)}) %all-gather.23.cloned.1.call-update) | async-done | bytes 1048592 | tf_op jit(solution)/shard_map/all_gather | solution.py:87
  467.1 4.7 convolution_convert_fusion
  474.4 8.3 all-to-all-start
  482.7 11.7 %all-gather = bf16[1,2,2048]{2,1,0:T(2,128)(2,1)S(1)} all-gather(bf16[1,2,256]{2,1,0:T(2,128)(2,1)S(1)} %convert_element_type.123), channel_id=2, replica_groups=mesh['ctx'=8,'tp'=4,'dp'=8] {'ctx'}, dimensions={2}, use_global_device_ids=true | all-gather | bytes 9216 | tf_op jit(solution)/shard_map/all_gather | solution.py:135
  495.1 5.8 multiply_convert_fusion
  506.0 3.7 copy.52
  509.6 127.4 %all-gather.17.cloned.1.call-done = bf16[4096,512]{1,0:T(8,128)(2,1)} async-done(((bf16[64,512]{1,0:T(8,128)(2,1)}), bf16[4096,512]{1,0:T(8,128)(2,1)}) %all-gather.17.cloned.1.call-update) | async-done | bytes 4194320 | tf_op jit(solution)/shard_map/all_gather | solution.py:76
  637.0 127.8 %all-gather.19.cloned.1.call-done = bf16[4096,512]{1,0:T(8,128)(2,1)} async-done(((bf16[64,512]{1,0:T(8,128)(2,1)}), bf16[4096,512]{1,0:T(8,128)(2,1)}) %all-gather.19.cloned.1.call-update) | async-done | bytes 4194320 | tf_op jit(solution)/shard_map/all_gather | solution.py:77
  764.8 6.7 fusion.25
  771.5 6.4 copy.65
  777.9 5.8 convolution_bitcast_fusion.1
  785.0 15.2 %all-gather.25.cloned.1.call-done = bf16[2,2048,128]{2,1,0:T(8,128)(2,1)} async-done(((bf16[2,256,128]{2,1,0:T(8,128)(2,1)}), bf16[2,2048,128]{2,1,0:T(8,128)(2,1)}) %all-gather.25.cloned.1.call-update) | async-done | bytes 1048592 | tf_op jit(solution)/shard_map/all_gather | solution.py:134
  800.2 67.1 %while.15 = (s32[]{:T(128)}, f32[1,4,512]{2,1,0:T(4,128)S(1)}, f32[1,4,512]{2,1,0:T(4,128)S(1)}, f32[1,4,512,128]{3,2,1,0:T(8,128)S(1)}, s32[16,256]{1,0:T(8,128...) while((s32[]{:T(128)}, f32[1,4,512]{2,1,0:T(4,128)S(1)}, ...), condition=%wide.region_4.5_spmd.clone, body=%wide.region_1.4_spmd.clone.sunk | while | flops 275394560 | bytes 9714829 | solution.py:152
  867.8 84.4 %all-gather.27.cloned.1.call-done = bf16[2,512,4096]{1,2,0:T(8,128)(2,1)} async-done(((bf16[2,512,64]{1,2,0:T(8,128)(2,1)}), bf16[2,512,4096]{1,2,0:T(8,128)(2,1)}) %all-gather.27.cloned.1.call-update) | async-done | bytes 8388624 | tf_op jit(solution)/shard_map/all_gather | solution.py:162
  952.2 4.3 add_convert_fusion
  956.6 3.4 convert_bitcast_fusion
  960.0 4.3 copy.61
  965.0 47.2 %reduce-scatter.2.cloned.1.call-done = bf16[512,1024]{0,1:T(8,128)(2,1)} async-done(((bf16[512,4096]{0,1:T(8,128)(2,1)}), bf16[512,1024]{0,1:T(8,128)(2,1)}) %reduce-scatter.2.cloned.1.call-update) | async-done | bytes 1048592 | tf_op jit(solution)/shard_map/reduce_scatter | solution.py:171
  1015.2 77.0 %psum.7 = f32[]{:T(128)} all-reduce(f32[]{:T(128)S(6)} %mul.222), channel_id=1, replica_groups=mesh['ctx'=8,'tp'=4,'dp'=8] {'ctx','tp','dp'}, use_global_device_ids=true, to_apply=%region_7.8 | all-reduce | flops 1 | bytes 8 | tf_op jit(solution)/shard_map/psum | solution.py:173
  (206 shorter events, 89.2 us)
Async XLA Ops:
  7.2 6.7 copy-start.1
  7.2 117.6 %all-gather.11.cloned.1.call-start = ((), (), s32[]{:S(2)}) async-start(), calls=%async_computation.2 | async-start | bytes 1064960 | tf_op jit(solution)/shard_map/all_gather | solution.py:81
  7.9 231.0 %all-gather.13.cloned.1.call-start = ((), (), s32[]{:S(2)}) async-start(), calls=%async_computation.3 | async-start | bytes 1064960 | tf_op jit(solution)/shard_map/all_gather | solution.py:82
  8.7 344.5 %all-gather.21.cloned.1.call-start = ((), (), s32[]{:S(2)}) async-start(), calls=%async_computation.7 | async-start | bytes 1064960 | tf_op jit(solution)/shard_map/all_gather | solution.py:86
  9.4 457.7 %all-gather.23.cloned.1.call-start = ((), (), s32[]{:S(2)}) async-start(), calls=%async_computation.8 | async-start | bytes 1064960 | tf_op jit(solution)/shard_map/all_gather | solution.py:87
  10.0 496.0 %all-gather.15.cloned.1.call-start = ((), (), s32[]{:S(2)}) async-start(), calls=%async_computation.4 | async-start | bytes 1179648 | tf_op jit(solution)/shard_map/all_gather | solution.py:133
  243.3 228.6 %copy-start.2 = (bf16[2048,16]{0,1:T(8,128)(2,1)S(1)}, bf16[2048,16]{0,1:T(8,128)(2,1)}, u32[]{:S(2)}) copy-start(bf16[2048,16]{0,1:T(8,128)(2,1)} %param.24) | copy-start | bytes 196612
  243.3 228.6 %copy-start.3 = (bf16[2048,16]{0,1:T(8,128)(2,1)S(1)}, bf16[2048,16]{0,1:T(8,128)(2,1)}, u32[]{:S(2)}) copy-start(bf16[2048,16]{0,1:T(8,128)(2,1)} %param.20) | copy-start | bytes 196612
  244.8 392.3 %all-gather.17.cloned.1.call-start = ((), (), s32[]{:S(2)}) async-start(), calls=%async_computation.5 | async-start | bytes 4259840 | tf_op jit(solution)/shard_map/all_gather | solution.py:76
  245.3 519.5 %all-gather.19.cloned.1.call-start = ((), (), s32[]{:S(2)}) async-start(), calls=%async_computation.6 | async-start | bytes 4259840 | tf_op jit(solution)/shard_map/all_gather | solution.py:77
  246.1 236.6 %copy-start = (s32[1,2,256]{2,1,0:T(2,128)S(1)}, s32[1,2,256]{2,1,0:T(2,128)}, u32[]{:S(2)}) copy-start(s32[1,2,256]{2,1,0:T(2,128)} %param.26) | copy-start | bytes 6148
  246.1 554.1 %all-gather.25.cloned.1.call-start = ((), (), s32[]{:S(2)}) async-start(), calls=%async_computation.9 | async-start | bytes 1179648 | tf_op jit(solution)/shard_map/all_gather | solution.py:134
  474.4 26.5 %all-to-all-start = ((bf16[4,2,8192]{2,1,0:T(2,128)(2,1)}), bf16[4,2,8192]{2,1,0:T(2,128)(2,1)S(1)}, u32[]{:S(2)}, u32[]{:S(2)}) async-start(bf16[4,2,8192]{2,1,0:T(2,128)(2,1)} %reshape.333), calls=%async_computation | async-start | bytes 262144 | tf_op jit(solution)/shard_map/all_to_all | solution.py:161
  482.7 469.5 %all-gather.27.cloned.1.call-start = ((), (), s32[]{:S(2)}) async-start(), calls=%async_computation.10 | async-start | bytes 8519680 | tf_op jit(solution)/shard_map/all_gather | solution.py:162
  503.0 509.2 %reduce-scatter.2.cloned.1.call-start = ((), (), s32[]{:S(2)}) async-start(), calls=%async_computation.11 | async-start | bytes 5242880 | tf_op jit(solution)/shard_map/reduce_scatter | solution.py:171
Sparse Core Ops, SparseCore 0:
  11.6 113.1 all-gather.10
  128.4 110.5 all-gather.12
  242.5 110.5 all-gather.20
  356.6 110.5 all-gather.22
  469.3 36.6 all-gather.14
  509.3 127.6 all-gather.16
  640.5 124.2 all-gather.18
  766.6 33.5 all-gather.24
  803.7 148.4 all-gather.26
  964.5 47.6 reduce-scatter.1
where the time goes:
time: 1100 us
  waiting for transfers between devices  849 us (77%)
  blocking collectives  88.7 us (8%)
  matrix products  73.1 us (7%)
  other arithmetic  41.2 us (4%)
  local copies, waits for them, and re-layouts  23 us (2%)
  between operations  18.1 us (2%)
    all_gather x1, waiting for transfers between devices, shards(): lax.all_gather(query_noise, ('ctx', 'dp'), axis=0, tiled=True)  128 us
    all_gather x1, waiting for transfers between devices, shards(): lax.all_gather(query_weight, ('ctx', 'dp'), axis=0, tiled=True)  127 us
    all_gather x1, waiting for transfers between devices, shards(): lax.all_gather(key_noise, ('ctx', 'dp'), axis=0, tiled=True)  114 us
    all_gather x1, waiting for transfers between devices, shards(): lax.all_gather(value_noise, ('ctx', 'dp'), axis=0, tiled=True)  114 us
    all_gather x1, waiting for transfers between devices, shards(): lax.all_gather(value_weight, ('ctx', 'dp'), axis=0, tiled=True)  107 us
    all_gather x1, waiting for transfers between devices, shards(): lax.all_gather(key_weight, ('ctx', 'dp'), axis=0, tiled=True)  105 us
    all_gather x1, waiting for transfers between devices, shards(): piece = lax.all_gather(own_rows, ('ctx', 'dp'), axis=2, tiled=True)  84.4 us
    psum x1, blocking collectives, shards(): loss = lax.psum(local_total, ('ctx', 'tp', 'dp')) / (seq_len * D)  77 us
  transfers between devices with their start and end apart: 11, of which 10 were waited for; matrix products, arithmetic and copies ran while one was open for 11% of the time, Pallas kernels for 0%

commit v1 on v0

v1 whole, which is shorter than its diff:
```python
import jax
import jax.numpy as jnp
from jax import lax
from jax.experimental import pallas as pl
from jax.experimental.pallas import tpu as pltpu
from jax.sharding import PartitionSpec as P

HD = 128

perturb_step = 0.004
rope_base = 500000.0
norm_epsilon = 1e-05
masked_score = -1e30


def perturbed(weight, noise, factor):
    return (weight.astype(jnp.float32) + factor * noise.astype(jnp.float32)).astype(jnp.bfloat16)


def dot_dims(lhs, rhs, dims):
    return lax.dot_general(lhs, rhs, (dims, ((), ())), preferred_element_type=jnp.float32)


def rope_tables(positions):
    half = HD // 2
    inverse = rope_base ** (-jnp.arange(half, dtype=jnp.float32) * 2.0 / HD)
    angles = positions.astype(jnp.float32)[:, None] * inverse[None, :]
    cosine = jnp.cos(angles)
    sine = jnp.sin(angles)
    return (
        jnp.concatenate([cosine, cosine], axis=1),
        jnp.concatenate([-sine, sine], axis=1),
    )


def project_kernel(normed_ref, weight_ref, cos_ref, sin_ref, out_ref, *, turned):
    sums = jnp.dot(normed_ref[...], weight_ref[...], preferred_element_type=jnp.float32)
    cosine = cos_ref[...]
    sine = sin_ref[...]
    for head in range(sums.shape[1] // HD):
        part = sums[:, head * HD : (head + 1) * HD]
        if head < turned:
            part = part * cosine + pltpu.roll(part, HD // 2, 1) * sine
        out_ref[:, head * HD : (head + 1) * HD] = part.astype(jnp.bfloat16)


def project(normed, weight, cosine, sine, width, turned, rows=128):
    count, model_width = normed.shape
    return pl.pallas_call(
        lambda *refs: project_kernel(*refs, turned=turned),
        grid=(count // rows,),
        in_specs=[
            pl.BlockSpec((rows, model_width), lambda i: (i, 0)),
            pl.BlockSpec((model_width, width), lambda i: (0, 0)),
            pl.BlockSpec((rows, HD), lambda i: (i, 0)),
            pl.BlockSpec((rows, HD), lambda i: (i, 0)),
        ],
        out_specs=pl.BlockSpec((rows, width), lambda i: (i, 0)),
        out_shape=jax.ShapeDtypeStruct((count, width), jnp.bfloat16),
        name="project",
    )(normed, weight, cosine, sine)


def attend_kernel(place_ref, query_ref, kv_ref, first_ref, out_ref, *, half_rows, heads, blocks):
    which = pl.program_id(0)
    queries = jnp.concatenate(
        [query_ref[0, :, h * HD : (h + 1) * HD] for h in range(heads)], axis=0
    )
    rows = heads * half_rows
    scale = 1.0 / HD**0.5
    first = first_ref[0]
    ctx = place_ref[0]
    own = jnp.where(which == 0, ctx, blocks - 1 - ctx)
    low = place_ref[1 + which]
    key_iota = lax.broadcasted_iota(jnp.int32, (half_rows, rows), 0)
    query_pos = own * half_rows + lax.rem(
        lax.broadcasted_iota(jnp.int32, (1, rows), 1), half_rows
    )

    def step(block, state):
        highest, totals, accum = state
        second = block >= blocks // 2
        holder = jnp.where(second, blocks - 1 - block, block)
        half = jnp.where(second, 1, 0)
        keys = kv_ref[holder, half, :half_rows, :HD]
        values = kv_ref[holder, half, :half_rows, HD : 2 * HD]
        scores = dot_dims(keys, queries, ((1,), (1,))) * scale
        key_pos = block * half_rows + key_iota
        allowed = (key_pos <= query_pos) & (key_pos >= first)
        limited = jnp.where(allowed, scores, masked_score)
        new_high = jnp.maximum(highest, jnp.max(limited, axis=0, keepdims=True))
        shrink = jnp.exp(highest - new_high)
        weights = jnp.where(allowed, jnp.exp(scores - new_high), 0.0)
        new_totals = totals * shrink + jnp.sum(weights, axis=0, keepdims=True)
        added = dot_dims(values, weights.astype(jnp.bfloat16), ((0,), (0,)))
        return (new_high, new_totals, accum * shrink + added)

    start = (
        jnp.full((1, rows), masked_score, jnp.float32),
        jnp.zeros((1, rows), jnp.float32),
        jnp.zeros((HD, rows), jnp.float32),
    )
    _, totals, accum = lax.fori_loop(low, own + 1, step, start)
    mixed = (accum / totals).astype(jnp.bfloat16)
    for h in range(heads):
        out_ref[0, :, h * HD : (h + 1) * HD] = mixed[:, h * half_rows : (h + 1) * half_rows].T


def attend(place, queries, kv, first, half_rows, heads, blocks):
    width = heads * HD
    return pl.pallas_call(
        lambda *refs: attend_kernel(*refs, half_rows=half_rows, heads=heads, blocks=blocks),
        grid_spec=pltpu.PrefetchScalarGridSpec(
            num_scalar_prefetch=1,
            grid=(2,),
            in_specs=[
                pl.BlockSpec((1, half_rows, width), lambda i, _: (i, 0, 0)),
                pl.BlockSpec(kv.shape, lambda i, _: (0, 0, 0, 0)),
                pl.BlockSpec((1, 1, heads * half_rows), lambda i, _: (i, 0, 0)),
            ],
            out_specs=pl.BlockSpec((1, half_rows, width), lambda i, _: (i, 0, 0)),
        ),
        out_shape=jax.ShapeDtypeStruct((2, half_rows, width), jnp.bfloat16),
        name="attend",
    )(place, queries, kv, first)


def blend_kernel(mixed_ref, weight_ref, out_ref, square_ref):
    owners = mixed_ref.shape[0]
    width = mixed_ref.shape[2]
    total = None
    for owner in range(owners):
        term = dot_dims(
            mixed_ref[owner], weight_ref[:, owner * width : (owner + 1) * width], ((1,), (1,))
        )
        term = term.astype(jnp.bfloat16).astype(jnp.float32)
        total = term if total is None else total + term
    branch = total.astype(jnp.bfloat16)
    out_ref[...] = branch
    square = jnp.square(branch.astype(jnp.float32))
    part = jnp.sum(square.reshape(-1, 8, square.shape[1]), axis=0)

    @pl.when(pl.program_id(0) == 0)
    def _():
        square_ref[...] = jnp.zeros_like(square_ref)

    square_ref[...] += part


def blend(mixed, weight, rows=128):
    owners, count, width = mixed.shape
    features = weight.shape[0]
    return pl.pallas_call(
        blend_kernel,
        grid=(count // rows,),
        in_specs=[
            pl.BlockSpec((owners, rows, width), lambda i: (0, i, 0)),
            pl.BlockSpec(weight.shape, lambda i: (0, 0)),
        ],
        out_specs=[
            pl.BlockSpec((rows, features), lambda i: (i, 0)),
            pl.BlockSpec((8, features), lambda i: (0, 0)),
        ],
        out_shape=[
            jax.ShapeDtypeStruct((count, features), jnp.bfloat16),
            jax.ShapeDtypeStruct((8, features), jnp.float32),
        ],
        name="blend",
    )(mixed, weight)


def shards(
    tokens,
    norm_gain,
    query_weight,
    key_weight,
    value_weight,
    output_weight,
    query_noise,
    key_noise,
    value_noise,
    output_noise,
    sign,
    segment_ids,
    doc_weight,
):
    factor = sign[0].astype(jnp.float32) * perturb_step
    half_rows = tokens.shape[2]
    model_width = tokens.shape[3]
    local_rows = 2 * half_rows
    ctx = lax.axis_index("ctx")
    ctx_count = lax.axis_size("ctx")
    seq_len = local_rows * ctx_count
    blocks = 2 * ctx_count
    heads = query_weight.shape[1] // HD
    width = heads * HD

    own_qkv = perturbed(
        jnp.concatenate([query_weight, key_weight, value_weight], axis=1),
        jnp.concatenate([query_noise, key_noise, value_noise], axis=1),
        factor,
    )
    own_out = perturbed(output_weight, output_noise, factor).T
    qkv_weight = lax.all_gather(own_qkv, ("ctx", "dp"), axis=0, tiled=True)

    rows_f = tokens[0].reshape(local_rows, model_width).astype(jnp.float32)
    normed = (
        rows_f
        * lax.rsqrt(jnp.mean(rows_f * rows_f, axis=-1, keepdims=True) + norm_epsilon)
        * norm_gain
    ).astype(jnp.bfloat16)
    offsets = jnp.arange(half_rows, dtype=jnp.int32)
    local_pos = jnp.concatenate(
        [ctx * half_rows + offsets, seq_len - (ctx + 1) * half_rows + offsets]
    )
    cosine, sine = rope_tables(local_pos)

    qkv = project(normed, qkv_weight, cosine, sine, width + 2 * HD, heads + 1)
    queries = qkv[:, :width].reshape(2, half_rows, width)
    kv_own = qkv[:, width:].reshape(2, half_rows, 2 * HD)
    seg_rows = segment_ids[0].astype(jnp.bfloat16).reshape(2, half_rows // (2 * HD), 2 * HD)
    pad = jnp.zeros((2, 16 - seg_rows.shape[1], 2 * HD), jnp.bfloat16)
    parcel = jnp.concatenate([kv_own, seg_rows, pad], axis=1)
    kv = lax.all_gather(parcel, "ctx", axis=0)

    all_seg = kv[:, :, half_rows, :]
    doc_first = jnp.sum(
        (all_seg[None] < jnp.arange(4, dtype=jnp.bfloat16)[:, None, None, None]).astype(jnp.int32),
        axis=(1, 2, 3),
    )
    first = jnp.zeros((2, half_rows), jnp.int32)
    for doc in range(1, 4):
        first = jnp.where(segment_ids[0] == doc, doc_first[doc], first)
    low = jnp.min(first, axis=1) // half_rows
    place = jnp.concatenate([ctx.reshape(1), low]).astype(jnp.int32)
    first = jnp.tile(first, (1, heads)).reshape(2, 1, heads * half_rows)
    mixed = attend(place, queries, kv, first, half_rows, heads, blocks)

    mixed_all = lax.all_gather(mixed.reshape(local_rows, width), "tp", axis=0)
    out_weight = lax.all_gather(own_out, ("ctx", "dp"), axis=0, tiled=True)
    branch, squares = blend(mixed_all, out_weight)
    local_total = jnp.sum(squares) * doc_weight[0]
    loss = lax.psum(local_total, ("ctx", "tp", "dp")) / (seq_len * model_width)
    return (branch.reshape(1, 2, half_rows, branch.shape[1]), loss.reshape(1))


def solution(mesh):
    return jax.shard_map(
        shards,
        mesh=mesh,
        in_specs=(
            P("dp", None, "ctx", None),
            P(),
            P(("ctx", "dp"), "tp"),
            P(("ctx", "dp"), "tp"),
            P(("ctx", "dp"), "tp"),
            P(None, ("tp", "ctx", "dp")),
            P(("ctx", "dp"), "tp"),
            P(("ctx", "dp"), "tp"),
            P(("ctx", "dp"), "tp"),
            P(None, ("tp", "ctx", "dp")),
            P(),
            P("dp", None, "ctx"),
            P("dp"),
        ),
        out_specs=(P("dp", None, "ctx", "tp"), P()),
        check_vma=False,
    )
```

time: 1100 us -> 460 us (0.42)
  waiting for transfers between devices: 849 us -> 313 us
  matrix products: 73.1 us -> 0 us
  Pallas kernels: 0 us -> 26.3 us
  other arithmetic: 41.2 us -> 19.7 us
  local copies, waits for them, and re-layouts: 23 us -> 5.1 us
  blocking collectives: 88.7 us -> 77 us
    all_gather x9 -> x4, waiting for transfers between devices: 798 us -> 313 us  [the longest x1 128 us: shards(): qkv_weight = lax.all_gather(own_qkv, ('ctx', 'dp'), axis=0, tiled=True)]
    dot_general x36 -> x0, matrix products: 73.1 us -> none  [the longest x16 29.2 us: attend(): jnp.einsum('hgrk,khd->hgrd', weights.astype(jnp.bfloat16), block_values,...]
    reduce_scatter x1 -> x0, waiting for transfers between devices: 47.2 us -> none  [shards(): lax.psum_scatter(terms.astype(jnp.bfloat16), 'tp', scatter_dimension=1, t...]
    pallas_call x0 -> x3, Pallas kernels: none -> 26.3 us  [the longest x1 9.23 us: blend(): pl.pallas_call(blend_kernel, grid=(count // rows,), in_specs=[pl.BlockSpe...]
    all_gather x1 -> x0, blocking collectives: 11.7 us -> none  [shards(): seg_part = lax.all_gather(seg_fold, 'ctx', axis=1, tiled=True)]
  transfers between devices with their start and end apart: 11 -> 4, of which waited for: 10 -> 4; matrix products, arithmetic and copies ran while one was open for 11% -> 4% of each run, Pallas kernels for 0% -> 2%
where the time goes in v1:
time: 460 us; the launch traced here: 459 us
  waiting for transfers between devices  313 us (68%)
  blocking collectives  77 us (17%)
  Pallas kernels  26.3 us (6%)
  other arithmetic  19.7 us (4%)
  between operations  17.6 us (4%)
  local copies, waits for them, and re-layouts  5.1 us (1%)
    all_gather x1, waiting for transfers between devices, shards(): qkv_weight = lax.all_gather(own_qkv, ('ctx', 'dp'), axis=0, tiled=True)  128 us
    all_gather x1, waiting for transfers between devices, shards(): out_weight = lax.all_gather(own_out, ('ctx', 'dp'), axis=0, tiled=True)  116 us
    psum x1, blocking collectives, shards(): loss = lax.psum(local_total, ('ctx', 'tp', 'dp')) / (seq_len * model_width)  77 us
    all_gather x1, waiting for transfers between devices, shards(): kv = lax.all_gather(parcel, 'ctx', axis=0)  34.8 us
    all_gather x1, waiting for transfers between devices, shards(): mixed_all = lax.all_gather(mixed.reshape(local_rows, width), 'tp', axis=0)  34.3 us
    pallas_call x1, Pallas kernels, blend(): pl.pallas_call(blend_kernel, grid=(count // rows,), in_specs=[pl.BlockSpe...  9.23 us
  transfers between devices with their start and end apart: 4, of which 4 were waited for; matrix products, arithmetic and copies ran while one was open for 4% of the time, Pallas kernels for 2%

profile of v1, /device:TPU:1, one launch (start us, length us, event | category | flops | bytes accessed | tf_op | source)
XLA Modules:
  0.0 459.1 jit_solution(15490871693083506606)
XLA Ops:
  7.9 1.6 add_convert_fusion
  9.6 3.1 multiply_reduce_fusion
  12.7 0.7 convert_bitcast_fusion
  13.5 1.0 fusion.2
  14.5 0.8 pad_maximum_fusion.refs_2_
  15.3 0.9 pad_maximum_fusion.1.refs_3_
  16.2 5.8 %fusion.1.refs_0_ = bf16[512,4096]{1,0:T(8,128)(2,1)} fusion(f32[4096]{0:T(1024)S(1)} %copy-done.2, f32[512]{0:T(512)S(1)} %bitcast.37, bf16[1,2,256,4096]{3,2,1,0:T(8,128)(2,1)} %param.13), kind=kLoop, calls=%fused_computation.2 | loop fusion | flops 8388608 | bytes 8407040 | tf_op jit(solution)/shard_map/convert_element_type | solution.py:211
  22.0 128.1 %all-gather.6.cloned.1.call-done.refs_1_ = bf16[4096,768]{1,0:T(8,128)(2,1)} async-done(((bf16[64,768]{1,0:T(8,128)(2,1)}), bf16[4096,768]{1,0:T(8,128)(2,1)}) %all-gather.6.cloned.1.call-update) | async-done | bytes 6291472 | tf_op jit(solution)/shard_map/all_gather | solution.py:204
  150.1 8.5 %project.1 = bf16[512,768]{1,0:T(8,128)(2,1)} custom-call(bf16[512,4096]{1,0:T(8,128)(2,1)} %fusion.1.refs_0_, bf16[4096,768]{1,0:T(8,128)(2,1)} %all-gather.6.cloned.1.call-done.refs_1_, f32[512,128]{1,0:T(8,128)} %pad_maximum_fusion.refs_2_, f32[512,128]{1,0:T(8,128)} %pad_maximum_fusion.1.refs_3_), custom_call_target="tpu_custom_call" | custom-call | tf_op jit(solution)/shard_map/project/pallas_call | solution.py:49
  158.6 1.0 slice.28
  159.6 0.8 maximum_maximum_fusion
  160.5 0.6 fusion.3
  161.2 1.9 slice.30
  163.1 34.8 %all-gather.12.cloned.1.call-done = bf16[16,272,256]{2,1,0:T(8,128)(2,1)} async-done(((bf16[2,272,256]{2,1,0:T(8,128)(2,1)}), bf16[16,272,256]{2,1,0:T(8,128)(2,1)}) %all-gather.12.cloned.1.call-update) | async-done | bytes 2228240 | tf_op jit(solution)/shard_map/all_gather | solution.py:224
  197.9 0.8 slice.29
  199.0 0.7 fusion.5
  199.6 2.1 fusion.4
  201.7 0.6 tile.9.refs_3_
  202.9 8.5 %attend.1 = bf16[2,256,512]{2,1,0:T(8,128)(2,1)} custom-call(s32[3]{0:T(128)} %pad_add_fusion.refs_0_, bf16[2,256,512]{2,1,0:T(8,128)(2,1)} %bitcast.33, bf16[8,2,272,256]{3,2,1,0:T(8,128)(2,1)} %bitcast.32, s32[2,1,1024]{2,1,0:T(1,128)} %tile.9.refs_3_), custom_call_target="tpu_custom_call" | custom-call | tf_op jit(solution)/shard_map/attend/pallas_call | solution.py:111
  212.1 116.1 %all-gather.10.cloned.1.call-done.weight_ref = bf16[1024,2048]{1,0:T(8,128)(2,1)} async-done(((bf16[16,2048]{1,0:T(8,128)(2,1)}), bf16[1024,2048]{1,0:T(8,128)(2,1)}) %all-gather.10.cloned.1.call-update) | async-done | bytes 4194320 | tf_op jit(solution)/shard_map/all_gather | solution.py:240
  328.3 34.3 %all-gather.8.cloned.1.call-done.mixed_ref = bf16[4,512,512]{2,1,0:T(8,128)(2,1)} async-done(((bf16[1,512,512]{2,1,0:T(8,128)(2,1)}), bf16[4,512,512]{2,1,0:T(8,128)(2,1)}) %all-gather.8.cloned.1.call-update) | async-done | bytes 2097168 | tf_op jit(solution)/shard_map/all_gather | solution.py:239
  362.5 9.2 %blend.1 = (bf16[512,1024]{1,0:T(8,128)(2,1)}, f32[8,1024]{1,0:T(8,128)}) custom-call(bf16[4,512,512]{2,1,0:T(8,128)(2,1)} %all-gather.8.cloned.1.call-done.mixed_ref, bf16[1024,2048]{1,0:T(8,128)(2,1)} %all-gather.10.cloned.1.call-done.weight_ref), custom_call_target="tpu_custom_call" | custom-call | tf_op jit(solution)/shard_map/blend/pallas_call | solution.py:153
  371.8 1.4 reduce_sum.29
  373.8 77.0 %psum.7 = f32[]{:T(128)} all-reduce(f32[]{:T(128)S(6)} %mul.79), channel_id=1, replica_groups=mesh['ctx'=8,'tp'=4,'dp'=8] {'ctx','tp','dp'}, use_global_device_ids=true, to_apply=%region_4.5 | all-reduce | flops 1 | bytes 8 | tf_op jit(solution)/shard_map/psum | solution.py:243
  (29 shorter events, 1.1 us)
Async XLA Ops:
  7.2 9.0 %copy-start.2 = (f32[4096]{0:T(1024)S(1)}, f32[4096]{0:T(1024)}, u32[]{:S(2)}) copy-start(f32[4096]{0:T(1024)} %param.14) | copy-start | bytes 49156
  7.2 142.9 %all-gather.6.cloned.1.call-start = ((), (), s32[]{:S(2)}) async-start(), calls=%async_computation | async-start | bytes 6389760 | tf_op jit(solution)/shard_map/all_gather | solution.py:204
  9.5 188.4 %all-gather.12.cloned.1.call-start = ((), (), s32[]{:S(2)}) async-start(), calls=%async_computation.3 | async-start | bytes 2506752 | tf_op jit(solution)/shard_map/all_gather | solution.py:224
  22.0 138.5 %copy-start = (bf16[2048,16]{0,1:T(8,128)(2,1)S(1)}, bf16[2048,16]{0,1:T(8,128)(2,1)}, u32[]{:S(2)}) copy-start(bf16[2048,16]{0,1:T(8,128)(2,1)} %param.22) | copy-start | bytes 196612
  22.0 138.5 %copy-start.1 = (bf16[2048,16]{0,1:T(8,128)(2,1)S(1)}, bf16[2048,16]{0,1:T(8,128)(2,1)}, u32[]{:S(2)}) copy-start(bf16[2048,16]{0,1:T(8,128)(2,1)} %param.18) | copy-start | bytes 196612
  22.0 177.6 %copy-start.3 = (s32[1,2,256]{2,1,0:T(2,128)S(1)}, s32[1,2,256]{2,1,0:T(2,128)}, u32[]{:S(2)}) copy-start(s32[1,2,256]{2,1,0:T(2,128)} %param.24) | copy-start | bytes 6148
  160.5 167.8 %all-gather.10.cloned.1.call-start = ((), (), s32[]{:S(2)}) async-start(), calls=%async_computation.2 | async-start | bytes 4259840 | tf_op jit(solution)/shard_map/all_gather | solution.py:240
  161.2 201.3 %all-gather.8.cloned.1.call-start = ((), (), s32[]{:S(2)}) async-start(), calls=%async_computation.1 | async-start | bytes 2621440 | tf_op jit(solution)/shard_map/all_gather | solution.py:239
Sparse Core Ops, SparseCore 0:
  12.2 137.8 all-gather.5
  160.6 37.2 all-gather.11
  201.4 126.8 all-gather.9
  330.5 31.9 all-gather.7

commit v2 on v1

v2 whole, which is shorter than its diff:
```python
import math

import jax
import jax.numpy as jnp
from jax import lax
from jax.experimental import pallas as pl
from jax.experimental.pallas import tpu as pltpu
from jax.sharding import PartitionSpec as P

HD = 128
LANES = 128

perturb_step = 0.004
rope_base = 500000.0
norm_epsilon = 1e-05
masked_score = -1e30
mesh_axes = ("ctx", "tp", "dp")


def perturbed(weight, noise, factor):
    return (weight.astype(jnp.float32) + factor * noise.astype(jnp.float32)).astype(jnp.bfloat16)


def dot_dims(lhs, rhs, dims):
    return lax.dot_general(lhs, rhs, (dims, ((), ())), preferred_element_type=jnp.float32)


def rope_tables(positions):
    half = HD // 2
    inverse = rope_base ** (-jnp.arange(half, dtype=jnp.float32) * 2.0 / HD)
    angles = positions.astype(jnp.float32)[:, None] * inverse[None, :]
    cosine = jnp.cos(angles)
    sine = jnp.sin(angles)
    return (
        jnp.concatenate([cosine, cosine], axis=1),
        jnp.concatenate([-sine, sine], axis=1),
    )


def fetch(values, source):
    sizes = [lax.axis_size(axis) for axis in mesh_axes]
    pairs = []
    for c in range(sizes[0]):
        for t in range(sizes[1]):
            for d in range(sizes[2]):
                fc, ft, fd = source(c, t, d)
                pairs.append(((fc * sizes[1] + ft) * sizes[2] + fd, (c * sizes[1] + t) * sizes[2] + d))
    return lax.ppermute(values, mesh_axes, pairs)


def from_z(values, step):
    count = lax.axis_size("ctx")
    return fetch(values, lambda c, t, d: ((c + step) % count, t, d))


def from_x(values, step):
    count = lax.axis_size("dp") // 2
    return fetch(values, lambda c, t, d: (c, t, ((d // 2 + step) % count) * 2 + d % 2))


def from_y(values):
    return fetch(values, lambda c, t, d: (c, t, d ^ 1))


def from_tp(values, flip):
    return fetch(values, lambda c, t, d: (c, t ^ flip, d))


def after(value, *others):
    return lax.optimization_barrier((value,) + others)[0]


def norm_kernel(place_ref, tokens_ref, gain_ref, out_ref, *, groups):
    width = tokens_ref.shape[1]
    depth = width // groups
    values = tokens_ref[...].astype(jnp.float32)
    mean = jnp.sum(values * values, axis=1, keepdims=True) / width
    rate = lax.rsqrt(mean + norm_epsilon)
    for group in range(groups):
        columns = slice(group * depth, (group + 1) * depth)
        part = tokens_ref[:, columns].astype(jnp.float32) * rate * gain_ref[:, columns]
        target = lax.rem(group + groups - place_ref[0], groups)
        target = pl.multiple_of(target * depth, depth)
        out_ref[:, pl.ds(target, depth)] = part.astype(jnp.bfloat16)


def norm(place, tokens, gain, groups, start, count, rows=64):
    width = tokens.shape[1]
    return pl.pallas_call(
        lambda *refs: norm_kernel(*refs, groups=groups),
        grid_spec=pltpu.PrefetchScalarGridSpec(
            num_scalar_prefetch=1,
            grid=(count // rows,),
            in_specs=[
                pl.BlockSpec((rows, width), lambda i, _: (i + start // rows, 0)),
                pl.BlockSpec((1, width), lambda i, _: (0, 0)),
            ],
            out_specs=pl.BlockSpec((rows, width), lambda i, _: (i, 0)),
        ),
        out_shape=jax.ShapeDtypeStruct((count, width), jnp.bfloat16),
        name="norm",
    )(place, tokens, gain.reshape(1, width))


def turn(part, cosine, sine):
    return part * cosine + pltpu.roll(part, HD // 2, 1) * sine


def run_copies(pairs, sems):
    copies = [
        pltpu.make_async_copy(source, target, sems.at[at])
        for at, (source, target) in enumerate(pairs)
    ]
    for copy in copies:
        copy.start()
    for copy in copies:
        copy.wait()


def halves_of(normed_any, normed_ref):
    rows = normed_any[0].shape[0]
    return [
        (piece, normed_ref.at[pl.ds(at * rows, rows)]) for at, piece in enumerate(normed_any)
    ]


def pair_kernel(*refs, count):
    first_any, second_any, cos_ref, sin_ref, seg_ref, parcel_ref = refs[count : count + 6]
    buffer, normed_ref, sems = refs[count + 6 :]
    pairs = halves_of((first_any, second_any), normed_ref)
    start = 0
    for piece in refs[:count]:
        size = piece.shape[0]
        pairs.append((piece, buffer.at[pl.ds(start, size)]))
        start += size
    run_copies(pairs, sems)
    half_rows = first_any.shape[0]
    sums = jnp.dot(normed_ref[...], buffer[...], preferred_element_type=jnp.float32)
    keys = turn(sums[:, :HD], cos_ref[...], sin_ref[...]).astype(jnp.bfloat16)
    values = sums[:, HD:].astype(jnp.bfloat16)
    for half in range(2):
        rows_of = slice(half * half_rows, (half + 1) * half_rows)
        parcel_ref[half, :half_rows] = keys[rows_of]
        parcel_ref[half, half_rows : 2 * half_rows] = values[rows_of]
        parcel_ref[half, 2 * half_rows :] = seg_ref[half]


def project_pair(pieces, normed, cosine, sine, seg_rows):
    half_rows, model_width = normed[0].shape
    any_spec = pl.BlockSpec(memory_space=pl.ANY)
    vmem_spec = pl.BlockSpec(memory_space=pltpu.VMEM)
    return pl.pallas_call(
        lambda *refs: pair_kernel(*refs, count=len(pieces)),
        in_specs=[any_spec] * (len(pieces) + 2) + [vmem_spec] * 3,
        out_specs=vmem_spec,
        out_shape=jax.ShapeDtypeStruct(
            (2, 2 * half_rows + seg_rows.shape[1], HD), jnp.bfloat16
        ),
        scratch_shapes=[
            pltpu.VMEM((model_width, 2 * HD), jnp.bfloat16),
            pltpu.VMEM((2 * half_rows, model_width), jnp.bfloat16),
            pltpu.SemaphoreType.DMA((len(pieces) + 2,)),
        ],
        name="project_pair",
    )(*pieces, *normed, cosine, sine, seg_rows)


def query_kernel(place_ref, *refs, groups, columns):
    own_any, next_any, top_any, low_any, last_any, first_any, second_any = refs[:7]
    cos_ref, sin_ref, out_ref, buffer, normed_ref, sums_ref, sems = refs[7:]
    depth = groups * LANES
    half = depth // 2
    pairs = halves_of((first_any, second_any), normed_ref)
    for piece, step, offset in (
        (own_any, 0, 0),
        (next_any, 1, 0),
        (top_any, 2, 0),
        (low_any, 2, half),
        (last_any, columns - 1, 0),
    ):
        column = lax.rem(place_ref[1] + step, columns)
        target = pl.multiple_of(column * depth + offset, half)
        pairs.append((piece, buffer.at[pl.ds(target, piece.shape[0])]))
    run_copies(pairs, sems)
    sums_ref[...] = jnp.zeros_like(sums_ref)

    def step(column, _):
        parts = []
        for group in range(groups):
            start = pl.multiple_of((group * columns + column) * LANES, LANES)
            parts.append(normed_ref[:, pl.ds(start, LANES)])
        start = pl.multiple_of(column * depth, depth)
        sums_ref[...] += jnp.dot(
            jnp.concatenate(parts, axis=1),
            buffer[pl.ds(start, depth)],
            preferred_element_type=jnp.float32,
        )
        return 0

    lax.fori_loop(0, columns, step, 0)
    for head in range(sums_ref.shape[1] // HD):
        lanes = slice(head * HD, (head + 1) * HD)
        part = turn(sums_ref[:, lanes], cos_ref[...], sin_ref[...])
        out_ref[:, lanes] = part.astype(jnp.bfloat16)


def project_queries(place, pieces, normed, cosine, sine, groups, columns):
    half_rows, model_width = normed[0].shape
    width = pieces[0].shape[1]
    any_spec = pl.BlockSpec(memory_space=pl.ANY)
    vmem_spec = pl.BlockSpec(memory_space=pltpu.VMEM)
    return pl.pallas_call(
        lambda *refs: query_kernel(*refs, groups=groups, columns=columns),
        in_specs=[pl.BlockSpec(memory_space=pltpu.SMEM)] + [any_spec] * 7 + [vmem_spec] * 2,
        out_specs=vmem_spec,
        out_shape=jax.ShapeDtypeStruct((2 * half_rows, width), jnp.bfloat16),
        scratch_shapes=[
            pltpu.VMEM((model_width, width), jnp.bfloat16),
            pltpu.VMEM((2 * half_rows, model_width), jnp.bfloat16),
            pltpu.VMEM((2 * half_rows, width), jnp.float32),
            pltpu.SemaphoreType.DMA((7,)),
        ],
        name="project_queries",
    )(place, *pieces, *normed, cosine, sine)


def attend_kernel(place_ref, *refs, half_rows, heads, ctx_count):
    query_ref, seg_ref, out_ref, key_buf, value_buf, seg_buf, sems = refs[ctx_count + 1 :]
    which = pl.program_id(0)
    ctx = place_ref[0]
    blocks = 2 * ctx_count
    span = 2 * half_rows
    seg_count = half_rows // LANES

    @pl.when(which == 0)
    def _():
        pairs = []
        sources = []
        for step in range(ctx_count + 1):
            parcel = refs[step]
            distance = step if step <= ctx_count // 2 else step - 1
            if parcel.shape[0] == 1:
                sources.append((parcel.at[0], distance, step - ctx_count // 2))
            else:
                sources.append((parcel.at[0], distance, 0))
                sources.append((parcel.at[1], distance, 1))
        for source, distance, half in sources:
            holder = lax.rem(ctx + distance, ctx_count)
            block = blocks - 1 - holder if half else holder
            rows = pl.ds(pl.multiple_of(block * half_rows, half_rows), half_rows)
            pairs.append((source.at[pl.ds(0, half_rows)], key_buf.at[rows]))
            pairs.append((source.at[pl.ds(half_rows, half_rows)], value_buf.at[rows]))
            pairs.append(
                (source.at[pl.ds(2 * half_rows, 16)], seg_buf.at[block])
            )
        run_copies(pairs, sems)

    all_seg = seg_buf[...].astype(jnp.float32)
    real = lax.broadcasted_iota(jnp.int32, all_seg.shape, 1) < seg_count
    own_seg = seg_ref[0]
    first = jnp.zeros(own_seg.shape, jnp.int32)
    for doc in range(1, 4):
        smaller = jnp.where(real & (all_seg < doc), 1.0, 0.0)
        before = jnp.sum(jnp.sum(smaller, axis=0), axis=(0, 1), keepdims=True)
        first = jnp.where(own_seg == doc, before.astype(jnp.int32), first)
    own = jnp.where(which == 0, ctx, blocks - 1 - ctx)
    low = jnp.min(first) // span
    last = own * half_rows // span
    inner = jnp.minimum((jnp.max(first) + span - 1) // span, last)

    queries = jnp.concatenate(
        [query_ref[:, h * HD : (h + 1) * HD] for h in range(heads)], axis=0
    )
    rows = heads * half_rows
    factor = math.log2(math.e) / HD**0.5
    first = jnp.concatenate([first] * heads, axis=1)
    query_pos = own * half_rows + lax.rem(
        lax.broadcasted_iota(jnp.int32, (1, rows), 1), half_rows
    )

    def step(block, state, masked):
        highest, totals, accum = state
        start = pl.multiple_of(block * span, span)
        scores = dot_dims(key_buf[pl.ds(start, span)], queries, ((1,), (1,)))
        if masked:
            key_pos = start + lax.broadcasted_iota(jnp.int32, (span, rows), 0)
            allowed = (key_pos <= query_pos) & (key_pos >= first)
            limited = jnp.where(allowed, scores, masked_score)
        else:
            limited = scores
        new_high = jnp.maximum(highest, jnp.max(limited, axis=0, keepdims=True))
        shrink = jnp.exp2((highest - new_high) * factor)
        weights = jnp.exp2((scores - new_high) * factor)
        if masked:
            weights = jnp.where(allowed, weights, 0.0)
        new_totals = totals * shrink + jnp.sum(weights, axis=0, keepdims=True)
        added = dot_dims(
            value_buf[pl.ds(start, span)], weights.astype(jnp.bfloat16), ((0,), (0,))
        )
        return (new_high, new_totals, accum * shrink + added)

    state = (
        jnp.full((1, rows), masked_score, jnp.float32),
        jnp.zeros((1, rows), jnp.float32),
        jnp.zeros((HD, rows), jnp.float32),
    )
    state = lax.fori_loop(inner, last, lambda b, s: step(b, s, False), state)
    edges = jnp.minimum(inner, last) - low
    state = lax.fori_loop(
        0,
        edges + 1,
        lambda b, s: step(jnp.where(b < edges, low + b, last), s, True),
        state,
    )
    _, totals, accum = state
    mixed = (accum / totals).astype(jnp.bfloat16)
    for h in range(heads):
        out_ref[:, h * HD : (h + 1) * HD] = mixed[:, h * half_rows : (h + 1) * half_rows].T


def attend(place, parcels, queries, seg, half_rows, heads):
    ctx_count = len(parcels) - 1
    width = heads * HD
    keys = 2 * ctx_count * half_rows
    return pl.pallas_call(
        lambda *refs: attend_kernel(
            *refs, half_rows=half_rows, heads=heads, ctx_count=ctx_count
        ),
        grid=(2,),
        in_specs=[pl.BlockSpec(memory_space=pltpu.SMEM)]
        + [pl.BlockSpec(memory_space=pl.ANY)] * len(parcels)
        + [
            pl.BlockSpec((half_rows, width), lambda i: (i, 0)),
            pl.BlockSpec((1, 1, half_rows), lambda i: (i, 0, 0)),
        ],
        out_specs=pl.BlockSpec((half_rows, width), lambda i: (i, 0)),
        out_shape=jax.ShapeDtypeStruct((2 * half_rows, width), jnp.bfloat16),
        scratch_shapes=[
            pltpu.VMEM((keys, HD), jnp.bfloat16),
            pltpu.VMEM((keys, HD), jnp.bfloat16),
            pltpu.VMEM((2 * ctx_count, 16, HD), jnp.bfloat16),
            pltpu.SemaphoreType.DMA((6 * ctx_count,)),
        ],
        name="attend",
    )(place, *parcels, queries, seg)


def blend_kernel(owner_ref, *refs):
    weight_any, out_ref, square_ref, mixed_buf, buffer, total_ref, sems = refs[4:]
    width = mixed_buf.shape[2]

    def weight_copy(step):
        columns = pl.ds(pl.multiple_of(owner_ref[step] * width, LANES), width)
        return pltpu.make_async_copy(
            weight_any.at[:, columns], buffer.at[step], sems.at[4 + step]
        )

    for step in range(4):
        weight_copy(step).start()
    run_copies([(refs[step], mixed_buf.at[step]) for step in range(4)], sems)
    total_ref[...] = jnp.zeros_like(total_ref)

    def add(step, _):
        weight_copy(step).wait()
        term = dot_dims(mixed_buf[step], buffer[step], ((1,), (1,)))
        total_ref[...] += term.astype(jnp.bfloat16).astype(jnp.float32)
        return 0

    lax.fori_loop(0, 4, add, 0)
    branch = total_ref[...].astype(jnp.bfloat16)
    out_ref[...] = branch
    square = jnp.square(branch.astype(jnp.float32))
    square = jnp.sum(square.reshape(-1, 8, square.shape[1]), axis=0)
    part = square[:, :LANES]
    for block in range(1, square.shape[1] // LANES):
        part += square[:, block * LANES : (block + 1) * LANES]
    square_ref[...] = part


def blend(owners, mixed, weight):
    count, width = mixed[0].shape
    features = weight.shape[0]
    any_spec = pl.BlockSpec(memory_space=pl.ANY)
    vmem_spec = pl.BlockSpec(memory_space=pltpu.VMEM)
    return pl.pallas_call(
        blend_kernel,
        in_specs=[pl.BlockSpec(memory_space=pltpu.SMEM)] + [any_spec] * 5,
        out_specs=[vmem_spec, vmem_spec],
        out_shape=[
            jax.ShapeDtypeStruct((count, features), jnp.bfloat16),
            jax.ShapeDtypeStruct((8, LANES), jnp.float32),
        ],
        scratch_shapes=[
            pltpu.VMEM((4, count, width), jnp.bfloat16),
            pltpu.VMEM((4, features, width), jnp.bfloat16),
            pltpu.VMEM((count, features), jnp.float32),
            pltpu.SemaphoreType.DMA((8,)),
        ],
        name="blend",
    )(owners, *mixed, weight)


def shards(
    tokens,
    norm_gain,
    query_weight,
    key_weight,
    value_weight,
    output_weight,
    query_noise,
    key_noise,
    value_noise,
    output_noise,
    sign,
    segment_ids,
    doc_weight,
):
    factor = sign[0].astype(jnp.float32) * perturb_step
    half_rows = tokens.shape[2]
    model_width = tokens.shape[3]
    local_rows = 2 * half_rows
    ctx = lax.axis_index("ctx")
    tp = lax.axis_index("tp")
    ctx_count = lax.axis_size("ctx")
    columns = lax.axis_size("dp") // 2
    x = lax.axis_index("dp") // 2
    seq_len = local_rows * ctx_count
    heads = query_weight.shape[1] // HD
    width = heads * HD

    own_pair = perturbed(
        jnp.concatenate([key_weight, value_weight], axis=1),
        jnp.concatenate([key_noise, value_noise], axis=1),
        factor,
    )
    own_query = perturbed(query_weight, query_noise, factor)
    dp_count = lax.axis_size("dp")
    spread = jnp.broadcast_to(own_pair[None], (dp_count,) + own_pair.shape)
    spread, own_query = lax.optimization_barrier((spread, own_query))
    other = from_y(own_query)
    line = lax.all_to_all(spread, "dp", 0, 0).reshape(-1, 2 * HD)
    own_out = perturbed(after(output_weight, own_query), output_noise, factor).T
    out_weight = lax.all_gather(own_out, ("ctx", "dp"), axis=0, tiled=True)
    even = lax.axis_index("dp") % 2 == 0
    right = jnp.where(
        even,
        jnp.concatenate([own_query, other], axis=0),
        jnp.concatenate([other, own_query], axis=0),
    )

    place = jnp.stack([ctx, x]).astype(jnp.int32)
    rows_in = tokens[0].reshape(local_rows, model_width)
    normed = [
        norm(place, rows_in, norm_gain, ctx_count, half * half_rows, half_rows)
        for half in range(2)
    ]
    offsets = jnp.arange(half_rows, dtype=jnp.int32)
    local_pos = jnp.concatenate(
        [ctx * half_rows + offsets, seq_len - (ctx + 1) * half_rows + offsets]
    )
    cosine, sine = rope_tables(local_pos)
    seg_rows = segment_ids[0].astype(jnp.bfloat16).reshape(2, half_rows // LANES, LANES)
    seg_rows = jnp.pad(seg_rows, ((0, 0), (0, 16 - seg_rows.shape[1]), (0, 0)))

    up, down = [line], [line]
    right_up, right_down = [right], [right]
    for step in range(3):
        ends = (up[-1], down[-1], right_up[-1], right_down[-1])
        if step:
            ends = lax.optimization_barrier(ends + (normed[step - 1],))
            normed[step - 1] = ends[4]
        else:
            ends = lax.optimization_barrier(ends)
        up.append(from_z(ends[0], 1))
        down.append(from_z(ends[1], -1))
        right_up.append(from_z(ends[2], 1))
        right_down.append(from_z(ends[3], -1))
    middle = line.shape[0] // 2
    last_up, last_down, last_right, cosine, sine, seg_rows = lax.optimization_barrier(
        (up[3][:middle], down[3][middle:], right_up[3], cosine, sine, seg_rows)
    )
    far_right = from_z(last_right, 1)
    pieces = up + [from_z(last_up, 1), from_z(last_down, -1)] + down[:0:-1]
    column = jnp.concatenate(right_up + [far_right] + right_down[:0:-1], axis=0)
    next_x = from_x(column, 1)
    last_x = from_x(column, -1)
    parcel = project_pair(pieces, (after(normed[0], column), normed[1]), cosine, sine, seg_rows)

    parcel_up, parcel_down = [parcel], [parcel]
    for step in range(3):
        ends = (parcel_up[-1], parcel_down[-1])
        if step == 2:
            ends = lax.optimization_barrier(ends + (next_x, last_x))[:2]
        parcel_up.append(from_z(ends[0], 1))
        parcel_down.append(from_z(ends[1], -1))
    parcels = (
        parcel_up
        + [from_z(parcel_up[3][:1], 1), from_z(parcel_down[3][1:], -1)]
        + parcel_down[:0:-1]
    )
    middle = column.shape[0] // 2
    next_half, last_half = lax.optimization_barrier(
        (next_x[:middle], last_x[middle:], parcel_up[1], parcel_down[1])
    )[:2]
    columns_in = [column, next_x, from_x(next_half, 1), from_x(last_half, -1), last_x]
    queries = project_queries(place, columns_in, normed, cosine, sine, ctx_count, columns)

    own_seg = segment_ids[0].reshape(2, 1, half_rows)
    mixed = attend(place, parcels, queries, own_seg, half_rows, heads)
    near = from_tp(mixed, 1)
    far = from_tp(mixed, 2)
    owners = jnp.stack([tp, tp ^ 1, tp ^ 2, tp ^ 3]).astype(jnp.int32)
    branch, squares = blend(owners, [mixed, near, far, from_tp(far, 1)], out_weight)
    local_total = jnp.sum(squares) * doc_weight[0]
    everyone = ctx_count * lax.axis_size("tp") * lax.axis_size("dp")
    shares = lax.all_to_all(
        jnp.broadcast_to(local_total, (everyone, LANES)), mesh_axes, 0, 0, tiled=True
    )
    loss = jnp.sum(shares[:, 0]) / (seq_len * model_width)
    return (branch.reshape(1, 2, half_rows, branch.shape[1]), loss.reshape(1))


def solution(mesh):
    return jax.shard_map(
        shards,
        mesh=mesh,
        in_specs=(
            P("dp", None, "ctx", None),
            P(),
            P(("ctx", "dp"), "tp"),
            P(("ctx", "dp"), "tp"),
            P(("ctx", "dp"), "tp"),
            P(None, ("tp", "ctx", "dp")),
            P(("ctx", "dp"), "tp"),
            P(("ctx", "dp"), "tp"),
            P(("ctx", "dp"), "tp"),
            P(None, ("tp", "ctx", "dp")),
            P(),
            P("dp", None, "ctx"),
            P("dp"),
        ),
        out_specs=(P("dp", None, "ctx", "tp"), P()),
        check_vma=False,
    )
```

time: 460 us -> 205 us (0.45)
  waiting for transfers between devices: 313 us -> 42.6 us
  starting transfers between devices: 0.16 us -> 60.5 us
  blocking collectives: 77 us -> 24.2 us
  Pallas kernels: 26.3 us -> 45.6 us
  other arithmetic: 19.7 us -> 9.09 us
    all_gather x3 -> x0, waiting for transfers between devices: 197 us -> none  [the longest x1 128 us: shards(): qkv_weight = lax.all_gather(own_qkv, ('ctx', 'dp'), axis=0, tiled=True)]
    all_gather x1, waiting for transfers between devices: 116 us -> 0.01 us  [shards(): out_weight = lax.all_gather(own_out, ('ctx', 'dp'), axis=0, tiled=True)]
    psum x1 -> x0, blocking collectives: 77 us -> none  [shards(): loss = lax.psum(local_total, ('ctx', 'tp', 'dp')) / (seq_len * model_width)]
    ppermute x0 -> x31, starting transfers between devices: none -> 53 us  [fetch(): return lax.ppermute(values, mesh_axes, pairs)]
    ppermute x0 -> x31, waiting for transfers between devices: none -> 40.3 us  [fetch(): return lax.ppermute(values, mesh_axes, pairs)]
    all_to_all x0 -> x1, blocking collectives: none -> 24.2 us  [shards(): lax.all_to_all(jnp.broadcast_to(local_total, (everyone, LANES)), mesh_axe...]
    pallas_call x2 -> x5, Pallas kernels: 17.7 us -> 32.5 us  [the longest x2 10.1 us: norm(): pl.pallas_call(lambda *refs: norm_kernel(*refs, groups=groups), grid_spec...]
    all_to_all x0 -> x1, starting transfers between devices: none -> 7.49 us  [shards(): line = lax.all_to_all(spread, 'dp', 0, 0).reshape(-1, 2 * HD)]
  transfers between devices with their start and end apart: 4 -> 33, of which waited for: 4 -> 18; matrix products, arithmetic and copies ran while one was open for 4% -> 3% of each run, Pallas kernels for 2% -> 18%
where the time goes in v2:
time: 205 us; the launch traced here: 204 us
  starting transfers between devices  60.5 us (30%)
  Pallas kernels  45.6 us (22%)
  waiting for transfers between devices  42.6 us (21%)
  blocking collectives  24.2 us (12%)
  between operations  18.1 us (9%)
  other arithmetic  9.09 us (4%)
  local copies, waits for them, and re-layouts  4.26 us (2%)
    ppermute x31, starting transfers between devices, fetch(): return lax.ppermute(values, mesh_axes, pairs)  53 us
    ppermute x31, waiting for transfers between devices, fetch(): return lax.ppermute(values, mesh_axes, pairs)  40.3 us
    all_to_all x1, blocking collectives, shards(): lax.all_to_all(jnp.broadcast_to(local_total, (everyone, LANES)), mesh_axe...  24.2 us
    pallas_call x1, Pallas kernels, attend(): pl.pallas_call(lambda *refs: attend_kernel(*refs, half_rows=half_rows, he...  13.1 us
    pallas_call x2, Pallas kernels, norm(): pl.pallas_call(lambda *refs: norm_kernel(*refs, groups=groups), grid_spec...  10.1 us
    pallas_call x1, Pallas kernels, project_queries(): pl.pallas_call(lambda *refs: query_kernel(*refs, groups=groups, columns=c...  8.62 us
    pallas_call x1, Pallas kernels, blend(): pl.pallas_call(blend_kernel, in_specs=[pl.BlockSpec(memory_space=pltpu.SM...  7.9 us
    all_to_all x1, starting transfers between devices, shards(): line = lax.all_to_all(spread, 'dp', 0, 0).reshape(-1, 2 * HD)  7.49 us
  transfers between devices with their start and end apart: 33, of which 18 were waited for; matrix products, arithmetic and copies ran while one was open for 3% of the time, Pallas kernels for 18%

profile of v2, /device:TPU:1, one launch (start us, length us, event | category | flops | bytes accessed | tf_op | source)
XLA Modules:
  0.0 204.3 jit_solution(1882759397280854911)
XLA Ops:
  11.8 7.5 %all-to-all-start = ((bf16[8,64,256]{2,1,0:T(8,128)(2,1)}), bf16[8,64,256]{2,1,0:T(8,128)(2,1)S(1)}, u32[]{:S(2)}, u32[]{:S(2)}) async-start(bf16[8,64,256]{2,1,0:T(8,128)(2,1)} %broadcast_in_dim.4), calls=%async_computation | async-start | bytes 524288 | tf_op jit(solution)/shard_map/all_to_all | solution.py:441
  19.3 3.0 %collective-permute-start = (bf16[64,512]{1,0:T(8,128)(2,1)S(1)}, bf16[64,512]{1,0:T(8,128)(2,1)S(1)}, u32[]{:S(2)}, u32[]{:S(2)}) collective-permute-start(bf16[64,512]{1,0:T(8,128)(2,1)S(1)} %add_convert_fusion.1), channel_id=1, source_target_pairs={{1,0},{0,1},{3,2},{2,3},{5,4},{4,5},{7,6},{6,7},{9,8},{8,9},{11,10... | collective-permute-start | bytes 196616 | tf_op jit(solution)/shard_map/ppermute | solution.py:48
  22.3 2.2 %collective-permute-done = bf16[64,512]{1,0:T(8,128)(2,1)S(1)} collective-permute-done((bf16[64,512]{1,0:T(8,128)(2,1)S(1)}, bf16[64,512]{1,0:T(8,128)(2,1)S(1)}, u32[]{:S(2)}, u32[]{:S(2)}) %collective-permute-start) | collective-permute-done | bytes 65568 | tf_op jit(solution)/shard_map/ppermute | solution.py:48
  24.5 2.2 %all-to-all-done = bf16[8,64,256]{2,1,0:T(8,128)(2,1)S(1)} async-done(((bf16[8,64,256]{2,1,0:T(8,128)(2,1)}), bf16[8,64,256]{2,1,0:T(8,128)(2,1)S(1)}, u32[]{:S(2)}, u32[]{:S(2)}) %all-to-all-start) | async-done | bytes 262176 | tf_op jit(solution)/shard_map/all_to_all | solution.py:441
  26.7 5.6 %collective-permute-start.1 = (bf16[512,256]{1,0:T(8,128)(2,1)S(1)}, bf16[512,256]{1,0:T(8,128)(2,1)S(1)}, u32[]{:S(2)}, u32[]{:S(2)}) collective-permute-start(bf16[512,256]{1,0:T(8,128)(2,1)S(1)} %bitcast.20), channel_id=1, source_target_pairs={{32,0},{33,1},{34,2},{35,3},{36,4},{37,5},{38,6},{39,7},{40,8},{41... | collective-permute-start | bytes 786440 | tf_op jit(solution)/shard_map/ppermute | solution.py:48
  32.3 2.7 %collective-permute-start.3 = (bf16[128,512]{1,0:T(8,128)(2,1)S(1)}, bf16[128,512]{1,0:T(8,128)(2,1)S(1)}, u32[]{:S(2)}, u32[]{:S(2)}) collective-permute-start(bf16[128,512]{1,0:T(8,128)(2,1)S(1)} %get-tuple-element.37), channel_id=1, source_target_pairs={{32,0},{33,1},{34,2},{35,3},{36,4},{37,5},{38,6},{39,7},{40,8},{41... | collective-permute-start | bytes 393224 | tf_op jit(solution)/shard_map/ppermute | solution.py:48
  35.6 4.9 %norm.2.refs_9_.refs_6_ = bf16[256,4096]{1,0:T(8,128)(2,1)} custom-call(s32[2]{0:T(128)} %pad_add_fusion.1.refs_0_, bf16[512,4096]{1,0:T(8,128)(2,1)} %bitcast.18, f32[1,4096]{1,0:T(1,128)} %bitcast.24), custom_call_target="tpu_custom_call" | custom-call | tf_op jit(solution)/shard_map/norm/pallas_call | solution.py:89
  43.8 5.1 %norm.3.refs_10_.refs_7_ = bf16[256,4096]{1,0:T(8,128)(2,1)} custom-call(s32[2]{0:T(128)} %pad_add_fusion.1.refs_0_, bf16[512,4096]{1,0:T(8,128)(2,1)} %bitcast.19, f32[1,4096]{1,0:T(1,128)} %bitcast.25), custom_call_target="tpu_custom_call" | custom-call | tf_op jit(solution)/shard_map/norm/pallas_call | solution.py:89
  48.9 2.2 %collective-permute-start.7 = (bf16[128,512]{1,0:T(8,128)(2,1)S(1)}, bf16[128,512]{1,0:T(8,128)(2,1)S(1)}, u32[]{:S(2)}, u32[]{:S(2)}) collective-permute-start(bf16[128,512]{1,0:T(8,128)(2,1)S(1)} %collective-permute-done.3), channel_id=1, source_target_pairs={{32,0},{33,1},{34,2},{35,3},{36,4},{37,5},{38,6},{39,7},{40,8},{41... | collective-permute-start | bytes 393224 | tf_op jit(solution)/shard_map/ppermute | solution.py:48
  53.5 2.8 %collective-permute-done.8 = bf16[128,512]{1,0:T(8,128)(2,1)S(1)} collective-permute-done((bf16[128,512]{1,0:T(8,128)(2,1)S(1)}, bf16[128,512]{1,0:T(8,128)(2,1)S(1)}, u32[]{:S(2)}, u32[]{:S(2)}) %collective-permute-start.8) | collective-permute-done | bytes 131104 | tf_op jit(solution)/shard_map/ppermute | solution.py:48
  65.5 4.5 %collective-permute-done.14 = bf16[128,512]{1,0:T(8,128)(2,1)S(1)} collective-permute-done((bf16[128,512]{1,0:T(8,128)(2,1)S(1)}, bf16[128,512]{1,0:T(8,128)(2,1)S(1)}, u32[]{:S(2)}, u32[]{:S(2)}) %collective-permute-start.14) | collective-permute-done | bytes 131104 | tf_op jit(solution)/shard_map/ppermute | solution.py:48
  71.7 3.8 %collective-permute-start.20 = (bf16[1024,512]{1,0:T(8,128)(2,1)S(1)}, bf16[1024,512]{1,0:T(8,128)(2,1)S(1)}, u32[]{:S(2)}, u32[]{:S(2)}) collective-permute-start(bf16[1024,512]{1,0:T(8,128)(2,1)S(1)} %constant_dynamic-update-slice_fusion.refs_1_), channel_id=1, source_target_pairs={{2,0},{3,1},{4,2},{5,3},{6,4},{7,5},{0,6},{1,7},{10,8},{11,9},{12,... | collective-permute-start | bytes 3145736 | tf_op jit(solution)/shard_map/ppermute | solution.py:48
  77.0 2.9 %collective-permute-done.12.refs_4_ = bf16[256,256]{1,0:T(8,128)(2,1)S(1)} collective-permute-done((bf16[256,256]{1,0:T(8,128)(2,1)S(1)}, bf16[256,256]{1,0:T(8,128)(2,1)S(1)}, u32[]{:S(2)}, u32[]{:S(2)}) %collective-permute-start.12) | collective-permute-done | bytes 131104 | tf_op jit(solution)/shard_map/ppermute | solution.py:48
  81.2 5.9 %project_pair.1.refs_1_ = bf16[2,528,128]{2,1,0:T(8,128)(2,1)} custom-call(bf16[512,256]{1,0:T(8,128)(2,1)} %bitcast.22, bf16[512,256]{1,0:T(8,128)(2,1)} %copy-done.15, bf16[512,256]{1,0:T(8,128)(2,1)} %copy-done.17, bf16[512,256]{1,0:T(8,128)(2,1)} %copy-done.6, bf16[256,256]{1,0:T(8,128)(2,1)} %copy-done.21, ...), custom_call_target="tpu_custom_call" | custom-call | tf_op jit(solution)/shard_map/project_pair/pallas_call | solution.py:152
  88.7 4.6 %collective-permute-done.16.refs_2_ = bf16[2,528,128]{2,1,0:T(8,128)(2,1)S(1)} collective-permute-done((bf16[2,528,128]{2,1,0:T(8,128)(2,1)}, bf16[2,528,128]{2,1,0:T(8,128)(2,1)S(1)}, u32[]{:S(2)}, u32[]{:S(2)}) %collective-permute-start.16) | collective-permute-done | bytes 270368 | tf_op jit(solution)/shard_map/ppermute | solution.py:48
  95.7 3.2 %collective-permute-done.21.refs_5_ = bf16[1024,512]{1,0:T(8,128)(2,1)S(1)} collective-permute-done((bf16[1024,512]{1,0:T(8,128)(2,1)S(1)}, bf16[1024,512]{1,0:T(8,128)(2,1)S(1)}, u32[]{:S(2)}, u32[]{:S(2)}) %collective-permute-start.21) | collective-permute-done | bytes 1048608 | tf_op jit(solution)/shard_map/ppermute | solution.py:48
  101.7 3.2 %collective-permute-done.19.refs_8_ = bf16[2,528,128]{2,1,0:T(8,128)(2,1)S(1)} collective-permute-done((bf16[2,528,128]{2,1,0:T(8,128)(2,1)S(1)}, bf16[2,528,128]{2,1,0:T(8,128)(2,1)S(1)}, u32[]{:S(2)}, u32[]{:S(2)}) %collective-permute-start.19) | collective-permute-done | bytes 270368 | tf_op jit(solution)/shard_map/ppermute | solution.py:48
  106.4 7.2 %collective-permute-done.22.refs_4_ = bf16[2,528,128]{2,1,0:T(8,128)(2,1)S(1)} collective-permute-done((bf16[2,528,128]{2,1,0:T(8,128)(2,1)S(1)}, bf16[2,528,128]{2,1,0:T(8,128)(2,1)S(1)}, u32[]{:S(2)}, u32[]{:S(2)}) %collective-permute-start.22) | collective-permute-done | bytes 270368 | tf_op jit(solution)/shard_map/ppermute | solution.py:48
  116.4 8.6 %project_queries.1.refs_10_ = bf16[512,512]{1,0:T(8,128)(2,1)} custom-call(s32[2]{0:T(128)} %pad_add_fusion.1.refs_0_, bf16[1024,512]{1,0:T(8,128)(2,1)} %copy-done.2, bf16[1024,512]{1,0:T(8,128)(2,1)} %copy-done, bf16[512,512]{1,0:T(8,128)(2,1)} %collective-permute-done.26.refs_3_, bf16[512,512]{1,0:T(8,128)(2,1)} %collective-permute-done.27.refs_4_, ...), custom_call_target="tpu_custom_call" | custom-call | tf_op jit(solution)/shard_map/project_queries/pallas_call | solution.py:212
  126.4 13.1 %attend.1.refs_0_ = bf16[512,512]{1,0:T(8,128)(2,1)} custom-call(s32[2]{0:T(128)} %pad_add_fusion.1.refs_0_, bf16[2,528,128]{2,1,0:T(8,128)(2,1)} %project_pair.1.refs_1_, bf16[2,528,128]{2,1,0:T(8,128)(2,1)} %copy-done.11, bf16[2,528,128]{2,1,0:T(8,128)(2,1)} %copy-done.13, bf16[2,528,128]{2,1,0:T(8,128)(2,1)} %copy-done.4, ...), custom_call_target="tpu_custom_call" | custom-call | tf_op jit(solution)/shard_map/attend/pallas_call | solution.py:325
  140.1 10.8 %collective-permute-start.28 = (bf16[512,512]{1,0:T(8,128)(2,1)}, bf16[512,512]{1,0:T(8,128)(2,1)S(1)}, u32[]{:S(2)}, u32[]{:S(2)}) collective-permute-start(bf16[512,512]{1,0:T(8,128)(2,1)} %attend.1.refs_0_), channel_id=1, source_target_pairs={{8,0},{9,1},{10,2},{11,3},{12,4},{13,5},{14,6},{15,7},{0,8},{1,9},... | collective-permute-start | bytes 1572872 | tf_op jit(solution)/shard_map/ppermute | solution.py:48
  150.9 7.8 %collective-permute-start.30 = (bf16[512,512]{1,0:T(8,128)(2,1)S(1)}, bf16[512,512]{1,0:T(8,128)(2,1)S(1)}, u32[]{:S(2)}, u32[]{:S(2)}) collective-permute-start(bf16[512,512]{1,0:T(8,128)(2,1)S(1)} %collective-permute-done.29.refs_2_), channel_id=1, source_target_pairs={{8,0},{9,1},{10,2},{11,3},{12,4},{13,5},{14,6},{15,7},{0,8},{1,9},... | collective-permute-start | bytes 1572872 | tf_op jit(solution)/shard_map/ppermute | solution.py:48
  161.0 7.9 %blend.1 = (bf16[512,1024]{1,0:T(8,128)(2,1)}, f32[8,128]{1,0:T(8,128)}) custom-call(s32[4]{0:T(128)} %pad_add_fusion.owner_ref, bf16[512,512]{1,0:T(8,128)(2,1)} %attend.1.refs_0_, bf16[512,512]{1,0:T(8,128)(2,1)} %copy-done.9, bf16[512,512]{1,0:T(8,128)(2,1)} %copy-done.8, bf16[512,512]{1,0:T(8,128)(2,1)} %copy-done.10, ...), custom_call_target="tpu_custom_call" | custom-call | tf_op jit(solution)/shard_map/blend/pallas_call | solution.py:385
  170.9 24.2 %all_to_all.14 = f32[256,1,128]{2,1,0:T(1,128)S(1)} all-to-all(f32[256,1,128]{2,1,0:T(1,128)S(1)} %broadcast_in_dim.5), channel_id=1, replica_groups=mesh['ctx'=8,'tp'=4,'dp'=8] {'ctx','tp','dp'}, dimensions={0} | all-to-all | bytes 262144 | tf_op jit(solution)/shard_map/all_to_all | solution.py:516
  (129 shorter events, 40.2 us)
Async XLA Ops:
  7.2 153.0 %all-gather.2.cloned.1.call-start = ((), (), s32[]{:S(2)}) async-start(), calls=%async_computation.2 | async-start | bytes 4259840 | tf_op jit(solution)/shard_map/all_gather | solution.py:443
  11.8 14.9 %all-to-all-start = ((bf16[8,64,256]{2,1,0:T(8,128)(2,1)}), bf16[8,64,256]{2,1,0:T(8,128)(2,1)S(1)}, u32[]{:S(2)}, u32[]{:S(2)}) async-start(bf16[8,64,256]{2,1,0:T(8,128)(2,1)} %broadcast_in_dim.4), calls=%async_computation | async-start | bytes 524288 | tf_op jit(solution)/shard_map/all_to_all | solution.py:441
  26.7 15.5 %collective-permute-start.1 = (bf16[512,256]{1,0:T(8,128)(2,1)S(1)}, bf16[512,256]{1,0:T(8,128)(2,1)S(1)}, u32[]{:S(2)}, u32[]{:S(2)}) collective-permute-start(bf16[512,256]{1,0:T(8,128)(2,1)S(1)} %bitcast.20), channel_id=1, source_target_pairs={{32,0},{33,1},{34,2},{35,3},{36,4},{37,5},{38,6},{39,7},{40,8},{41... | collective-permute-start | bytes 786440 | tf_op jit(solution)/shard_map/ppermute | solution.py:48
  32.3 9.9 %collective-permute-start.2 = (bf16[512,256]{1,0:T(8,128)(2,1)S(1)}, bf16[512,256]{1,0:T(8,128)(2,1)S(1)}, u32[]{:S(2)}, u32[]{:S(2)}) collective-permute-start(bf16[512,256]{1,0:T(8,128)(2,1)S(1)} %bitcast.21), channel_id=1, source_target_pairs={{224,0},{225,1},{226,2},{227,3},{228,4},{229,5},{230,6},{231,7},{2... | collective-permute-start | bytes 786440 | tf_op jit(solution)/shard_map/ppermute | solution.py:48
  32.3 8.2 %collective-permute-start.3 = (bf16[128,512]{1,0:T(8,128)(2,1)S(1)}, bf16[128,512]{1,0:T(8,128)(2,1)S(1)}, u32[]{:S(2)}, u32[]{:S(2)}) collective-permute-start(bf16[128,512]{1,0:T(8,128)(2,1)S(1)} %get-tuple-element.37), channel_id=1, source_target_pairs={{32,0},{33,1},{34,2},{35,3},{36,4},{37,5},{38,6},{39,7},{40,8},{41... | collective-permute-start | bytes 393224 | tf_op jit(solution)/shard_map/ppermute | solution.py:48
  35.0 7.2 %collective-permute-start.4 = (bf16[128,512]{1,0:T(8,128)(2,1)S(1)}, bf16[128,512]{1,0:T(8,128)(2,1)S(1)}, u32[]{:S(2)}, u32[]{:S(2)}) collective-permute-start(bf16[128,512]{1,0:T(8,128)(2,1)S(1)} %get-tuple-element.37), channel_id=1, source_target_pairs={{224,0},{225,1},{226,2},{227,3},{228,4},{229,5},{230,6},{231,7},{2... | collective-permute-start | bytes 393224 | tf_op jit(solution)/shard_map/ppermute | solution.py:48
  42.2 14.2 %collective-permute-start.5 = (bf16[512,256]{1,0:T(8,128)(2,1)S(1)}, bf16[512,256]{1,0:T(8,128)(2,1)S(1)}, u32[]{:S(2)}, u32[]{:S(2)}) collective-permute-start(bf16[512,256]{1,0:T(8,128)(2,1)S(1)} %collective-permute-done.1.refs_1_), channel_id=1, source_target_pairs={{32,0},{33,1},{34,2},{35,3},{36,4},{37,5},{38,6},{39,7},{40,8},{41... | collective-permute-start | bytes 786440 | tf_op jit(solution)/shard_map/ppermute | solution.py:48
  43.3 13.1 %collective-permute-start.6 = (bf16[512,256]{1,0:T(8,128)(2,1)S(1)}, bf16[512,256]{1,0:T(8,128)(2,1)S(1)}, u32[]{:S(2)}, u32[]{:S(2)}) collective-permute-start(bf16[512,256]{1,0:T(8,128)(2,1)S(1)} %collective-permute-done.2.refs_8_), channel_id=1, source_target_pairs={{224,0},{225,1},{226,2},{227,3},{228,4},{229,5},{230,6},{231,7},{2... | collective-permute-start | bytes 786440 | tf_op jit(solution)/shard_map/ppermute | solution.py:48
  56.5 7.2 %collective-permute-start.10 = (bf16[512,256]{1,0:T(8,128)(2,1)S(1)}, bf16[512,256]{1,0:T(8,128)(2,1)S(1)}, u32[]{:S(2)}, u32[]{:S(2)}) collective-permute-start(bf16[512,256]{1,0:T(8,128)(2,1)S(1)} %collective-permute-done.6.refs_7_), channel_id=1, source_target_pairs={{224,0},{225,1},{226,2},{227,3},{228,4},{229,5},{230,6},{231,7},{2... | collective-permute-start | bytes 786440 | tf_op jit(solution)/shard_map/ppermute | solution.py:48
  65.2 6.4 %collective-permute-start.15 = (bf16[128,512]{1,0:T(8,128)(2,1)S(1)}, bf16[128,512]{1,0:T(8,128)(2,1)S(1)}, u32[]{:S(2)}, u32[]{:S(2)}) collective-permute-start(bf16[128,512]{1,0:T(8,128)(2,1)S(1)} %collective-permute-done.8), channel_id=1, source_target_pairs={{224,0},{225,1},{226,2},{227,3},{228,4},{229,5},{230,6},{231,7},{2... | collective-permute-start | bytes 393224 | tf_op jit(solution)/shard_map/ppermute | solution.py:48
  71.7 24.0 %collective-permute-start.20 = (bf16[1024,512]{1,0:T(8,128)(2,1)S(1)}, bf16[1024,512]{1,0:T(8,128)(2,1)S(1)}, u32[]{:S(2)}, u32[]{:S(2)}) collective-permute-start(bf16[1024,512]{1,0:T(8,128)(2,1)S(1)} %constant_dynamic-update-slice_fusion.refs_1_), channel_id=1, source_target_pairs={{2,0},{3,1},{4,2},{5,3},{6,4},{7,5},{0,6},{1,7},{10,8},{11,9},{12,... | collective-permute-start | bytes 3145736 | tf_op jit(solution)/shard_map/ppermute | solution.py:48
  75.5 23.4 %collective-permute-start.21 = (bf16[1024,512]{1,0:T(8,128)(2,1)S(1)}, bf16[1024,512]{1,0:T(8,128)(2,1)S(1)}, u32[]{:S(2)}, u32[]{:S(2)}) collective-permute-start(bf16[1024,512]{1,0:T(8,128)(2,1)S(1)} %constant_dynamic-update-slice_fusion.refs_1_), channel_id=1, source_target_pairs={{6,0},{7,1},{0,2},{1,3},{2,4},{3,5},{4,6},{5,7},{14,8},{15,9},{8,1... | collective-permute-start | bytes 3145736 | tf_op jit(solution)/shard_map/ppermute | solution.py:48
  88.1 7.3 %collective-permute-start.18 = (bf16[2,528,128]{2,1,0:T(8,128)(2,1)}, bf16[2,528,128]{2,1,0:T(8,128)(2,1)S(1)}, u32[]{:S(2)}, u32[]{:S(2)}) collective-permute-start(bf16[2,528,128]{2,1,0:T(8,128)(2,1)} %project_pair.1.refs_1_), channel_id=1, source_target_pairs={{224,0},{225,1},{226,2},{227,3},{228,4},{229,5},{230,6},{231,7},{2... | collective-permute-start | bytes 811016 | tf_op jit(solution)/shard_map/ppermute | solution.py:48
  93.2 8.5 %collective-permute-start.17 = (bf16[2,528,128]{2,1,0:T(8,128)(2,1)S(1)}, bf16[2,528,128]{2,1,0:T(8,128)(2,1)S(1)}, u32[]{:S(2)}, u32[]{:S(2)}) collective-permute-start(bf16[2,528,128]{2,1,0:T(8,128)(2,1)S(1)} %collective-permute-done.16.refs_2_), channel_id=1, source_target_pairs={{32,0},{33,1},{34,2},{35,3},{36,4},{37,5},{38,6},{39,7},{40,8},{41... | collective-permute-start | bytes 811016 | tf_op jit(solution)/shard_map/ppermute | solution.py:48
  95.4 9.5 %collective-permute-start.19 = (bf16[2,528,128]{2,1,0:T(8,128)(2,1)S(1)}, bf16[2,528,128]{2,1,0:T(8,128)(2,1)S(1)}, u32[]{:S(2)}, u32[]{:S(2)}) collective-permute-start(bf16[2,528,128]{2,1,0:T(8,128)(2,1)S(1)} %collective-permute-done.18.refs_9_), channel_id=1, source_target_pairs={{224,0},{225,1},{226,2},{227,3},{228,4},{229,5},{230,6},{231,7},{2... | collective-permute-start | bytes 811016 | tf_op jit(solution)/shard_map/ppermute | solution.py:48
  99.0 17.4 %collective-permute-start.26 = (bf16[512,512]{1,0:T(8,128)(2,1)S(1)}, bf16[512,512]{1,0:T(8,128)(2,1)}, u32[]{:S(2)}, u32[]{:S(2)}) collective-permute-start(bf16[512,512]{1,0:T(8,128)(2,1)S(1)} %slice.36), channel_id=1, source_target_pairs={{2,0},{3,1},{4,2},{5,3},{6,4},{7,5},{0,6},{1,7},{10,8},{11,9},{12,... | collective-permute-start | bytes 1572872 | tf_op jit(solution)/shard_map/ppermute | solution.py:48
  99.3 17.1 %collective-permute-start.27 = (bf16[512,512]{1,0:T(8,128)(2,1)S(1)}, bf16[512,512]{1,0:T(8,128)(2,1)}, u32[]{:S(2)}, u32[]{:S(2)}) collective-permute-start(bf16[512,512]{1,0:T(8,128)(2,1)S(1)} %slice.37), channel_id=1, source_target_pairs={{6,0},{7,1},{0,2},{1,3},{2,4},{3,5},{4,6},{5,7},{14,8},{15,9},{8,1... | collective-permute-start | bytes 1572872 | tf_op jit(solution)/shard_map/ppermute | solution.py:48
  104.9 8.7 %collective-permute-start.22 = (bf16[2,528,128]{2,1,0:T(8,128)(2,1)S(1)}, bf16[2,528,128]{2,1,0:T(8,128)(2,1)S(1)}, u32[]{:S(2)}, u32[]{:S(2)}) collective-permute-start(bf16[2,528,128]{2,1,0:T(8,128)(2,1)S(1)} %collective-permute-done.17.refs_3_), channel_id=1, source_target_pairs={{32,0},{33,1},{34,2},{35,3},{36,4},{37,5},{38,6},{39,7},{40,8},{41... | collective-permute-start | bytes 811016 | tf_op jit(solution)/shard_map/ppermute | solution.py:48
  105.1 9.7 %collective-permute-start.24 = (bf16[2,528,128]{2,1,0:T(8,128)(2,1)S(1)}, bf16[2,528,128]{2,1,0:T(8,128)(2,1)S(1)}, u32[]{:S(2)}, u32[]{:S(2)}) collective-permute-start(bf16[2,528,128]{2,1,0:T(8,128)(2,1)S(1)} %collective-permute-done.19.refs_8_), channel_id=1, source_target_pairs={{224,0},{225,1},{226,2},{227,3},{228,4},{229,5},{230,6},{231,7},{2... | collective-permute-start | bytes 811016 | tf_op jit(solution)/shard_map/ppermute | solution.py:48
  113.6 11.5 %collective-permute-start.23 = (bf16[1,528,128]{2,1,0:T(8,128)(2,1)S(1)}, bf16[1,528,128]{2,1,0:T(8,128)(2,1)S(1)}, u32[]{:S(2)}, u32[]{:S(2)}) collective-permute-start(bf16[1,528,128]{2,1,0:T(8,128)(2,1)S(1)} %slice.34), channel_id=1, source_target_pairs={{32,0},{33,1},{34,2},{35,3},{36,4},{37,5},{38,6},{39,7},{40,8},{41... | collective-permute-start | bytes 405512 | tf_op jit(solution)/shard_map/ppermute | solution.py:48
  114.8 10.3 %collective-permute-start.25 = (bf16[1,528,128]{2,1,0:T(8,128)(2,1)S(1)}, bf16[1,528,128]{2,1,0:T(8,128)(2,1)S(1)}, u32[]{:S(2)}, u32[]{:S(2)}) collective-permute-start(bf16[1,528,128]{2,1,0:T(8,128)(2,1)S(1)} %slice.35), channel_id=1, source_target_pairs={{224,0},{225,1},{226,2},{227,3},{228,4},{229,5},{230,6},{231,7},{2... | collective-permute-start | bytes 405512 | tf_op jit(solution)/shard_map/ppermute | solution.py:48
  139.5 11.3 %collective-permute-start.29 = (bf16[512,512]{1,0:T(8,128)(2,1)}, bf16[512,512]{1,0:T(8,128)(2,1)S(1)}, u32[]{:S(2)}, u32[]{:S(2)}) collective-permute-start(bf16[512,512]{1,0:T(8,128)(2,1)} %attend.1.refs_0_), channel_id=1, source_target_pairs={{16,0},{17,1},{18,2},{19,3},{20,4},{21,5},{22,6},{23,7},{24,8},{25... | collective-permute-start | bytes 1572872 | tf_op jit(solution)/shard_map/ppermute | solution.py:48
  140.1 19.8 %collective-permute-start.28 = (bf16[512,512]{1,0:T(8,128)(2,1)}, bf16[512,512]{1,0:T(8,128)(2,1)S(1)}, u32[]{:S(2)}, u32[]{:S(2)}) collective-permute-start(bf16[512,512]{1,0:T(8,128)(2,1)} %attend.1.refs_0_), channel_id=1, source_target_pairs={{8,0},{9,1},{10,2},{11,3},{12,4},{13,5},{14,6},{15,7},{0,8},{1,9},... | collective-permute-start | bytes 1572872 | tf_op jit(solution)/shard_map/ppermute | solution.py:48
  150.9 9.3 %collective-permute-start.30 = (bf16[512,512]{1,0:T(8,128)(2,1)S(1)}, bf16[512,512]{1,0:T(8,128)(2,1)S(1)}, u32[]{:S(2)}, u32[]{:S(2)}) collective-permute-start(bf16[512,512]{1,0:T(8,128)(2,1)S(1)} %collective-permute-done.29.refs_2_), channel_id=1, source_target_pairs={{8,0},{9,1},{10,2},{11,3},{12,4},{13,5},{14,6},{15,7},{0,8},{1,9},... | collective-permute-start | bytes 1572872 | tf_op jit(solution)/shard_map/ppermute | solution.py:48
  (32 other events, 357.5 us)
Sparse Core Ops, SparseCore 0:
  11.9 129.2 all-gather.1

commit v3 on v2

--- a/solution.py
+++ b/solution.py
@@ -130,8 +130,8 @@
     pairs = halves_of((first_any, second_any), normed_ref)
     start = 0
     for piece in refs[:count]:
-        size = piece.shape[0]
-        pairs.append((piece, buffer.at[pl.ds(start, size)]))
+        size = piece.shape[0] * 2 // 3
+        pairs.append((piece.at[pl.ds(0, size)], buffer.at[pl.ds(start, size)]))
         start += size
     run_copies(pairs, sems)
     half_rows = first_any.shape[0]
@@ -166,47 +166,56 @@
 
 
 def query_kernel(place_ref, *refs, groups, columns):
-    own_any, next_any, top_any, low_any, last_any, first_any, second_any = refs[:7]
-    cos_ref, sin_ref, out_ref, buffer, normed_ref, sums_ref, sems = refs[7:]
+    own_any, next_any, first_half, second_half, last_any, first_any, second_any = refs[:7]
+    cos_ref, sin_ref, out_ref, buffer, normed_ref, sems = refs[7:]
     depth = groups * LANES
-    half = depth // 2
-    pairs = halves_of((first_any, second_any), normed_ref)
-    for piece, step, offset in (
-        (own_any, 0, 0),
-        (next_any, 1, 0),
-        (top_any, 2, 0),
-        (low_any, 2, half),
-        (last_any, columns - 1, 0),
+    width = own_any.shape[1]
+    copies = []
+
+    def load(source, target):
+        copy = pltpu.make_async_copy(source, target, sems.at[len(copies)])
+        copy.start()
+        copies.append(copy)
+
+    for source, target in halves_of((first_any, second_any), normed_ref):
+        load(source, target)
+    for step, sources in (
+        (0, (own_any.at[pl.ds(0, depth)], own_any.at[pl.ds(depth, depth)])),
+        (1, (next_any.at[pl.ds(0, depth)], next_any.at[pl.ds(depth, depth)])),
+        (2, (first_half, second_half)),
+        (3, (last_any.at[pl.ds(0, depth)], last_any.at[pl.ds(depth, depth)])),
     ):
+        for half in range(2):
+            load(
+                sources[half],
+                buffer.at[pl.ds(step * depth, depth), pl.ds(half * width, width)],
+            )
+    copies[0].wait()
+    copies[1].wait()
+    sums = None
+    for step in range(columns):
+        copies[2 + 2 * step].wait()
+        copies[3 + 2 * step].wait()
         column = lax.rem(place_ref[1] + step, columns)
-        target = pl.multiple_of(column * depth + offset, half)
-        pairs.append((piece, buffer.at[pl.ds(target, piece.shape[0])]))
-    run_copies(pairs, sems)
-    sums_ref[...] = jnp.zeros_like(sums_ref)
-
-    def step(column, _):
         parts = []
         for group in range(groups):
             start = pl.multiple_of((group * columns + column) * LANES, LANES)
             parts.append(normed_ref[:, pl.ds(start, LANES)])
-        start = pl.multiple_of(column * depth, depth)
-        sums_ref[...] += jnp.dot(
+        term = jnp.dot(
             jnp.concatenate(parts, axis=1),
-            buffer[pl.ds(start, depth)],
+            buffer[step * depth : (step + 1) * depth],
             preferred_element_type=jnp.float32,
         )
-        return 0
-
-    lax.fori_loop(0, columns, step, 0)
-    for head in range(sums_ref.shape[1] // HD):
+        sums = term if sums is None else sums + term
+    for head in range(sums.shape[1] // HD):
         lanes = slice(head * HD, (head + 1) * HD)
-        part = turn(sums_ref[:, lanes], cos_ref[...], sin_ref[...])
+        part = turn(sums[:, lanes], cos_ref[...], sin_ref[...])
         out_ref[:, lanes] = part.astype(jnp.bfloat16)
 
 
 def project_queries(place, pieces, normed, cosine, sine, groups, columns):
     half_rows, model_width = normed[0].shape
-    width = pieces[0].shape[1]
+    width = 2 * pieces[0].shape[1]
     any_spec = pl.BlockSpec(memory_space=pl.ANY)
     vmem_spec = pl.BlockSpec(memory_space=pltpu.VMEM)
     return pl.pallas_call(
@@ -217,8 +226,7 @@
         scratch_shapes=[
             pltpu.VMEM((model_width, width), jnp.bfloat16),
             pltpu.VMEM((2 * half_rows, model_width), jnp.bfloat16),
-            pltpu.VMEM((2 * half_rows, width), jnp.float32),
-            pltpu.SemaphoreType.DMA((7,)),
+            pltpu.SemaphoreType.DMA((2 + 2 * columns,)),
         ],
         name="project_queries",
     )(place, *pieces, *normed, cosine, sine)
@@ -462,28 +470,38 @@
     seg_rows = segment_ids[0].astype(jnp.bfloat16).reshape(2, half_rows // LANES, LANES)
     seg_rows = jnp.pad(seg_rows, ((0, 0), (0, 16 - seg_rows.shape[1]), (0, 0)))
 
-    up, down = [line], [line]
-    right_up, right_down = [right], [right]
+    depth = line.shape[0]
+    fold = right.shape[0]
+    ring = jnp.concatenate([line, right[:, : 2 * HD], right[:, 2 * HD :]], axis=0)
+    up, down = [ring], [ring]
     for step in range(3):
-        ends = (up[-1], down[-1], right_up[-1], right_down[-1])
+        ends = (up[-1], down[-1])
         if step:
             ends = lax.optimization_barrier(ends + (normed[step - 1],))
-            normed[step - 1] = ends[4]
+            normed[step - 1] = ends[2]
         else:
             ends = lax.optimization_barrier(ends)
         up.append(from_z(ends[0], 1))
         down.append(from_z(ends[1], -1))
-        right_up.append(from_z(ends[2], 1))
-        right_down.append(from_z(ends[3], -1))
-    middle = line.shape[0] // 2
-    last_up, last_down, last_right, cosine, sine, seg_rows = lax.optimization_barrier(
-        (up[3][:middle], down[3][middle:], right_up[3], cosine, sine, seg_rows)
-    )
-    far_right = from_z(last_right, 1)
-    pieces = up + [from_z(last_up, 1), from_z(last_down, -1)] + down[:0:-1]
-    column = jnp.concatenate(right_up + [far_right] + right_down[:0:-1], axis=0)
+    last_up = jnp.concatenate([up[3][: depth // 2], up[3][depth : depth + fold]], axis=0)
+    last_down = jnp.concatenate([down[3][depth // 2 : depth], down[3][depth + fold :]], axis=0)
+    last_up, last_down, cosine, sine, seg_rows = lax.optimization_barrier(
+        (last_up, last_down, cosine, sine, seg_rows)
+    )
+    far_up = from_z(last_up, 1)
+    far_down = from_z(last_down, -1)
+    column = jnp.concatenate(
+        [piece[depth : depth + fold] for piece in up]
+        + [far_up[depth // 2 :]]
+        + [piece[depth : depth + fold] for piece in down[:0:-1]]
+        + [piece[depth + fold :] for piece in up]
+        + [far_down[depth // 2 :]]
+        + [piece[depth + fold :] for piece in down[:0:-1]],
+        axis=0,
+    )
     next_x = from_x(column, 1)
     last_x = from_x(column, -1)
+    pieces = up + [far_up, far_down] + down[:0:-1]
     parcel = project_pair(pieces, (after(normed[0], column), normed[1]), cosine, sine, seg_rows)
 
     parcel_up, parcel_down = [parcel], [parcel]

time: 205 us -> 197 us (0.961)
  starting transfers between devices: 60.5 us -> 48.8 us
  blocking collectives: 24.2 us -> 30.8 us
  Pallas kernels: 45.6 us -> 39.4 us
    ppermute x31 -> x24, starting transfers between devices: 53 us -> 44.7 us  [fetch(): return lax.ppermute(values, mesh_axes, pairs)]
    all_to_all x1, blocking collectives: 24.2 us -> 30.8 us  [shards(): lax.all_to_all(jnp.broadcast_to(local_total, (everyone, LANES)), mesh_axe...]
    pallas_call x1, Pallas kernels: 13.1 us -> 8.13 us  [attend(): pl.pallas_call(lambda *refs: attend_kernel(*refs, half_rows=half_rows, he...]
    all_to_all x1, waiting for transfers between devices: 2.23 us -> 7.23 us  [shards(): line = lax.all_to_all(spread, 'dp', 0, 0).reshape(-1, 2 * HD)]
    ppermute x31 -> x24, waiting for transfers between devices: 40.3 us -> 36.7 us  [fetch(): return lax.ppermute(values, mesh_axes, pairs)]
    all_to_all x1, starting transfers between devices: 7.49 us -> 4.02 us  [shards(): line = lax.all_to_all(spread, 'dp', 0, 0).reshape(-1, 2 * HD)]
  transfers between devices with their start and end apart: 33 -> 26, of which waited for: 18 -> 12; matrix products, arithmetic and copies ran while one was open for 3% -> 4% of each run, Pallas kernels for 18% -> 16%
where the time goes in v3:
time: 197 us; the launch traced here: 196 us
  starting transfers between devices  48.8 us (25%)
  waiting for transfers between devices  43.9 us (22%)
  Pallas kernels  39.4 us (20%)
  blocking collectives  30.8 us (16%)
  between operations  18.2 us (9%)
  other arithmetic  9.2 us (5%)
  local copies, waits for them, and re-layouts  5.7 us (3%)
    ppermute x24, starting transfers between devices, fetch(): return lax.ppermute(values, mesh_axes, pairs)  44.7 us
    ppermute x24, waiting for transfers between devices, fetch(): return lax.ppermute(values, mesh_axes, pairs)  36.7 us
    all_to_all x1, blocking collectives, shards(): lax.all_to_all(jnp.broadcast_to(local_total, (everyone, LANES)), mesh_axe...  30.8 us
    pallas_call x2, Pallas kernels, norm(): pl.pallas_call(lambda *refs: norm_kernel(*refs, groups=groups), grid_spec...  10 us
    pallas_call x1, Pallas kernels, attend(): pl.pallas_call(lambda *refs: attend_kernel(*refs, half_rows=half_rows, he...  8.13 us
    pallas_call x1, Pallas kernels, blend(): pl.pallas_call(blend_kernel, in_specs=[pl.BlockSpec(memory_space=pltpu.SM...  7.9 us
    pallas_call x1, Pallas kernels, project_queries(): pl.pallas_call(lambda *refs: query_kernel(*refs, groups=groups, columns=c...  7.38 us
    all_to_all x1, waiting for transfers between devices, shards(): line = lax.all_to_all(spread, 'dp', 0, 0).reshape(-1, 2 * HD)  7.23 us
  transfers between devices with their start and end apart: 26, of which 12 were waited for; matrix products, arithmetic and copies ran while one was open for 4% of the time, Pallas kernels for 16%

profile of v3, /device:TPU:1, one launch (start us, length us, event | category | flops | bytes accessed | tf_op | source)
XLA Modules:
  0.0 196.0 jit_solution(13169392658918627631)
XLA Ops:
  11.8 3.8 %collective-permute-start = (bf16[64,512]{1,0:T(8,128)(2,1)S(1)}, bf16[64,512]{1,0:T(8,128)(2,1)S(1)}, u32[]{:S(2)}, u32[]{:S(2)}) collective-permute-start(bf16[64,512]{1,0:T(8,128)(2,1)S(1)} %add_convert_fusion.1), channel_id=1, source_target_pairs={{1,0},{0,1},{3,2},{2,3},{5,4},{4,5},{7,6},{6,7},{9,8},{8,9},{11,10... | collective-permute-start | bytes 196616 | tf_op jit(solution)/shard_map/ppermute | solution.py:48
  15.6 4.0 %all-to-all-start = ((bf16[8,64,256]{2,1,0:T(8,128)(2,1)}), bf16[8,64,256]{2,1,0:T(8,128)(2,1)S(1)}, u32[]{:S(2)}, u32[]{:S(2)}) async-start(bf16[8,64,256]{2,1,0:T(8,128)(2,1)} %broadcast_in_dim.4), calls=%async_computation | async-start | bytes 524288 | tf_op jit(solution)/shard_map/all_to_all | solution.py:449
  19.7 7.2 %all-to-all-done = bf16[8,64,256]{2,1,0:T(8,128)(2,1)S(1)} async-done(((bf16[8,64,256]{2,1,0:T(8,128)(2,1)}), bf16[8,64,256]{2,1,0:T(8,128)(2,1)S(1)}, u32[]{:S(2)}, u32[]{:S(2)}) %all-to-all-start) | async-done | bytes 262176 | tf_op jit(solution)/shard_map/all_to_all | solution.py:449
  27.0 5.7 %collective-permute-start.1 = (bf16[768,256]{1,0:T(8,128)(2,1)S(1)}, bf16[768,256]{1,0:T(8,128)(2,1)S(1)}, u32[]{:S(2)}, u32[]{:S(2)}) collective-permute-start(bf16[768,256]{1,0:T(8,128)(2,1)S(1)} %pad_maximum_fusion.refs_0_), channel_id=1, source_target_pairs={{32,0},{33,1},{34,2},{35,3},{36,4},{37,5},{38,6},{39,7},{40,8},{41... | collective-permute-start | bytes 1179656 | tf_op jit(solution)/shard_map/ppermute | solution.py:48
  33.3 4.9 %norm.2.refs_9_.refs_6_ = bf16[256,4096]{1,0:T(8,128)(2,1)} custom-call(s32[2]{0:T(128)} %pad_add_fusion.1.refs_0_, bf16[512,4096]{1,0:T(8,128)(2,1)} %bitcast.18, f32[1,4096]{1,0:T(1,128)} %bitcast.22), custom_call_target="tpu_custom_call" | custom-call | tf_op jit(solution)/shard_map/norm/pallas_call | solution.py:89
  38.2 5.1 %norm.3.refs_10_.refs_7_ = bf16[256,4096]{1,0:T(8,128)(2,1)} custom-call(s32[2]{0:T(128)} %pad_add_fusion.1.refs_0_, bf16[512,4096]{1,0:T(8,128)(2,1)} %bitcast.19, f32[1,4096]{1,0:T(1,128)} %bitcast.23), custom_call_target="tpu_custom_call" | custom-call | tf_op jit(solution)/shard_map/norm/pallas_call | solution.py:89
  44.0 2.7 %collective-permute-start.3 = (bf16[768,256]{1,0:T(8,128)(2,1)S(1)}, bf16[768,256]{1,0:T(8,128)(2,1)S(1)}, u32[]{:S(2)}, u32[]{:S(2)}) collective-permute-start(bf16[768,256]{1,0:T(8,128)(2,1)S(1)} %collective-permute-done.1.refs_1_), channel_id=1, source_target_pairs={{32,0},{33,1},{34,2},{35,3},{36,4},{37,5},{38,6},{39,7},{40,8},{41... | collective-permute-start | bytes 1179656 | tf_op jit(solution)/shard_map/ppermute | solution.py:48
  49.5 3.4 %collective-permute-done.3.refs_2_ = bf16[768,256]{1,0:T(8,128)(2,1)S(1)} collective-permute-done((bf16[768,256]{1,0:T(8,128)(2,1)S(1)}, bf16[768,256]{1,0:T(8,128)(2,1)S(1)}, u32[]{:S(2)}, u32[]{:S(2)}) %collective-permute-start.3) | collective-permute-done | bytes 393248 | tf_op jit(solution)/shard_map/ppermute | solution.py:48
  52.9 2.9 %collective-permute-done.4.refs_7_ = bf16[768,256]{1,0:T(8,128)(2,1)S(1)} collective-permute-done((bf16[768,256]{1,0:T(8,128)(2,1)S(1)}, bf16[768,256]{1,0:T(8,128)(2,1)S(1)}, u32[]{:S(2)}, u32[]{:S(2)}) %collective-permute-start.4) | collective-permute-done | bytes 393248 | tf_op jit(solution)/shard_map/ppermute | solution.py:48
  57.3 6.9 %collective-permute-done.6.refs_6_ = bf16[768,256]{1,0:T(8,128)(2,1)S(1)} collective-permute-done((bf16[768,256]{1,0:T(8,128)(2,1)S(1)}, bf16[768,256]{1,0:T(8,128)(2,1)S(1)}, u32[]{:S(2)}, u32[]{:S(2)}) %collective-permute-start.6) | collective-permute-done | bytes 393248 | tf_op jit(solution)/shard_map/ppermute | solution.py:48
  65.9 4.0 %collective-permute-done.7.refs_4_ = bf16[384,256]{1,0:T(8,128)(2,1)S(1)} collective-permute-done((bf16[384,256]{1,0:T(8,128)(2,1)S(1)}, bf16[384,256]{1,0:T(8,128)(2,1)S(1)}, u32[]{:S(2)}, u32[]{:S(2)}) %collective-permute-start.7) | collective-permute-done | bytes 196640 | tf_op jit(solution)/shard_map/ppermute | solution.py:48
  70.0 1.6 collective-permute-done.8.refs_5_
  73.4 5.9 %project_pair.1.refs_1_ = bf16[2,528,128]{2,1,0:T(8,128)(2,1)} custom-call(bf16[768,256]{1,0:T(8,128)(2,1)} %copy-done.2, bf16[768,256]{1,0:T(8,128)(2,1)} %copy-done.6, bf16[768,256]{1,0:T(8,128)(2,1)} %copy-done.8, bf16[768,256]{1,0:T(8,128)(2,1)} %copy-done.5, bf16[384,256]{1,0:T(8,128)(2,1)} %copy-done.16, bf16[384,256]{1,0:T(8,128)(2,1)} %copy-done.17, ...), custom_call_target="tpu_custom_call" | custom-call | tf_op jit(solution)/shard_map/project_pair/pallas_call | solution.py:152
  81.0 4.9 %collective-permute-done.9.refs_2_ = bf16[2,528,128]{2,1,0:T(8,128)(2,1)S(1)} collective-permute-done((bf16[2,528,128]{2,1,0:T(8,128)(2,1)}, bf16[2,528,128]{2,1,0:T(8,128)(2,1)S(1)}, u32[]{:S(2)}, u32[]{:S(2)}) %collective-permute-start.9) | collective-permute-done | bytes 270368 | tf_op jit(solution)/shard_map/ppermute | solution.py:48
  87.4 7.1 %collective-permute-done.13.refs_2_ = bf16[2048,256]{1,0:T(8,128)(2,1)S(1)} collective-permute-done((bf16[2048,256]{1,0:T(8,128)(2,1)S(1)}, bf16[2048,256]{1,0:T(8,128)(2,1)S(1)}, u32[]{:S(2)}, u32[]{:S(2)}) %collective-permute-start.13) | collective-permute-done | bytes 1048608 | tf_op jit(solution)/shard_map/ppermute | solution.py:48
  97.1 2.9 %collective-permute-start.15 = (bf16[2,528,128]{2,1,0:T(8,128)(2,1)S(1)}, bf16[2,528,128]{2,1,0:T(8,128)(2,1)S(1)}, u32[]{:S(2)}, u32[]{:S(2)}) collective-permute-start(bf16[2,528,128]{2,1,0:T(8,128)(2,1)S(1)} %collective-permute-done.10.refs_3_), channel_id=1, source_target_pairs={{32,0},{33,1},{34,2},{35,3},{36,4},{37,5},{38,6},{39,7},{40,8},{41... | collective-permute-start | bytes 811016 | tf_op jit(solution)/shard_map/ppermute | solution.py:48
  100.0 4.6 %collective-permute-done.15.refs_4_ = bf16[2,528,128]{2,1,0:T(8,128)(2,1)S(1)} collective-permute-done((bf16[2,528,128]{2,1,0:T(8,128)(2,1)S(1)}, bf16[2,528,128]{2,1,0:T(8,128)(2,1)S(1)}, u32[]{:S(2)}, u32[]{:S(2)}) %collective-permute-start.15) | collective-permute-done | bytes 270368 | tf_op jit(solution)/shard_map/ppermute | solution.py:48
  105.3 3.5 %collective-permute-start.16 = (bf16[1,528,128]{2,1,0:T(8,128)(2,1)}, bf16[1,528,128]{2,1,0:T(8,128)(2,1)}, u32[]{:S(2)}, u32[]{:S(2)}) collective-permute-start(bf16[1,528,128]{2,1,0:T(8,128)(2,1)} %slice.116), channel_id=1, source_target_pairs={{32,0},{33,1},{34,2},{35,3},{36,4},{37,5},{38,6},{39,7},{40,8},{41... | collective-permute-start | bytes 405512 | tf_op jit(solution)/shard_map/ppermute | solution.py:48
  110.9 7.4 %project_queries.1.refs_10_ = bf16[512,512]{1,0:T(8,128)(2,1)} custom-call(s32[2]{0:T(128)} %pad_add_fusion.1.refs_0_, bf16[2048,256]{1,0:T(8,128)(2,1)} %copy-done.4, bf16[2048,256]{1,0:T(8,128)(2,1)} %copy-done, bf16[1024,256]{1,0:T(8,128)(2,1)} %copy-done.12, bf16[1024,256]{1,0:T(8,128)(2,1)} %collective-permute-done.20.refs_4_, ...), custom_call_target="tpu_custom_call" | custom-call | tf_op jit(solution)/shard_map/project_queries/pallas_call | solution.py:221
  118.4 8.1 %attend.1.refs_0_ = bf16[512,512]{1,0:T(8,128)(2,1)} custom-call(s32[2]{0:T(128)} %pad_add_fusion.1.refs_0_, bf16[2,528,128]{2,1,0:T(8,128)(2,1)} %project_pair.1.refs_1_, bf16[2,528,128]{2,1,0:T(8,128)(2,1)} %copy-done.18, bf16[2,528,128]{2,1,0:T(8,128)(2,1)} %copy-done.20, bf16[2,528,128]{2,1,0:T(8,128)(2,1)} %copy-done.10, ...), custom_call_target="tpu_custom_call" | custom-call | tf_op jit(solution)/shard_map/attend/pallas_call | solution.py:333
  126.6 9.0 %collective-permute-start.21 = (bf16[512,512]{1,0:T(8,128)(2,1)}, bf16[512,512]{1,0:T(8,128)(2,1)S(1)}, u32[]{:S(2)}, u32[]{:S(2)}) collective-permute-start(bf16[512,512]{1,0:T(8,128)(2,1)} %attend.1.refs_0_), channel_id=1, source_target_pairs={{8,0},{9,1},{10,2},{11,3},{12,4},{13,5},{14,6},{15,7},{0,8},{1,9},... | collective-permute-start | bytes 1572872 | tf_op jit(solution)/shard_map/ppermute | solution.py:48
  135.6 8.1 %collective-permute-start.23 = (bf16[512,512]{1,0:T(8,128)(2,1)S(1)}, bf16[512,512]{1,0:T(8,128)(2,1)S(1)}, u32[]{:S(2)}, u32[]{:S(2)}) collective-permute-start(bf16[512,512]{1,0:T(8,128)(2,1)S(1)} %collective-permute-done.22.refs_2_), channel_id=1, source_target_pairs={{8,0},{9,1},{10,2},{11,3},{12,4},{13,5},{14,6},{15,7},{0,8},{1,9},... | collective-permute-start | bytes 1572872 | tf_op jit(solution)/shard_map/ppermute | solution.py:48
  146.0 7.9 %blend.1 = (bf16[512,1024]{1,0:T(8,128)(2,1)}, f32[8,128]{1,0:T(8,128)}) custom-call(s32[4]{0:T(128)} %pad_add_fusion.owner_ref, bf16[512,512]{1,0:T(8,128)(2,1)} %attend.1.refs_0_, bf16[512,512]{1,0:T(8,128)(2,1)} %copy-done.14, bf16[512,512]{1,0:T(8,128)(2,1)} %copy-done.13, bf16[512,512]{1,0:T(8,128)(2,1)} %copy-done.15, ...), custom_call_target="tpu_custom_call" | custom-call | tf_op jit(solution)/shard_map/blend/pallas_call | solution.py:393
  155.9 30.8 %all_to_all.14 = f32[256,1,128]{2,1,0:T(1,128)S(1)} all-to-all(f32[256,1,128]{2,1,0:T(1,128)S(1)} %broadcast_in_dim.5), channel_id=1, replica_groups=mesh['ctx'=8,'tp'=4,'dp'=8] {'ctx','tp','dp'}, dimensions={0} | all-to-all | bytes 262144 | tf_op jit(solution)/shard_map/all_to_all | solution.py:534
  (128 shorter events, 25.1 us)
Async XLA Ops:
  7.2 138.1 %all-gather.2.cloned.1.call-start = ((), (), s32[]{:S(2)}) async-start(), calls=%async_computation.2 | async-start | bytes 4259840 | tf_op jit(solution)/shard_map/all_gather | solution.py:451
  11.8 7.9 %collective-permute-start = (bf16[64,512]{1,0:T(8,128)(2,1)S(1)}, bf16[64,512]{1,0:T(8,128)(2,1)S(1)}, u32[]{:S(2)}, u32[]{:S(2)}) collective-permute-start(bf16[64,512]{1,0:T(8,128)(2,1)S(1)} %add_convert_fusion.1), channel_id=1, source_target_pairs={{1,0},{0,1},{3,2},{2,3},{5,4},{4,5},{7,6},{6,7},{9,8},{8,9},{11,10... | collective-permute-start | bytes 196616 | tf_op jit(solution)/shard_map/ppermute | solution.py:48
  15.6 11.3 %all-to-all-start = ((bf16[8,64,256]{2,1,0:T(8,128)(2,1)}), bf16[8,64,256]{2,1,0:T(8,128)(2,1)S(1)}, u32[]{:S(2)}, u32[]{:S(2)}) async-start(bf16[8,64,256]{2,1,0:T(8,128)(2,1)} %broadcast_in_dim.4), calls=%async_computation | async-start | bytes 524288 | tf_op jit(solution)/shard_map/all_to_all | solution.py:449
  27.0 17.0 %collective-permute-start.1 = (bf16[768,256]{1,0:T(8,128)(2,1)S(1)}, bf16[768,256]{1,0:T(8,128)(2,1)S(1)}, u32[]{:S(2)}, u32[]{:S(2)}) collective-permute-start(bf16[768,256]{1,0:T(8,128)(2,1)S(1)} %pad_maximum_fusion.refs_0_), channel_id=1, source_target_pairs={{32,0},{33,1},{34,2},{35,3},{36,4},{37,5},{38,6},{39,7},{40,8},{41... | collective-permute-start | bytes 1179656 | tf_op jit(solution)/shard_map/ppermute | solution.py:48
  32.6 11.4 %collective-permute-start.2 = (bf16[768,256]{1,0:T(8,128)(2,1)S(1)}, bf16[768,256]{1,0:T(8,128)(2,1)S(1)}, u32[]{:S(2)}, u32[]{:S(2)}) collective-permute-start(bf16[768,256]{1,0:T(8,128)(2,1)S(1)} %pad_maximum_fusion.refs_0_), channel_id=1, source_target_pairs={{224,0},{225,1},{226,2},{227,3},{228,4},{229,5},{230,6},{231,7},{2... | collective-permute-start | bytes 1179656 | tf_op jit(solution)/shard_map/ppermute | solution.py:48
  44.0 8.9 %collective-permute-start.3 = (bf16[768,256]{1,0:T(8,128)(2,1)S(1)}, bf16[768,256]{1,0:T(8,128)(2,1)S(1)}, u32[]{:S(2)}, u32[]{:S(2)}) collective-permute-start(bf16[768,256]{1,0:T(8,128)(2,1)S(1)} %collective-permute-done.1.refs_1_), channel_id=1, source_target_pairs={{32,0},{33,1},{34,2},{35,3},{36,4},{37,5},{38,6},{39,7},{40,8},{41... | collective-permute-start | bytes 1179656 | tf_op jit(solution)/shard_map/ppermute | solution.py:48
  46.8 9.1 %collective-permute-start.4 = (bf16[768,256]{1,0:T(8,128)(2,1)S(1)}, bf16[768,256]{1,0:T(8,128)(2,1)S(1)}, u32[]{:S(2)}, u32[]{:S(2)}) collective-permute-start(bf16[768,256]{1,0:T(8,128)(2,1)S(1)} %collective-permute-done.2.refs_8_), channel_id=1, source_target_pairs={{224,0},{225,1},{226,2},{227,3},{228,4},{229,5},{230,6},{231,7},{2... | collective-permute-start | bytes 1179656 | tf_op jit(solution)/shard_map/ppermute | solution.py:48
  55.8 8.4 %collective-permute-start.5 = (bf16[768,256]{1,0:T(8,128)(2,1)S(1)}, bf16[768,256]{1,0:T(8,128)(2,1)S(1)}, u32[]{:S(2)}, u32[]{:S(2)}) collective-permute-start(bf16[768,256]{1,0:T(8,128)(2,1)S(1)} %collective-permute-done.3.refs_2_), channel_id=1, source_target_pairs={{32,0},{33,1},{34,2},{35,3},{36,4},{37,5},{38,6},{39,7},{40,8},{41... | collective-permute-start | bytes 1179656 | tf_op jit(solution)/shard_map/ppermute | solution.py:48
  56.4 7.8 %collective-permute-start.6 = (bf16[768,256]{1,0:T(8,128)(2,1)S(1)}, bf16[768,256]{1,0:T(8,128)(2,1)S(1)}, u32[]{:S(2)}, u32[]{:S(2)}) collective-permute-start(bf16[768,256]{1,0:T(8,128)(2,1)S(1)} %collective-permute-done.4.refs_7_), channel_id=1, source_target_pairs={{224,0},{225,1},{226,2},{227,3},{228,4},{229,5},{230,6},{231,7},{2... | collective-permute-start | bytes 1179656 | tf_op jit(solution)/shard_map/ppermute | solution.py:48
  64.5 7.2 %collective-permute-start.8 = (bf16[384,256]{1,0:T(8,128)(2,1)S(1)}, bf16[384,256]{1,0:T(8,128)(2,1)S(1)}, u32[]{:S(2)}, u32[]{:S(2)}) collective-permute-start(bf16[384,256]{1,0:T(8,128)(2,1)S(1)} %pad_maximum_fusion.4), channel_id=1, source_target_pairs={{224,0},{225,1},{226,2},{227,3},{228,4},{229,5},{230,6},{231,7},{2... | collective-permute-start | bytes 589832 | tf_op jit(solution)/shard_map/ppermute | solution.py:48
  71.7 22.8 %collective-permute-start.13 = (bf16[2048,256]{1,0:T(8,128)(2,1)S(1)}, bf16[2048,256]{1,0:T(8,128)(2,1)S(1)}, u32[]{:S(2)}, u32[]{:S(2)}) collective-permute-start(bf16[2048,256]{1,0:T(8,128)(2,1)S(1)} %slice_dynamic-update-slice_fusion.refs_1_), channel_id=1, source_target_pairs={{2,0},{3,1},{4,2},{5,3},{6,4},{7,5},{0,6},{1,7},{10,8},{11,9},{12,... | collective-permute-start | bytes 3145736 | tf_op jit(solution)/shard_map/ppermute | solution.py:48
  72.3 23.1 %collective-permute-start.14 = (bf16[2048,256]{1,0:T(8,128)(2,1)S(1)}, bf16[2048,256]{1,0:T(8,128)(2,1)S(1)}, u32[]{:S(2)}, u32[]{:S(2)}) collective-permute-start(bf16[2048,256]{1,0:T(8,128)(2,1)S(1)} %slice_dynamic-update-slice_fusion.refs_1_), channel_id=1, source_target_pairs={{6,0},{7,1},{0,2},{1,3},{2,4},{3,5},{4,6},{5,7},{14,8},{15,9},{8,1... | collective-permute-start | bytes 3145736 | tf_op jit(solution)/shard_map/ppermute | solution.py:48
  79.7 7.7 %collective-permute-start.11 = (bf16[2,528,128]{2,1,0:T(8,128)(2,1)}, bf16[2,528,128]{2,1,0:T(8,128)(2,1)S(1)}, u32[]{:S(2)}, u32[]{:S(2)}) collective-permute-start(bf16[2,528,128]{2,1,0:T(8,128)(2,1)} %project_pair.1.refs_1_), channel_id=1, source_target_pairs={{224,0},{225,1},{226,2},{227,3},{228,4},{229,5},{230,6},{231,7},{2... | collective-permute-start | bytes 811016 | tf_op jit(solution)/shard_map/ppermute | solution.py:48
  86.0 11.0 %collective-permute-start.10 = (bf16[2,528,128]{2,1,0:T(8,128)(2,1)S(1)}, bf16[2,528,128]{2,1,0:T(8,128)(2,1)S(1)}, u32[]{:S(2)}, u32[]{:S(2)}) collective-permute-start(bf16[2,528,128]{2,1,0:T(8,128)(2,1)S(1)} %collective-permute-done.9.refs_2_), channel_id=1, source_target_pairs={{32,0},{33,1},{34,2},{35,3},{36,4},{37,5},{38,6},{39,7},{40,8},{41... | collective-permute-start | bytes 811016 | tf_op jit(solution)/shard_map/ppermute | solution.py:48
  87.4 9.7 %collective-permute-start.12 = (bf16[2,528,128]{2,1,0:T(8,128)(2,1)S(1)}, bf16[2,528,128]{2,1,0:T(8,128)(2,1)S(1)}, u32[]{:S(2)}, u32[]{:S(2)}) collective-permute-start(bf16[2,528,128]{2,1,0:T(8,128)(2,1)S(1)} %collective-permute-done.11.refs_9_), channel_id=1, source_target_pairs={{224,0},{225,1},{226,2},{227,3},{228,4},{229,5},{230,6},{231,7},{2... | collective-permute-start | bytes 811016 | tf_op jit(solution)/shard_map/ppermute | solution.py:48
  95.4 14.7 %collective-permute-start.19 = (bf16[1024,256]{1,0:T(8,128)(2,1)S(1)}, bf16[1024,256]{1,0:T(8,128)(2,1)S(1)}, u32[]{:S(2)}, u32[]{:S(2)}) collective-permute-start(bf16[1024,256]{1,0:T(8,128)(2,1)S(1)} %slice.118), channel_id=1, source_target_pairs={{2,0},{3,1},{4,2},{5,3},{6,4},{7,5},{0,6},{1,7},{10,8},{11,9},{12,... | collective-permute-start | bytes 1572872 | tf_op jit(solution)/shard_map/ppermute | solution.py:48
  96.5 13.6 %collective-permute-start.20 = (bf16[1024,256]{1,0:T(8,128)(2,1)S(1)}, bf16[1024,256]{1,0:T(8,128)(2,1)}, u32[]{:S(2)}, u32[]{:S(2)}) collective-permute-start(bf16[1024,256]{1,0:T(8,128)(2,1)S(1)} %slice.119), channel_id=1, source_target_pairs={{6,0},{7,1},{0,2},{1,3},{2,4},{3,5},{4,6},{5,7},{14,8},{15,9},{8,1... | collective-permute-start | bytes 1572872 | tf_op jit(solution)/shard_map/ppermute | solution.py:48
  97.1 7.5 %collective-permute-start.15 = (bf16[2,528,128]{2,1,0:T(8,128)(2,1)S(1)}, bf16[2,528,128]{2,1,0:T(8,128)(2,1)S(1)}, u32[]{:S(2)}, u32[]{:S(2)}) collective-permute-start(bf16[2,528,128]{2,1,0:T(8,128)(2,1)S(1)} %collective-permute-done.10.refs_3_), channel_id=1, source_target_pairs={{32,0},{33,1},{34,2},{35,3},{36,4},{37,5},{38,6},{39,7},{40,8},{41... | collective-permute-start | bytes 811016 | tf_op jit(solution)/shard_map/ppermute | solution.py:48
  100.0 8.9 %collective-permute-start.17 = (bf16[2,528,128]{2,1,0:T(8,128)(2,1)S(1)}, bf16[2,528,128]{2,1,0:T(8,128)(2,1)S(1)}, u32[]{:S(2)}, u32[]{:S(2)}) collective-permute-start(bf16[2,528,128]{2,1,0:T(8,128)(2,1)S(1)} %collective-permute-done.12.refs_8_), channel_id=1, source_target_pairs={{224,0},{225,1},{226,2},{227,3},{228,4},{229,5},{230,6},{231,7},{2... | collective-permute-start | bytes 811016 | tf_op jit(solution)/shard_map/ppermute | solution.py:48
  105.3 13.0 %collective-permute-start.16 = (bf16[1,528,128]{2,1,0:T(8,128)(2,1)}, bf16[1,528,128]{2,1,0:T(8,128)(2,1)}, u32[]{:S(2)}, u32[]{:S(2)}) collective-permute-start(bf16[1,528,128]{2,1,0:T(8,128)(2,1)} %slice.116), channel_id=1, source_target_pairs={{32,0},{33,1},{34,2},{35,3},{36,4},{37,5},{38,6},{39,7},{40,8},{41... | collective-permute-start | bytes 405512 | tf_op jit(solution)/shard_map/ppermute | solution.py:48
  109.5 8.8 %collective-permute-start.18 = (bf16[1,528,128]{2,1,0:T(8,128)(2,1)}, bf16[1,528,128]{2,1,0:T(8,128)(2,1)}, u32[]{:S(2)}, u32[]{:S(2)}) collective-permute-start(bf16[1,528,128]{2,1,0:T(8,128)(2,1)} %slice.117), channel_id=1, source_target_pairs={{224,0},{225,1},{226,2},{227,3},{228,4},{229,5},{230,6},{231,7},{2... | collective-permute-start | bytes 405512 | tf_op jit(solution)/shard_map/ppermute | solution.py:48
  126.5 9.1 %collective-permute-start.22 = (bf16[512,512]{1,0:T(8,128)(2,1)}, bf16[512,512]{1,0:T(8,128)(2,1)S(1)}, u32[]{:S(2)}, u32[]{:S(2)}) collective-permute-start(bf16[512,512]{1,0:T(8,128)(2,1)} %attend.1.refs_0_), channel_id=1, source_target_pairs={{16,0},{17,1},{18,2},{19,3},{20,4},{21,5},{22,6},{23,7},{24,8},{25... | collective-permute-start | bytes 1572872 | tf_op jit(solution)/shard_map/ppermute | solution.py:48
  126.6 18.3 %collective-permute-start.21 = (bf16[512,512]{1,0:T(8,128)(2,1)}, bf16[512,512]{1,0:T(8,128)(2,1)S(1)}, u32[]{:S(2)}, u32[]{:S(2)}) collective-permute-start(bf16[512,512]{1,0:T(8,128)(2,1)} %attend.1.refs_0_), channel_id=1, source_target_pairs={{8,0},{9,1},{10,2},{11,3},{12,4},{13,5},{14,6},{15,7},{0,8},{1,9},... | collective-permute-start | bytes 1572872 | tf_op jit(solution)/shard_map/ppermute | solution.py:48
  135.6 9.6 %collective-permute-start.23 = (bf16[512,512]{1,0:T(8,128)(2,1)S(1)}, bf16[512,512]{1,0:T(8,128)(2,1)S(1)}, u32[]{:S(2)}, u32[]{:S(2)}) collective-permute-start(bf16[512,512]{1,0:T(8,128)(2,1)S(1)} %collective-permute-done.22.refs_2_), channel_id=1, source_target_pairs={{8,0},{9,1},{10,2},{11,3},{12,4},{13,5},{14,6},{15,7},{0,8},{1,9},... | collective-permute-start | bytes 1572872 | tf_op jit(solution)/shard_map/ppermute | solution.py:48
  (25 other events, 312.8 us)
Sparse Core Ops, SparseCore 0:
  11.9 128.7 all-gather.1

commit v4 on v3

--- a/solution.py
+++ b/solution.py
@@ -117,25 +117,47 @@
         copy.wait()
 
 
-def halves_of(normed_any, normed_ref):
-    rows = normed_any[0].shape[0]
-    return [
-        (piece, normed_ref.at[pl.ds(at * rows, rows)]) for at, piece in enumerate(normed_any)
-    ]
-
-
-def pair_kernel(*refs, count):
-    first_any, second_any, cos_ref, sin_ref, seg_ref, parcel_ref = refs[count : count + 6]
-    buffer, normed_ref, sems = refs[count + 6 :]
-    pairs = halves_of((first_any, second_any), normed_ref)
+def load_columns(normed_any, normed_ref, ranges):
+    pairs = []
+    target = 0
+    for start, size in ranges:
+        for half, source in enumerate(normed_any):
+            rows = source.shape[0]
+            pairs.append(
+                (
+                    source.at[:, pl.ds(start, size)],
+                    normed_ref.at[pl.ds(half * rows, rows), pl.ds(target, size)],
+                )
+            )
+        target += size
+    return pairs
+
+
+def pair_sums(pieces, normed_any, ranges, buffer, normed_ref, sems):
+    pairs = load_columns(normed_any, normed_ref, ranges)
     start = 0
-    for piece in refs[:count]:
+    for piece in pieces:
         size = piece.shape[0] * 2 // 3
         pairs.append((piece.at[pl.ds(0, size)], buffer.at[pl.ds(start, size)]))
         start += size
     run_copies(pairs, sems)
-    half_rows = first_any.shape[0]
-    sums = jnp.dot(normed_ref[...], buffer[...], preferred_element_type=jnp.float32)
+    return jnp.dot(normed_ref[...], buffer[...], preferred_element_type=jnp.float32)
+
+
+def pair_first_kernel(*refs, count, ranges):
+    out_ref, buffer, normed_ref, sems = refs[count + 2 :]
+    out_ref[...] = pair_sums(
+        refs[:count], refs[count : count + 2], ranges, buffer, normed_ref, sems
+    )
+
+
+def pair_last_kernel(*refs, count, ranges):
+    sums_ref, cos_ref, sin_ref, seg_ref, parcel_ref = refs[count + 2 : count + 7]
+    buffer, normed_ref, sems = refs[count + 7 :]
+    sums = sums_ref[...] + pair_sums(
+        refs[:count], refs[count : count + 2], ranges, buffer, normed_ref, sems
+    )
+    half_rows = refs[count].shape[0]
     keys = turn(sums[:, :HD], cos_ref[...], sin_ref[...]).astype(jnp.bfloat16)
     values = sums[:, HD:].astype(jnp.bfloat16)
     for half in range(2):
@@ -145,57 +167,50 @@
         parcel_ref[half, 2 * half_rows :] = seg_ref[half]
 
 
-def project_pair(pieces, normed, cosine, sine, seg_rows):
-    half_rows, model_width = normed[0].shape
+def project_pair(pieces, normed, ranges, tail=None):
+    half_rows = normed[0].shape[0]
+    depth = sum(size for _, size in ranges)
+    count = len(pieces)
     any_spec = pl.BlockSpec(memory_space=pl.ANY)
     vmem_spec = pl.BlockSpec(memory_space=pltpu.VMEM)
+    kernel = pair_first_kernel if tail is None else pair_last_kernel
+    if tail is None:
+        out = jax.ShapeDtypeStruct((2 * half_rows, 2 * HD), jnp.float32)
+    else:
+        out = jax.ShapeDtypeStruct((2, 2 * half_rows + tail[3].shape[1], HD), jnp.bfloat16)
+    extra = () if tail is None else tail
     return pl.pallas_call(
-        lambda *refs: pair_kernel(*refs, count=len(pieces)),
-        in_specs=[any_spec] * (len(pieces) + 2) + [vmem_spec] * 3,
+        lambda *refs: kernel(*refs, count=count, ranges=ranges),
+        in_specs=[any_spec] * (count + 2) + [vmem_spec] * len(extra),
         out_specs=vmem_spec,
-        out_shape=jax.ShapeDtypeStruct(
-            (2, 2 * half_rows + seg_rows.shape[1], HD), jnp.bfloat16
-        ),
+        out_shape=out,
         scratch_shapes=[
-            pltpu.VMEM((model_width, 2 * HD), jnp.bfloat16),
-            pltpu.VMEM((2 * half_rows, model_width), jnp.bfloat16),
-            pltpu.SemaphoreType.DMA((len(pieces) + 2,)),
+            pltpu.VMEM((depth, 2 * HD), jnp.bfloat16),
+            pltpu.VMEM((2 * half_rows, depth), jnp.bfloat16),
+            pltpu.SemaphoreType.DMA((count + 2 * len(ranges),)),
         ],
-        name="project_pair",
-    )(*pieces, *normed, cosine, sine, seg_rows)
-
-
-def query_kernel(place_ref, *refs, groups, columns):
-    own_any, next_any, first_half, second_half, last_any, first_any, second_any = refs[:7]
-    cos_ref, sin_ref, out_ref, buffer, normed_ref, sems = refs[7:]
+        name="pair_first" if tail is None else "pair_last",
+    )(*pieces, *normed, *extra)
+
+
+def column_parts(source, depth):
+    return (source.at[pl.ds(0, depth)], source.at[pl.ds(depth, depth)])
+
+
+def query_first_kernel(place_ref, *refs, groups, columns):
+    own_any, next_any, last_any, first_any, second_any, out_ref = refs[:6]
+    buffer, normed_ref, sems = refs[6:]
     depth = groups * LANES
     width = own_any.shape[1]
-    copies = []
-
-    def load(source, target):
-        copy = pltpu.make_async_copy(source, target, sems.at[len(copies)])
-        copy.start()
-        copies.append(copy)
-
-    for source, target in halves_of((first_any, second_any), normed_ref):
-        load(source, target)
-    for step, sources in (
-        (0, (own_any.at[pl.ds(0, depth)], own_any.at[pl.ds(depth, depth)])),
-        (1, (next_any.at[pl.ds(0, depth)], next_any.at[pl.ds(depth, depth)])),
-        (2, (first_half, second_half)),
-        (3, (last_any.at[pl.ds(0, depth)], last_any.at[pl.ds(depth, depth)])),
-    ):
-        for half in range(2):
-            load(
-                sources[half],
-                buffer.at[pl.ds(step * depth, depth), pl.ds(half * width, width)],
+    pairs = load_columns((first_any, second_any), normed_ref, ((0, normed_ref.shape[1]),))
+    for at, source in enumerate((own_any, next_any, last_any)):
+        for half, part in enumerate(column_parts(source, depth)):
+            pairs.append(
+                (part, buffer.at[pl.ds(at * depth, depth), pl.ds(half * width, width)])
             )
-    copies[0].wait()
-    copies[1].wait()
+    run_copies(pairs, sems)
     sums = None
-    for step in range(columns):
-        copies[2 + 2 * step].wait()
-        copies[3 + 2 * step].wait()
+    for at, step in enumerate((0, 1, columns - 1)):
         column = lax.rem(place_ref[1] + step, columns)
         parts = []
         for group in range(groups):
@@ -203,33 +218,58 @@
             parts.append(normed_ref[:, pl.ds(start, LANES)])
         term = jnp.dot(
             jnp.concatenate(parts, axis=1),
-            buffer[step * depth : (step + 1) * depth],
+            buffer[at * depth : (at + 1) * depth],
             preferred_element_type=jnp.float32,
         )
         sums = term if sums is None else sums + term
+    out_ref[...] = sums
+
+
+def query_last_kernel(place_ref, *refs, groups, columns):
+    top_any, low_any, first_any, second_any = refs[:4]
+    sums_ref, cos_ref, sin_ref, out_ref, buffer, normed_ref, sems = refs[4:]
+    width = top_any.shape[1]
+    column = lax.rem(place_ref[1] + columns // 2, columns)
+    ranges = [
+        (pl.multiple_of((group * columns + column) * LANES, LANES), LANES)
+        for group in range(groups)
+    ]
+    pairs = load_columns((first_any, second_any), normed_ref, ranges)
+    for half, part in enumerate((top_any, low_any)):
+        pairs.append((part, buffer.at[:, pl.ds(half * width, width)]))
+    run_copies(pairs, sems)
+    sums = sums_ref[...] + jnp.dot(
+        normed_ref[...], buffer[...], preferred_element_type=jnp.float32
+    )
     for head in range(sums.shape[1] // HD):
         lanes = slice(head * HD, (head + 1) * HD)
         part = turn(sums[:, lanes], cos_ref[...], sin_ref[...])
         out_ref[:, lanes] = part.astype(jnp.bfloat16)
 
 
-def project_queries(place, pieces, normed, cosine, sine, groups, columns):
+def project_queries(place, pieces, normed, groups, columns, tail=None):
     half_rows, model_width = normed[0].shape
     width = 2 * pieces[0].shape[1]
+    depth = groups * LANES
     any_spec = pl.BlockSpec(memory_space=pl.ANY)
     vmem_spec = pl.BlockSpec(memory_space=pltpu.VMEM)
+    kernel = query_first_kernel if tail is None else query_last_kernel
+    extra = () if tail is None else tail
+    shape = (2 * half_rows, width)
     return pl.pallas_call(
-        lambda *refs: query_kernel(*refs, groups=groups, columns=columns),
-        in_specs=[pl.BlockSpec(memory_space=pltpu.SMEM)] + [any_spec] * 7 + [vmem_spec] * 2,
+        lambda *refs: kernel(*refs, groups=groups, columns=columns),
+        in_specs=[pl.BlockSpec(memory_space=pltpu.SMEM)]
+        + [any_spec] * (len(pieces) + 2)
+        + [vmem_spec] * len(extra),
         out_specs=vmem_spec,
-        out_shape=jax.ShapeDtypeStruct((2 * half_rows, width), jnp.bfloat16),
+        out_shape=jax.ShapeDtypeStruct(shape, jnp.float32 if tail is None else jnp.bfloat16),
         scratch_shapes=[
-            pltpu.VMEM((model_width, width), jnp.bfloat16),
-            pltpu.VMEM((2 * half_rows, model_width), jnp.bfloat16),
-            pltpu.SemaphoreType.DMA((2 + 2 * columns,)),
+            pltpu.VMEM((depth * (3 if tail is None else 1), width), jnp.bfloat16),
+            pltpu.VMEM((2 * half_rows, model_width if tail is None else depth), jnp.bfloat16),
+            pltpu.SemaphoreType.DMA((8 if tail is None else 2 * groups + 2,)),
         ],
-        name="project_queries",
-    )(place, *pieces, *normed, cosine, sine)
+        name="query_first" if tail is None else "query_last",
+    )(place, *pieces, *normed, *extra)
 
 
 def attend_kernel(place_ref, *refs, half_rows, heads, ctx_count):
@@ -382,7 +422,7 @@
     part = square[:, :LANES]
     for block in range(1, square.shape[1] // LANES):
         part += square[:, block * LANES : (block + 1) * LANES]
-    square_ref[...] = part
+    square_ref[...] = jnp.sum(part, axis=0, keepdims=True)
 
 
 def blend(owners, mixed, weight):
@@ -396,7 +436,7 @@
         out_specs=[vmem_spec, vmem_spec],
         out_shape=[
             jax.ShapeDtypeStruct((count, features), jnp.bfloat16),
-            jax.ShapeDtypeStruct((8, LANES), jnp.float32),
+            jax.ShapeDtypeStruct((1, LANES), jnp.float32),
         ],
         scratch_shapes=[
             pltpu.VMEM((4, count, width), jnp.bfloat16),
@@ -458,10 +498,7 @@
 
     place = jnp.stack([ctx, x]).astype(jnp.int32)
     rows_in = tokens[0].reshape(local_rows, model_width)
-    normed = [
-        norm(place, rows_in, norm_gain, ctx_count, half * half_rows, half_rows)
-        for half in range(2)
-    ]
+    normed = [norm(place, rows_in, norm_gain, ctx_count, 0, half_rows)]
     offsets = jnp.arange(half_rows, dtype=jnp.int32)
     local_pos = jnp.concatenate(
         [ctx * half_rows + offsets, seq_len - (ctx + 1) * half_rows + offsets]
@@ -483,10 +520,20 @@
             ends = lax.optimization_barrier(ends)
         up.append(from_z(ends[0], 1))
         down.append(from_z(ends[1], -1))
+        if step == 0:
+            normed.append(
+                norm(
+                    after(place, up[1]), rows_in, norm_gain, ctx_count, half_rows, half_rows
+                )
+            )
+    span = model_width // ctx_count
+    pair_partial = project_pair(
+        [down[2], down[1], up[0], up[1], up[2]], normed, ((6 * span, 2 * span), (0, 3 * span))
+    )
     last_up = jnp.concatenate([up[3][: depth // 2], up[3][depth : depth + fold]], axis=0)
     last_down = jnp.concatenate([down[3][depth // 2 : depth], down[3][depth + fold :]], axis=0)
-    last_up, last_down, cosine, sine, seg_rows = lax.optimization_barrier(
-        (last_up, last_down, cosine, sine, seg_rows)
+    last_up, last_down, cosine, sine, seg_rows, pair_partial = lax.optimization_barrier(
+        (last_up, last_down, cosine, sine, seg_rows, pair_partial)
     )
     far_up = from_z(last_up, 1)
     far_down = from_z(last_down, -1)
@@ -501,8 +548,12 @@
     )
     next_x = from_x(column, 1)
     last_x = from_x(column, -1)
-    pieces = up + [far_up, far_down] + down[:0:-1]
-    parcel = project_pair(pieces, (after(normed[0], column), normed[1]), cosine, sine, seg_rows)
+    parcel = project_pair(
+        [up[3], far_up, far_down, down[3]],
+        (after(normed[0], column), normed[1]),
+        ((3 * span, 3 * span),),
+        (pair_partial, cosine, sine, seg_rows),
+    )
 
     parcel_up, parcel_down = [parcel], [parcel]
     for step in range(3):
@@ -511,17 +562,27 @@
             ends = lax.optimization_barrier(ends + (next_x, last_x))[:2]
         parcel_up.append(from_z(ends[0], 1))
         parcel_down.append(from_z(ends[1], -1))
-    parcels = (
-        parcel_up
-        + [from_z(parcel_up[3][:1], 1), from_z(parcel_down[3][1:], -1)]
-        + parcel_down[:0:-1]
-    )
     middle = column.shape[0] // 2
     next_half, last_half = lax.optimization_barrier(
         (next_x[:middle], last_x[middle:], parcel_up[1], parcel_down[1])
     )[:2]
-    columns_in = [column, next_x, from_x(next_half, 1), from_x(last_half, -1), last_x]
-    queries = project_queries(place, columns_in, normed, cosine, sine, ctx_count, columns)
+    query_partial = project_queries(
+        place, [column, next_x, last_x], normed, ctx_count, columns
+    )
+    last_up, last_down, query_partial = lax.optimization_barrier(
+        (parcel_up[3][:1], parcel_down[3][1:], query_partial)
+    )
+    parcels = (
+        parcel_up + [from_z(last_up, 1), from_z(last_down, -1)] + parcel_down[:0:-1]
+    )
+    queries = project_queries(
+        place,
+        [from_x(next_half, 1), from_x(last_half, -1)],
+        normed,
+        ctx_count,
+        columns,
+        (query_partial, cosine, sine),
+    )
 
     own_seg = segment_ids[0].reshape(2, 1, half_rows)
     mixed = attend(place, parcels, queries, own_seg, half_rows, heads)
@@ -529,12 +590,15 @@
     far = from_tp(mixed, 2)
     owners = jnp.stack([tp, tp ^ 1, tp ^ 2, tp ^ 3]).astype(jnp.int32)
     branch, squares = blend(owners, [mixed, near, far, from_tp(far, 1)], out_weight)
-    local_total = jnp.sum(squares) * doc_weight[0]
     everyone = ctx_count * lax.axis_size("tp") * lax.axis_size("dp")
     shares = lax.all_to_all(
-        jnp.broadcast_to(local_total, (everyone, LANES)), mesh_axes, 0, 0, tiled=True
-    )
-    loss = jnp.sum(shares[:, 0]) / (seq_len * model_width)
+        jnp.broadcast_to(squares * doc_weight[0], (everyone, LANES)),
+        mesh_axes,
+        0,
+        0,
+        tiled=True,
+    )
+    loss = jnp.sum(shares) / (seq_len * model_width)
     return (branch.reshape(1, 2, half_rows, branch.shape[1]), loss.reshape(1))
 
 

time: 197 us -> 197 us (level)
  waiting for transfers between devices: 43.9 us -> 30.3 us
  Pallas kernels: 39.4 us -> 48.6 us
  local copies, waits for them, and re-layouts: 5.7 us -> 12.9 us
    ppermute x24, waiting for transfers between devices: 36.7 us -> 24.3 us  [fetch(): return lax.ppermute(values, mesh_axes, pairs)]
    pallas_call x2 -> x4, Pallas kernels: 13.3 us -> 20 us  [the longest x2 11.9 us: project_queries(): pl.pallas_call(lambda *refs: kernel(*refs, groups=groups, columns=columns...]
    unnamed x61 -> x59, local copies, waits for them, and re-layouts: 2.2 us -> 8.15 us
    pallas_call x1, Pallas kernels: 8.13 us -> 10.8 us  [attend(): pl.pallas_call(lambda *refs: attend_kernel(*refs, half_rows=half_rows, he...]
  transfers between devices with their start and end apart: 26 -> 26, of which waited for: 12 -> 12; matrix products, arithmetic and copies ran while one was open for 4% -> 7% of each run, Pallas kernels for 16% -> 21%
where the time goes in v4:
time: 197 us
  Pallas kernels  48.6 us (25%)
  starting transfers between devices  48.5 us (25%)
  waiting for transfers between devices  30.3 us (15%)
  blocking collectives  29.8 us (15%)
  between operations  17.5 us (9%)
  local copies, waits for them, and re-layouts  12.9 us (7%)
  other arithmetic  9.22 us (5%)
    ppermute x24, starting transfers between devices, fetch(): return lax.ppermute(values, mesh_axes, pairs)  44.4 us
    all_to_all x1, blocking collectives, shards(): lax.all_to_all(jnp.broadcast_to(squares * doc_weight[0], (everyone, LANES...  29.8 us
    ppermute x24, waiting for transfers between devices, fetch(): return lax.ppermute(values, mesh_axes, pairs)  24.3 us
    pallas_call x2, Pallas kernels, project_queries(): pl.pallas_call(lambda *refs: kernel(*refs, groups=groups, columns=columns...  11.9 us
    pallas_call x1, Pallas kernels, attend(): pl.pallas_call(lambda *refs: attend_kernel(*refs, half_rows=half_rows, he...  10.8 us
    pallas_call x2, Pallas kernels, norm(): pl.pallas_call(lambda *refs: norm_kernel(*refs, groups=groups), grid_spec...  9.9 us
    unnamed x59, local copies, waits for them, and re-layouts  8.15 us
    pallas_call x2, Pallas kernels, project_pair(): pl.pallas_call(lambda *refs: kernel(*refs, count=count, ranges=ranges), i...  8.08 us
  transfers between devices with their start and end apart: 26, of which 12 were waited for; matrix products, arithmetic and copies ran while one was open for 7% of the time, Pallas kernels for 21%

profile of v4, /device:TPU:1, one launch (start us, length us, event | category | flops | bytes accessed | tf_op | source)
XLA Modules:
  0.0 196.8 jit_solution(13912917981730037509)
XLA Ops:
  11.8 3.8 %collective-permute-start = (bf16[64,512]{1,0:T(8,128)(2,1)S(1)}, bf16[64,512]{1,0:T(8,128)(2,1)S(1)}, u32[]{:S(2)}, u32[]{:S(2)}) collective-permute-start(bf16[64,512]{1,0:T(8,128)(2,1)S(1)} %add_convert_fusion.1), channel_id=1, source_target_pairs={{1,0},{0,1},{3,2},{2,3},{5,4},{4,5},{7,6},{6,7},{9,8},{8,9},{11,10... | collective-permute-start | bytes 196616 | tf_op jit(solution)/shard_map/ppermute | solution.py:48
  15.6 4.0 %all-to-all-start = ((bf16[8,64,256]{2,1,0:T(8,128)(2,1)}), bf16[8,64,256]{2,1,0:T(8,128)(2,1)S(1)}, u32[]{:S(2)}, u32[]{:S(2)}) async-start(bf16[8,64,256]{2,1,0:T(8,128)(2,1)} %broadcast_in_dim.4), calls=%async_computation | async-start | bytes 524288 | tf_op jit(solution)/shard_map/all_to_all | solution.py:489
  21.0 5.9 %all-to-all-done = bf16[8,64,256]{2,1,0:T(8,128)(2,1)S(1)} async-done(((bf16[8,64,256]{2,1,0:T(8,128)(2,1)}), bf16[8,64,256]{2,1,0:T(8,128)(2,1)S(1)}, u32[]{:S(2)}, u32[]{:S(2)}) %all-to-all-start) | async-done | bytes 262176 | tf_op jit(solution)/shard_map/all_to_all | solution.py:489
  27.0 5.7 %collective-permute-start.1 = (bf16[768,256]{1,0:T(8,128)(2,1)S(1)}, bf16[768,256]{1,0:T(8,128)(2,1)S(1)}, u32[]{:S(2)}, u32[]{:S(2)}) collective-permute-start(bf16[768,256]{1,0:T(8,128)(2,1)S(1)} %pad_maximum_fusion.refs_2_), channel_id=1, source_target_pairs={{32,0},{33,1},{34,2},{35,3},{36,4},{37,5},{38,6},{39,7},{40,8},{41... | collective-permute-start | bytes 1179656 | tf_op jit(solution)/shard_map/ppermute | solution.py:48
  33.2 4.9 %norm.2.refs_5_.refs_4_.refs_3_ = bf16[256,4096]{1,0:T(8,128)(2,1)} custom-call(s32[2]{0:T(128)} %pad_add_fusion.1.refs_0_, bf16[512,4096]{1,0:T(8,128)(2,1)} %bitcast.20, f32[1,4096]{1,0:T(1,128)} %bitcast.24), custom_call_target="tpu_custom_call" | custom-call | tf_op jit(solution)/shard_map/norm/pallas_call | solution.py:89
  39.2 3.3 %collective-permute-done.2.refs_1_ = bf16[768,256]{1,0:T(8,128)(2,1)S(1)} collective-permute-done((bf16[768,256]{1,0:T(8,128)(2,1)S(1)}, bf16[768,256]{1,0:T(8,128)(2,1)S(1)}, u32[]{:S(2)}, u32[]{:S(2)}) %collective-permute-start.2) | collective-permute-done | bytes 393248 | tf_op jit(solution)/shard_map/ppermute | solution.py:48
  46.7 5.0 %norm.3.refs_6_.refs_5_.refs_4_ = bf16[256,4096]{1,0:T(8,128)(2,1)} custom-call(s32[2]{0:T(128)} %pad_add_fusion.1.refs_0_, bf16[512,4096]{1,0:T(8,128)(2,1)} %bitcast.21, f32[1,4096]{1,0:T(1,128)} %bitcast.25), custom_call_target="tpu_custom_call" | custom-call | tf_op jit(solution)/shard_map/norm/pallas_call | solution.py:89
  54.5 3.8 %pair_first.1.refs_6_ = f32[512,256]{1,0:T(8,128)} custom-call(bf16[768,256]{1,0:T(8,128)(2,1)} %copy-done.8, bf16[768,256]{1,0:T(8,128)(2,1)} %copy-done.6, bf16[768,256]{1,0:T(8,128)(2,1)} %copy-done.2, bf16[768,256]{1,0:T(8,128)(2,1)} %copy-done.7, bf16[768,256]{1,0:T(8,128)(2,1)} %collective-permute-done.3.refs_4_, ...), custom_call_target="tpu_custom_call" | custom-call | tf_op jit(solution)/shard_map/pair_first/pallas_call | solution.py:182
  59.8 2.8 %collective-permute-start.7 = (bf16[384,256]{1,0:T(8,128)(2,1)S(1)}, bf16[384,256]{1,0:T(8,128)(2,1)S(1)}, u32[]{:S(2)}, u32[]{:S(2)}) collective-permute-start(bf16[384,256]{1,0:T(8,128)(2,1)S(1)} %pad_maximum_fusion.3), channel_id=1, source_target_pairs={{32,0},{33,1},{34,2},{35,3},{36,4},{37,5},{38,6},{39,7},{40,8},{41... | collective-permute-start | bytes 589832 | tf_op jit(solution)/shard_map/ppermute | solution.py:48
  62.7 4.2 %collective-permute-done.7.refs_1_ = bf16[384,256]{1,0:T(8,128)(2,1)S(1)} collective-permute-done((bf16[384,256]{1,0:T(8,128)(2,1)S(1)}, bf16[384,256]{1,0:T(8,128)(2,1)S(1)}, u32[]{:S(2)}, u32[]{:S(2)}) %collective-permute-start.7) | collective-permute-done | bytes 196640 | tf_op jit(solution)/shard_map/ppermute | solution.py:48
  73.7 4.3 %pair_last.1.refs_1_ = bf16[2,528,128]{2,1,0:T(8,128)(2,1)} custom-call(bf16[768,256]{1,0:T(8,128)(2,1)} %copy-done.5, bf16[384,256]{1,0:T(8,128)(2,1)} %copy-done.15, bf16[384,256]{1,0:T(8,128)(2,1)} %copy-done.16, bf16[768,256]{1,0:T(8,128)(2,1)} %copy-done.3, bf16[256,4096]{1,0:T(8,128)(2,1)} %norm.2.refs_5_.refs_4_.refs_3_, ...), custom_call_target="tpu_custom_call" | custom-call | tf_op jit(solution)/shard_map/pair_last/pallas_call | solution.py:182
  78.0 3.0 %collective-permute-start.9 = (bf16[2,528,128]{2,1,0:T(8,128)(2,1)}, bf16[2,528,128]{2,1,0:T(8,128)(2,1)S(1)}, u32[]{:S(2)}, u32[]{:S(2)}) collective-permute-start(bf16[2,528,128]{2,1,0:T(8,128)(2,1)} %pair_last.1.refs_1_), channel_id=1, source_target_pairs={{32,0},{33,1},{34,2},{35,3},{36,4},{37,5},{38,6},{39,7},{40,8},{41... | collective-permute-start | bytes 811016 | tf_op jit(solution)/shard_map/ppermute | solution.py:48
  81.0 4.2 %collective-permute-done.9.refs_2_ = bf16[2,528,128]{2,1,0:T(8,128)(2,1)S(1)} collective-permute-done((bf16[2,528,128]{2,1,0:T(8,128)(2,1)}, bf16[2,528,128]{2,1,0:T(8,128)(2,1)S(1)}, u32[]{:S(2)}, u32[]{:S(2)}) %collective-permute-start.9) | collective-permute-done | bytes 270368 | tf_op jit(solution)/shard_map/ppermute | solution.py:48
  85.1 3.3 %collective-permute-start.10 = (bf16[2,528,128]{2,1,0:T(8,128)(2,1)S(1)}, bf16[2,528,128]{2,1,0:T(8,128)(2,1)}, u32[]{:S(2)}, u32[]{:S(2)}) collective-permute-start(bf16[2,528,128]{2,1,0:T(8,128)(2,1)S(1)} %collective-permute-done.9.refs_2_), channel_id=1, source_target_pairs={{32,0},{33,1},{34,2},{35,3},{36,4},{37,5},{38,6},{39,7},{40,8},{41... | collective-permute-start | bytes 811016 | tf_op jit(solution)/shard_map/ppermute | solution.py:48
  88.6 5.6 %collective-permute-done.13.refs_2_ = bf16[2048,256]{1,0:T(8,128)(2,1)S(1)} collective-permute-done((bf16[2048,256]{1,0:T(8,128)(2,1)S(1)}, bf16[2048,256]{1,0:T(8,128)(2,1)S(1)}, u32[]{:S(2)}, u32[]{:S(2)}) %collective-permute-start.13) | collective-permute-done | bytes 1048608 | tf_op jit(solution)/shard_map/ppermute | solution.py:48
  97.8 3.2 %collective-permute-start.15 = (bf16[2,528,128]{2,1,0:T(8,128)(2,1)}, bf16[2,528,128]{2,1,0:T(8,128)(2,1)S(1)}, u32[]{:S(2)}, u32[]{:S(2)}) collective-permute-start(bf16[2,528,128]{2,1,0:T(8,128)(2,1)} %collective-permute-done.10.refs_3_), channel_id=1, source_target_pairs={{32,0},{33,1},{34,2},{35,3},{36,4},{37,5},{38,6},{39,7},{40,8},{41... | collective-permute-start | bytes 811016 | tf_op jit(solution)/shard_map/ppermute | solution.py:48
  101.0 7.0 %query_first.1.refs_5_ = f32[512,512]{1,0:T(8,128)} custom-call(s32[2]{0:T(128)} %pad_add_fusion.1.refs_0_, bf16[2048,256]{1,0:T(8,128)(2,1)} %copy-done.4, bf16[2048,256]{1,0:T(8,128)(2,1)} %copy-done, bf16[2048,256]{1,0:T(8,128)(2,1)} %copy-done.1, bf16[256,4096]{1,0:T(8,128)(2,1)} %norm.2.refs_5_.refs_4_.refs_3_, ...), custom_call_target="tpu_custom_call" | custom-call | tf_op jit(solution)/shard_map/query_first/pallas_call | solution.py:259
  108.1 3.5 %collective-permute-done.16.refs_7_ = bf16[2,528,128]{2,1,0:T(8,128)(2,1)S(1)} collective-permute-done((bf16[2,528,128]{2,1,0:T(8,128)(2,1)}, bf16[2,528,128]{2,1,0:T(8,128)(2,1)S(1)}, u32[]{:S(2)}, u32[]{:S(2)}) %collective-permute-start.16) | collective-permute-done | bytes 270368 | tf_op jit(solution)/shard_map/ppermute | solution.py:48
  114.5 4.9 %query_last.1.refs_10_ = bf16[512,512]{1,0:T(8,128)(2,1)} custom-call(s32[2]{0:T(128)} %pad_add_fusion.1.refs_0_, bf16[1024,256]{1,0:T(8,128)(2,1)} %collective-permute-done.19.refs_1_, bf16[1024,256]{1,0:T(8,128)(2,1)} %copy-done.14, bf16[256,4096]{1,0:T(8,128)(2,1)} %norm.2.refs_5_.refs_4_.refs_3_, bf16[256,4096]{1,0:T(8,128)(2,1)} %norm.3.refs_6_.refs_5_.refs_4_, ...), custom_call_target="tpu_custom_call" | custom-call | tf_op jit(solution)/shard_map/query_last/pallas_call | solution.py:259
  120.7 10.8 %attend.1.refs_0_ = bf16[512,512]{1,0:T(8,128)(2,1)} custom-call(s32[2]{0:T(128)} %pad_add_fusion.1.refs_0_, bf16[2,528,128]{2,1,0:T(8,128)(2,1)} %pair_last.1.refs_1_, bf16[2,528,128]{2,1,0:T(8,128)(2,1)} %copy-done.17, bf16[2,528,128]{2,1,0:T(8,128)(2,1)} %collective-permute-done.10.refs_3_, bf16[2,528,128]{2,1,0:T(8,128)(2,1)} %copy-done.9, ...), custom_call_target="tpu_custom_call" | custom-call | tf_op jit(solution)/shard_map/attend/pallas_call | solution.py:373
  132.7 6.1 %collective-permute-start.21 = (bf16[512,512]{1,0:T(8,128)(2,1)}, bf16[512,512]{1,0:T(8,128)(2,1)S(1)}, u32[]{:S(2)}, u32[]{:S(2)}) collective-permute-start(bf16[512,512]{1,0:T(8,128)(2,1)} %attend.1.refs_0_), channel_id=1, source_target_pairs={{8,0},{9,1},{10,2},{11,3},{12,4},{13,5},{14,6},{15,7},{0,8},{1,9},... | collective-permute-start | bytes 1572872 | tf_op jit(solution)/shard_map/ppermute | solution.py:48
  140.1 6.7 %collective-permute-start.23 = (bf16[512,512]{1,0:T(8,128)(2,1)S(1)}, bf16[512,512]{1,0:T(8,128)(2,1)S(1)}, u32[]{:S(2)}, u32[]{:S(2)}) collective-permute-start(bf16[512,512]{1,0:T(8,128)(2,1)S(1)} %collective-permute-done.22.refs_2_), channel_id=1, source_target_pairs={{8,0},{9,1},{10,2},{11,3},{12,4},{13,5},{14,6},{15,7},{0,8},{1,9},... | collective-permute-start | bytes 1572872 | tf_op jit(solution)/shard_map/ppermute | solution.py:48
  149.1 7.9 %blend.1 = (bf16[512,1024]{1,0:T(8,128)(2,1)}, f32[1,128]{1,0:T(1,128)}) custom-call(s32[4]{0:T(128)} %pad_add_fusion.owner_ref, bf16[512,512]{1,0:T(8,128)(2,1)} %attend.1.refs_0_, bf16[512,512]{1,0:T(8,128)(2,1)} %copy-done.12, bf16[512,512]{1,0:T(8,128)(2,1)} %copy-done.11, bf16[512,512]{1,0:T(8,128)(2,1)} %copy-done.13, ...), custom_call_target="tpu_custom_call" | custom-call | tf_op jit(solution)/shard_map/blend/pallas_call | solution.py:433
  157.7 29.8 %all_to_all.11 = f32[256,1,128]{2,1,0:T(1,128)S(1)} all-to-all(f32[256,1,128]{2,1,0:T(1,128)S(1)} %broadcast_in_dim.5), channel_id=1, replica_groups=mesh['ctx'=8,'tp'=4,'dp'=8] {'ctx','tp','dp'}, dimensions={0} | all-to-all | bytes 262144 | tf_op jit(solution)/shard_map/all_to_all | solution.py:594
  (128 shorter events, 35.5 us)
Async XLA Ops:
  7.2 141.1 %all-gather.2.cloned.1.call-start = ((), (), s32[]{:S(2)}) async-start(), calls=%async_computation.2 | async-start | bytes 4259840 | tf_op jit(solution)/shard_map/all_gather | solution.py:491
  11.8 9.2 %collective-permute-start = (bf16[64,512]{1,0:T(8,128)(2,1)S(1)}, bf16[64,512]{1,0:T(8,128)(2,1)S(1)}, u32[]{:S(2)}, u32[]{:S(2)}) collective-permute-start(bf16[64,512]{1,0:T(8,128)(2,1)S(1)} %add_convert_fusion.1), channel_id=1, source_target_pairs={{1,0},{0,1},{3,2},{2,3},{5,4},{4,5},{7,6},{6,7},{9,8},{8,9},{11,10... | collective-permute-start | bytes 196616 | tf_op jit(solution)/shard_map/ppermute | solution.py:48
  15.6 11.3 %all-to-all-start = ((bf16[8,64,256]{2,1,0:T(8,128)(2,1)}), bf16[8,64,256]{2,1,0:T(8,128)(2,1)S(1)}, u32[]{:S(2)}, u32[]{:S(2)}) async-start(bf16[8,64,256]{2,1,0:T(8,128)(2,1)} %broadcast_in_dim.4), calls=%async_computation | async-start | bytes 524288 | tf_op jit(solution)/shard_map/all_to_all | solution.py:489
  27.0 12.2 %collective-permute-start.1 = (bf16[768,256]{1,0:T(8,128)(2,1)S(1)}, bf16[768,256]{1,0:T(8,128)(2,1)S(1)}, u32[]{:S(2)}, u32[]{:S(2)}) collective-permute-start(bf16[768,256]{1,0:T(8,128)(2,1)S(1)} %pad_maximum_fusion.refs_2_), channel_id=1, source_target_pairs={{32,0},{33,1},{34,2},{35,3},{36,4},{37,5},{38,6},{39,7},{40,8},{41... | collective-permute-start | bytes 1179656 | tf_op jit(solution)/shard_map/ppermute | solution.py:48
  32.6 9.9 %collective-permute-start.2 = (bf16[768,256]{1,0:T(8,128)(2,1)S(1)}, bf16[768,256]{1,0:T(8,128)(2,1)S(1)}, u32[]{:S(2)}, u32[]{:S(2)}) collective-permute-start(bf16[768,256]{1,0:T(8,128)(2,1)S(1)} %pad_maximum_fusion.refs_2_), channel_id=1, source_target_pairs={{224,0},{225,1},{226,2},{227,3},{228,4},{229,5},{230,6},{231,7},{2... | collective-permute-start | bytes 1179656 | tf_op jit(solution)/shard_map/ppermute | solution.py:48
  42.5 9.2 %collective-permute-start.3 = (bf16[768,256]{1,0:T(8,128)(2,1)S(1)}, bf16[768,256]{1,0:T(8,128)(2,1)}, u32[]{:S(2)}, u32[]{:S(2)}) collective-permute-start(bf16[768,256]{1,0:T(8,128)(2,1)S(1)} %collective-permute-done.1.refs_3_), channel_id=1, source_target_pairs={{32,0},{33,1},{34,2},{35,3},{36,4},{37,5},{38,6},{39,7},{40,8},{41... | collective-permute-start | bytes 1179656 | tf_op jit(solution)/shard_map/ppermute | solution.py:48
  42.6 9.0 %collective-permute-start.4 = (bf16[768,256]{1,0:T(8,128)(2,1)S(1)}, bf16[768,256]{1,0:T(8,128)(2,1)S(1)}, u32[]{:S(2)}, u32[]{:S(2)}) collective-permute-start(bf16[768,256]{1,0:T(8,128)(2,1)S(1)} %collective-permute-done.2.refs_1_), channel_id=1, source_target_pairs={{224,0},{225,1},{226,2},{227,3},{228,4},{229,5},{230,6},{231,7},{2... | collective-permute-start | bytes 1179656 | tf_op jit(solution)/shard_map/ppermute | solution.py:48
  51.7 8.0 %collective-permute-start.6 = (bf16[768,256]{1,0:T(8,128)(2,1)S(1)}, bf16[768,256]{1,0:T(8,128)(2,1)S(1)}, u32[]{:S(2)}, u32[]{:S(2)}) collective-permute-start(bf16[768,256]{1,0:T(8,128)(2,1)S(1)} %collective-permute-done.4.refs_0_), channel_id=1, source_target_pairs={{224,0},{225,1},{226,2},{227,3},{228,4},{229,5},{230,6},{231,7},{2... | collective-permute-start | bytes 1179656 | tf_op jit(solution)/shard_map/ppermute | solution.py:48
  51.8 7.9 %collective-permute-start.5 = (bf16[768,256]{1,0:T(8,128)(2,1)}, bf16[768,256]{1,0:T(8,128)(2,1)S(1)}, u32[]{:S(2)}, u32[]{:S(2)}) collective-permute-start(bf16[768,256]{1,0:T(8,128)(2,1)} %collective-permute-done.3.refs_4_), channel_id=1, source_target_pairs={{32,0},{33,1},{34,2},{35,3},{36,4},{37,5},{38,6},{39,7},{40,8},{41... | collective-permute-start | bytes 1179656 | tf_op jit(solution)/shard_map/ppermute | solution.py:48
  62.7 7.7 %collective-permute-start.8 = (bf16[384,256]{1,0:T(8,128)(2,1)S(1)}, bf16[384,256]{1,0:T(8,128)(2,1)S(1)}, u32[]{:S(2)}, u32[]{:S(2)}) collective-permute-start(bf16[384,256]{1,0:T(8,128)(2,1)S(1)} %pad_maximum_fusion.4), channel_id=1, source_target_pairs={{224,0},{225,1},{226,2},{227,3},{228,4},{229,5},{230,6},{231,7},{2... | collective-permute-start | bytes 589832 | tf_op jit(solution)/shard_map/ppermute | solution.py:48
  72.2 22.1 %collective-permute-start.13 = (bf16[2048,256]{1,0:T(8,128)(2,1)S(1)}, bf16[2048,256]{1,0:T(8,128)(2,1)S(1)}, u32[]{:S(2)}, u32[]{:S(2)}) collective-permute-start(bf16[2048,256]{1,0:T(8,128)(2,1)S(1)} %slice_dynamic-update-slice_fusion.refs_1_), channel_id=1, source_target_pairs={{2,0},{3,1},{4,2},{5,3},{6,4},{7,5},{0,6},{1,7},{10,8},{11,9},{12,... | collective-permute-start | bytes 3145736 | tf_op jit(solution)/shard_map/ppermute | solution.py:48
  72.7 22.5 %collective-permute-start.14 = (bf16[2048,256]{1,0:T(8,128)(2,1)S(1)}, bf16[2048,256]{1,0:T(8,128)(2,1)S(1)}, u32[]{:S(2)}, u32[]{:S(2)}) collective-permute-start(bf16[2048,256]{1,0:T(8,128)(2,1)S(1)} %slice_dynamic-update-slice_fusion.refs_1_), channel_id=1, source_target_pairs={{6,0},{7,1},{0,2},{1,3},{2,4},{3,5},{4,6},{5,7},{14,8},{15,9},{8,1... | collective-permute-start | bytes 3145736 | tf_op jit(solution)/shard_map/ppermute | solution.py:48
  81.0 7.7 %collective-permute-start.11 = (bf16[2,528,128]{2,1,0:T(8,128)(2,1)}, bf16[2,528,128]{2,1,0:T(8,128)(2,1)S(1)}, u32[]{:S(2)}, u32[]{:S(2)}) collective-permute-start(bf16[2,528,128]{2,1,0:T(8,128)(2,1)} %pair_last.1.refs_1_), channel_id=1, source_target_pairs={{224,0},{225,1},{226,2},{227,3},{228,4},{229,5},{230,6},{231,7},{2... | collective-permute-start | bytes 811016 | tf_op jit(solution)/shard_map/ppermute | solution.py:48
  85.1 12.4 %collective-permute-start.10 = (bf16[2,528,128]{2,1,0:T(8,128)(2,1)S(1)}, bf16[2,528,128]{2,1,0:T(8,128)(2,1)}, u32[]{:S(2)}, u32[]{:S(2)}) collective-permute-start(bf16[2,528,128]{2,1,0:T(8,128)(2,1)S(1)} %collective-permute-done.9.refs_2_), channel_id=1, source_target_pairs={{32,0},{33,1},{34,2},{35,3},{36,4},{37,5},{38,6},{39,7},{40,8},{41... | collective-permute-start | bytes 811016 | tf_op jit(solution)/shard_map/ppermute | solution.py:48
  88.6 9.2 %collective-permute-start.12 = (bf16[2,528,128]{2,1,0:T(8,128)(2,1)S(1)}, bf16[2,528,128]{2,1,0:T(8,128)(2,1)}, u32[]{:S(2)}, u32[]{:S(2)}) collective-permute-start(bf16[2,528,128]{2,1,0:T(8,128)(2,1)S(1)} %collective-permute-done.11.refs_9_), channel_id=1, source_target_pairs={{224,0},{225,1},{226,2},{227,3},{228,4},{229,5},{230,6},{231,7},{2... | collective-permute-start | bytes 811016 | tf_op jit(solution)/shard_map/ppermute | solution.py:48
  96.1 17.6 %collective-permute-start.19 = (bf16[1024,256]{1,0:T(8,128)(2,1)}, bf16[1024,256]{1,0:T(8,128)(2,1)}, u32[]{:S(2)}, u32[]{:S(2)}) collective-permute-start(bf16[1024,256]{1,0:T(8,128)(2,1)} %slice.114), channel_id=1, source_target_pairs={{2,0},{3,1},{4,2},{5,3},{6,4},{7,5},{0,6},{1,7},{10,8},{11,9},{12,... | collective-permute-start | bytes 1572872 | tf_op jit(solution)/shard_map/ppermute | solution.py:48
  97.0 16.7 %collective-permute-start.20 = (bf16[1024,256]{1,0:T(8,128)(2,1)}, bf16[1024,256]{1,0:T(8,128)(2,1)S(1)}, u32[]{:S(2)}, u32[]{:S(2)}) collective-permute-start(bf16[1024,256]{1,0:T(8,128)(2,1)} %slice.115), channel_id=1, source_target_pairs={{6,0},{7,1},{0,2},{1,3},{2,4},{3,5},{4,6},{5,7},{14,8},{15,9},{8,1... | collective-permute-start | bytes 1572872 | tf_op jit(solution)/shard_map/ppermute | solution.py:48
  97.8 10.2 %collective-permute-start.15 = (bf16[2,528,128]{2,1,0:T(8,128)(2,1)}, bf16[2,528,128]{2,1,0:T(8,128)(2,1)S(1)}, u32[]{:S(2)}, u32[]{:S(2)}) collective-permute-start(bf16[2,528,128]{2,1,0:T(8,128)(2,1)} %collective-permute-done.10.refs_3_), channel_id=1, source_target_pairs={{32,0},{33,1},{34,2},{35,3},{36,4},{37,5},{38,6},{39,7},{40,8},{41... | collective-permute-start | bytes 811016 | tf_op jit(solution)/shard_map/ppermute | solution.py:48
  101.0 10.5 %collective-permute-start.16 = (bf16[2,528,128]{2,1,0:T(8,128)(2,1)}, bf16[2,528,128]{2,1,0:T(8,128)(2,1)S(1)}, u32[]{:S(2)}, u32[]{:S(2)}) collective-permute-start(bf16[2,528,128]{2,1,0:T(8,128)(2,1)} %collective-permute-done.12.refs_8_), channel_id=1, source_target_pairs={{224,0},{225,1},{226,2},{227,3},{228,4},{229,5},{230,6},{231,7},{2... | collective-permute-start | bytes 811016 | tf_op jit(solution)/shard_map/ppermute | solution.py:48
  111.6 7.9 %collective-permute-start.17 = (bf16[1,528,128]{2,1,0:T(8,128)(2,1)S(1)}, bf16[1,528,128]{2,1,0:T(8,128)(2,1)S(1)}, u32[]{:S(2)}, u32[]{:S(2)}) collective-permute-start(bf16[1,528,128]{2,1,0:T(8,128)(2,1)S(1)} %slice.112), channel_id=1, source_target_pairs={{32,0},{33,1},{34,2},{35,3},{36,4},{37,5},{38,6},{39,7},{40,8},{41... | collective-permute-start | bytes 405512 | tf_op jit(solution)/shard_map/ppermute | solution.py:48
  111.6 7.8 %collective-permute-start.18 = (bf16[1,528,128]{2,1,0:T(8,128)(2,1)S(1)}, bf16[1,528,128]{2,1,0:T(8,128)(2,1)S(1)}, u32[]{:S(2)}, u32[]{:S(2)}) collective-permute-start(bf16[1,528,128]{2,1,0:T(8,128)(2,1)S(1)} %slice.113), channel_id=1, source_target_pairs={{224,0},{225,1},{226,2},{227,3},{228,4},{229,5},{230,6},{231,7},{2... | collective-permute-start | bytes 405512 | tf_op jit(solution)/shard_map/ppermute | solution.py:48
  131.6 8.5 %collective-permute-start.22 = (bf16[512,512]{1,0:T(8,128)(2,1)}, bf16[512,512]{1,0:T(8,128)(2,1)S(1)}, u32[]{:S(2)}, u32[]{:S(2)}) collective-permute-start(bf16[512,512]{1,0:T(8,128)(2,1)} %attend.1.refs_0_), channel_id=1, source_target_pairs={{16,0},{17,1},{18,2},{19,3},{20,4},{21,5},{22,6},{23,7},{24,8},{25... | collective-permute-start | bytes 1572872 | tf_op jit(solution)/shard_map/ppermute | solution.py:48
  132.7 15.4 %collective-permute-start.21 = (bf16[512,512]{1,0:T(8,128)(2,1)}, bf16[512,512]{1,0:T(8,128)(2,1)S(1)}, u32[]{:S(2)}, u32[]{:S(2)}) collective-permute-start(bf16[512,512]{1,0:T(8,128)(2,1)} %attend.1.refs_0_), channel_id=1, source_target_pairs={{8,0},{9,1},{10,2},{11,3},{12,4},{13,5},{14,6},{15,7},{0,8},{1,9},... | collective-permute-start | bytes 1572872 | tf_op jit(solution)/shard_map/ppermute | solution.py:48
  140.1 8.2 %collective-permute-start.23 = (bf16[512,512]{1,0:T(8,128)(2,1)S(1)}, bf16[512,512]{1,0:T(8,128)(2,1)S(1)}, u32[]{:S(2)}, u32[]{:S(2)}) collective-permute-start(bf16[512,512]{1,0:T(8,128)(2,1)S(1)} %collective-permute-done.22.refs_2_), channel_id=1, source_target_pairs={{8,0},{9,1},{10,2},{11,3},{12,4},{13,5},{14,6},{15,7},{0,8},{1,9},... | collective-permute-start | bytes 1572872 | tf_op jit(solution)/shard_map/ppermute | solution.py:48
  (24 other events, 222.8 us)
Sparse Core Ops, SparseCore 0:
  11.9 129.0 all-gather.1

commit v5 on v4

--- a/solution.py
+++ b/solution.py
@@ -193,21 +193,40 @@
     )(*pieces, *normed, *extra)
 
 
-def column_parts(source, depth):
-    return (source.at[pl.ds(0, depth)], source.at[pl.ds(depth, depth)])
+def place_columns(source, rows, buffer, first, half, near, late):
+    width = source.shape[1]
+    head = 3 * LANES
+    lanes = pl.ds(half * width, width)
+    depth = 8 * LANES
+    pairs = []
+    if near:
+        pairs.append(
+            (source.at[pl.ds(rows, head)], buffer.at[pl.ds(first, head), lanes])
+        )
+        tail = 2 * LANES
+        pairs.append(
+            (
+                source.at[pl.ds(rows + head, tail)],
+                buffer.at[pl.ds(first + depth - tail, tail), lanes],
+            )
+        )
+        rows += head + tail
+    if late:
+        pairs.append(
+            (source.at[pl.ds(rows, head)], buffer.at[pl.ds(first + head, head), lanes])
+        )
+    return pairs
 
 
 def query_first_kernel(place_ref, *refs, groups, columns):
-    own_any, next_any, last_any, first_any, second_any, out_ref = refs[:6]
-    buffer, normed_ref, sems = refs[6:]
+    first_any, second_any, out_ref, buffer, normed_ref, sems = refs[6:]
     depth = groups * LANES
-    width = own_any.shape[1]
     pairs = load_columns((first_any, second_any), normed_ref, ((0, normed_ref.shape[1]),))
-    for at, source in enumerate((own_any, next_any, last_any)):
-        for half, part in enumerate(column_parts(source, depth)):
-            pairs.append(
-                (part, buffer.at[pl.ds(at * depth, depth), pl.ds(half * width, width)])
-            )
+    for at in range(3):
+        near, late = refs[2 * at : 2 * at + 2]
+        for half in range(2):
+            pairs += place_columns(near, half * 5 * LANES, buffer, at * depth, half, True, False)
+            pairs += place_columns(late, half * 3 * LANES, buffer, at * depth, half, False, True)
     run_copies(pairs, sems)
     sums = None
     for at, step in enumerate((0, 1, columns - 1)):
@@ -228,7 +247,6 @@
 def query_last_kernel(place_ref, *refs, groups, columns):
     top_any, low_any, first_any, second_any = refs[:4]
     sums_ref, cos_ref, sin_ref, out_ref, buffer, normed_ref, sems = refs[4:]
-    width = top_any.shape[1]
     column = lax.rem(place_ref[1] + columns // 2, columns)
     ranges = [
         (pl.multiple_of((group * columns + column) * LANES, LANES), LANES)
@@ -236,7 +254,7 @@
     ]
     pairs = load_columns((first_any, second_any), normed_ref, ranges)
     for half, part in enumerate((top_any, low_any)):
-        pairs.append((part, buffer.at[:, pl.ds(half * width, width)]))
+        pairs += place_columns(part, 0, buffer, 0, half, True, True)
     run_copies(pairs, sems)
     sums = sums_ref[...] + jnp.dot(
         normed_ref[...], buffer[...], preferred_element_type=jnp.float32
@@ -266,7 +284,7 @@
         scratch_shapes=[
             pltpu.VMEM((depth * (3 if tail is None else 1), width), jnp.bfloat16),
             pltpu.VMEM((2 * half_rows, model_width if tail is None else depth), jnp.bfloat16),
-            pltpu.SemaphoreType.DMA((8 if tail is None else 2 * groups + 2,)),
+            pltpu.SemaphoreType.DMA((20 if tail is None else 2 * groups + 6,)),
         ],
         name="query_first" if tail is None else "query_last",
     )(place, *pieces, *normed, *extra)
@@ -476,6 +494,9 @@
     heads = query_weight.shape[1] // HD
     width = heads * HD
 
+    own_out = perturbed(output_weight, output_noise, factor).T
+    out_weight = lax.all_gather(own_out, ("ctx", "dp"), axis=0, tiled=True)
+    key_weight, query_weight = lax.optimization_barrier((key_weight, query_weight, own_out))[:2]
     own_pair = perturbed(
         jnp.concatenate([key_weight, value_weight], axis=1),
         jnp.concatenate([key_noise, value_noise], axis=1),
@@ -487,8 +508,6 @@
     spread, own_query = lax.optimization_barrier((spread, own_query))
     other = from_y(own_query)
     line = lax.all_to_all(spread, "dp", 0, 0).reshape(-1, 2 * HD)
-    own_out = perturbed(after(output_weight, own_query), output_noise, factor).T
-    out_weight = lax.all_gather(own_out, ("ctx", "dp"), axis=0, tiled=True)
     even = lax.axis_index("dp") % 2 == 0
     right = jnp.where(
         even,
@@ -530,58 +549,76 @@
     pair_partial = project_pair(
         [down[2], down[1], up[0], up[1], up[2]], normed, ((6 * span, 2 * span), (0, 3 * span))
     )
+    near_pieces = [up[0], up[1], up[2], down[2], down[1]]
+    near = jnp.concatenate(
+        [piece[depth : depth + fold] for piece in near_pieces]
+        + [piece[depth + fold :] for piece in near_pieces],
+        axis=0,
+    )
     last_up = jnp.concatenate([up[3][: depth // 2], up[3][depth : depth + fold]], axis=0)
     last_down = jnp.concatenate([down[3][depth // 2 : depth], down[3][depth + fold :]], axis=0)
-    last_up, last_down, cosine, sine, seg_rows, pair_partial = lax.optimization_barrier(
-        (last_up, last_down, cosine, sine, seg_rows, pair_partial)
-    )
+    last_up, last_down, cosine, sine, seg_rows, pair_partial, near = lax.optimization_barrier(
+        (last_up, last_down, cosine, sine, seg_rows, pair_partial, near)
+    )
+    near_next = from_x(near, 1)
+    near_last = from_x(near, -1)
     far_up = from_z(last_up, 1)
     far_down = from_z(last_down, -1)
-    column = jnp.concatenate(
-        [piece[depth : depth + fold] for piece in up]
-        + [far_up[depth // 2 :]]
-        + [piece[depth : depth + fold] for piece in down[:0:-1]]
-        + [piece[depth + fold :] for piece in up]
-        + [far_down[depth // 2 :]]
-        + [piece[depth + fold :] for piece in down[:0:-1]],
+    late = jnp.concatenate(
+        [
+            up[3][depth : depth + fold],
+            far_up[depth // 2 :],
+            down[3][depth : depth + fold],
+            up[3][depth + fold :],
+            far_down[depth // 2 :],
+            down[3][depth + fold :],
+        ],
         axis=0,
     )
-    next_x = from_x(column, 1)
-    last_x = from_x(column, -1)
     parcel = project_pair(
         [up[3], far_up, far_down, down[3]],
-        (after(normed[0], column), normed[1]),
+        normed,
         ((3 * span, 3 * span),),
         (pair_partial, cosine, sine, seg_rows),
     )
 
-    parcel_up, parcel_down = [parcel], [parcel]
-    for step in range(3):
-        ends = (parcel_up[-1], parcel_down[-1])
-        if step == 2:
-            ends = lax.optimization_barrier(ends + (next_x, last_x))[:2]
-        parcel_up.append(from_z(ends[0], 1))
-        parcel_down.append(from_z(ends[1], -1))
-    middle = column.shape[0] // 2
-    next_half, last_half = lax.optimization_barrier(
-        (next_x[:middle], last_x[middle:], parcel_up[1], parcel_down[1])
-    )[:2]
+    late, near_next, near_last, _ = lax.optimization_barrier(
+        (late, near_next, near_last, parcel)
+    )
+    late_next = from_x(late, 1)
+    late_last = from_x(late, -1)
+
+    parcel_up = [parcel, from_z(parcel, 1)]
+    parcel_down = [parcel, from_z(parcel, -1)]
+    ends = lax.optimization_barrier((parcel_up[1], parcel_down[1], near_next, near_last))
+    parcel_up.append(from_z(ends[0], 1))
+    parcel_down.append(from_z(ends[1], -1))
+    near_half = near.shape[0] // 2
+    late_half = late.shape[0] // 2
+    far_next = from_x(
+        jnp.concatenate([near_next[:near_half], late_next[:late_half]], axis=0), 1
+    )
+    far_last = from_x(
+        jnp.concatenate([near_last[near_half:], late_last[late_half:]], axis=0), -1
+    )
     query_partial = project_queries(
-        place, [column, next_x, last_x], normed, ctx_count, columns
-    )
-    last_up, last_down, query_partial = lax.optimization_barrier(
-        (parcel_up[3][:1], parcel_down[3][1:], query_partial)
-    )
-    parcels = (
-        parcel_up + [from_z(last_up, 1), from_z(last_down, -1)] + parcel_down[:0:-1]
-    )
-    queries = project_queries(
         place,
-        [from_x(next_half, 1), from_x(last_half, -1)],
+        [near, late, near_next, late_next, near_last, late_last],
         normed,
         ctx_count,
         columns,
-        (query_partial, cosine, sine),
+    )
+    ends = lax.optimization_barrier((parcel_up[2], parcel_down[2], query_partial))
+    parcel_up.append(from_z(ends[0], 1))
+    parcel_down.append(from_z(ends[1], -1))
+    queries = project_queries(
+        place, [far_next, far_last], normed, ctx_count, columns, (ends[2], cosine, sine)
+    )
+    last_up, last_down, queries = lax.optimization_barrier(
+        (parcel_up[3][:1], parcel_down[3][1:], queries)
+    )
+    parcels = (
+        parcel_up + [from_z(last_up, 1), from_z(last_down, -1)] + parcel_down[:0:-1]
     )
 
     own_seg = segment_ids[0].reshape(2, 1, half_rows)

time: 197 us -> 213 us (1.081)
  starting transfers between devices: 48.5 us -> 56.9 us
  waiting for transfers between devices: 30.3 us -> 35.5 us
    ppermute x24 -> x26, starting transfers between devices: 44.4 us -> 52.8 us  [fetch(): return lax.ppermute(values, mesh_axes, pairs)]
    ppermute x24 -> x26, waiting for transfers between devices: 24.3 us -> 28.3 us  [fetch(): return lax.ppermute(values, mesh_axes, pairs)]
    unnamed x59 -> x64, local copies, waits for them, and re-layouts: 8.15 us -> 10.7 us
  transfers between devices with their start and end apart: 26 -> 28, of which waited for: 12 -> 13; matrix products, arithmetic and copies ran while one was open for 7% -> 9% of each run, Pallas kernels for 21% -> 19%
where the time goes in v5:
time: 213 us; the launch traced here: 211 us
  starting transfers between devices  56.9 us (27%)
  Pallas kernels  47.2 us (22%)
  waiting for transfers between devices  35.5 us (17%)
  blocking collectives  29.3 us (14%)
  between operations  17.5 us (8%)
  local copies, waits for them, and re-layouts  14.5 us (7%)
  other arithmetic  10.4 us (5%)
    ppermute x26, starting transfers between devices, fetch(): return lax.ppermute(values, mesh_axes, pairs)  52.8 us
    all_to_all x1, blocking collectives, shards(): lax.all_to_all(jnp.broadcast_to(squares * doc_weight[0], (everyone, LANES...  29.3 us
    ppermute x26, waiting for transfers between devices, fetch(): return lax.ppermute(values, mesh_axes, pairs)  28.3 us
    pallas_call x2, Pallas kernels, project_queries(): pl.pallas_call(lambda *refs: kernel(*refs, groups=groups, columns=columns...  11.7 us
    unnamed x64, local copies, waits for them, and re-layouts  10.7 us
    pallas_call x2, Pallas kernels, norm(): pl.pallas_call(lambda *refs: norm_kernel(*refs, groups=groups), grid_spec...  9.93 us
    pallas_call x1, Pallas kernels, attend(): pl.pallas_call(lambda *refs: attend_kernel(*refs, half_rows=half_rows, he...  9.69 us
    pallas_call x2, Pallas kernels, project_pair(): pl.pallas_call(lambda *refs: kernel(*refs, count=count, ranges=ranges), i...  7.96 us
  transfers between devices with their start and end apart: 28, of which 13 were waited for; matrix products, arithmetic and copies ran while one was open for 9% of the time, Pallas kernels for 19%

profile of v5, /device:TPU:1, one launch (start us, length us, event | category | flops | bytes accessed | tf_op | source)
XLA Modules:
  0.0 211.2 jit_solution(4878248523963452089)
XLA Ops:
  11.8 3.7 %collective-permute-start = (bf16[64,512]{1,0:T(8,128)(2,1)S(1)}, bf16[64,512]{1,0:T(8,128)(2,1)S(1)}, u32[]{:S(2)}, u32[]{:S(2)}) collective-permute-start(bf16[64,512]{1,0:T(8,128)(2,1)S(1)} %add_convert_fusion), channel_id=1, source_target_pairs={{1,0},{0,1},{3,2},{2,3},{5,4},{4,5},{7,6},{6,7},{9,8},{8,9},{11,10... | collective-permute-start | bytes 196616 | tf_op jit(solution)/shard_map/ppermute | solution.py:48
  15.5 4.0 %all-to-all-start = ((bf16[8,64,256]{2,1,0:T(8,128)(2,1)}), bf16[8,64,256]{2,1,0:T(8,128)(2,1)S(1)}, u32[]{:S(2)}, u32[]{:S(2)}) async-start(bf16[8,64,256]{2,1,0:T(8,128)(2,1)} %broadcast_in_dim.4), calls=%async_computation | async-start | bytes 524288 | tf_op jit(solution)/shard_map/all_to_all | solution.py:510
  19.7 7.2 %all-to-all-done = bf16[8,64,256]{2,1,0:T(8,128)(2,1)S(1)} async-done(((bf16[8,64,256]{2,1,0:T(8,128)(2,1)}), bf16[8,64,256]{2,1,0:T(8,128)(2,1)S(1)}, u32[]{:S(2)}, u32[]{:S(2)}) %all-to-all-start) | async-done | bytes 262176 | tf_op jit(solution)/shard_map/all_to_all | solution.py:510
  26.9 5.7 %collective-permute-start.1 = (bf16[768,256]{1,0:T(8,128)(2,1)S(1)}, bf16[768,256]{1,0:T(8,128)(2,1)S(1)}, u32[]{:S(2)}, u32[]{:S(2)}) collective-permute-start(bf16[768,256]{1,0:T(8,128)(2,1)S(1)} %pad_maximum_fusion.2.refs_2_), channel_id=1, source_target_pairs={{32,0},{33,1},{34,2},{35,3},{36,4},{37,5},{38,6},{39,7},{40,8},{41... | collective-permute-start | bytes 1179656 | tf_op jit(solution)/shard_map/ppermute | solution.py:48
  33.2 4.9 %norm.2.refs_5_.refs_4_.refs_7_.refs_3_ = bf16[256,4096]{1,0:T(8,128)(2,1)} custom-call(s32[2]{0:T(128)} %pad_add_fusion.1.refs_0_, bf16[512,4096]{1,0:T(8,128)(2,1)} %bitcast.20, f32[1,4096]{1,0:T(1,128)} %bitcast.24), custom_call_target="tpu_custom_call" | custom-call | tf_op jit(solution)/shard_map/norm/pallas_call | solution.py:89
  39.2 3.3 %collective-permute-done.2.refs_1_ = bf16[768,256]{1,0:T(8,128)(2,1)S(1)} collective-permute-done((bf16[768,256]{1,0:T(8,128)(2,1)S(1)}, bf16[768,256]{1,0:T(8,128)(2,1)S(1)}, u32[]{:S(2)}, u32[]{:S(2)}) %collective-permute-start.2) | collective-permute-done | bytes 393248 | tf_op jit(solution)/shard_map/ppermute | solution.py:48
  46.3 5.0 %norm.3.refs_6_.refs_5_.refs_8_.refs_4_ = bf16[256,4096]{1,0:T(8,128)(2,1)} custom-call(s32[2]{0:T(128)} %pad_add_fusion.1.refs_0_, bf16[512,4096]{1,0:T(8,128)(2,1)} %bitcast.21, f32[1,4096]{1,0:T(1,128)} %bitcast.25), custom_call_target="tpu_custom_call" | custom-call | tf_op jit(solution)/shard_map/norm/pallas_call | solution.py:89
  51.5 2.7 %collective-permute-start.5 = (bf16[768,256]{1,0:T(8,128)(2,1)S(1)}, bf16[768,256]{1,0:T(8,128)(2,1)S(1)}, u32[]{:S(2)}, u32[]{:S(2)}) collective-permute-start(bf16[768,256]{1,0:T(8,128)(2,1)S(1)} %collective-permute-done.3.refs_4_), channel_id=1, source_target_pairs={{32,0},{33,1},{34,2},{35,3},{36,4},{37,5},{38,6},{39,7},{40,8},{41... | collective-permute-start | bytes 1179656 | tf_op jit(solution)/shard_map/ppermute | solution.py:48
  54.1 3.8 %pair_first.1.refs_6_ = f32[512,256]{1,0:T(8,128)} custom-call(bf16[768,256]{1,0:T(8,128)(2,1)} %copy-done.11, bf16[768,256]{1,0:T(8,128)(2,1)} %copy-done.8, bf16[768,256]{1,0:T(8,128)(2,1)} %copy-done, bf16[768,256]{1,0:T(8,128)(2,1)} %copy-done.9, bf16[768,256]{1,0:T(8,128)(2,1)} %copy-done.10, bf16[256,4096]{1,0:T(8,128)(2,1)} %norm.2.refs_5_.refs_4_.refs_7_.refs_3_, ...), custom_call_target="tpu_custom_call" | custom-call | tf_op jit(solution)/shard_map/pair_first/pallas_call | solution.py:182
  71.5 4.2 %pair_last.1.refs_1_ = bf16[2,528,128]{2,1,0:T(8,128)(2,1)} custom-call(bf16[768,256]{1,0:T(8,128)(2,1)} %copy-done.4, bf16[384,256]{1,0:T(8,128)(2,1)} %copy-done.19, bf16[384,256]{1,0:T(8,128)(2,1)} %copy-done.18, bf16[768,256]{1,0:T(8,128)(2,1)} %copy-done.3, bf16[256,4096]{1,0:T(8,128)(2,1)} %norm.2.refs_5_.refs_4_.refs_7_.refs_3_, ...), custom_call_target="tpu_custom_call" | custom-call | tf_op jit(solution)/shard_map/pair_last/pallas_call | solution.py:182
  79.9 3.7 %collective-permute-done.11.refs_3_ = bf16[1280,256]{1,0:T(8,128)(2,1)S(1)} collective-permute-done((bf16[1280,256]{1,0:T(8,128)(2,1)S(1)}, bf16[1280,256]{1,0:T(8,128)(2,1)S(1)}, u32[]{:S(2)}, u32[]{:S(2)}) %collective-permute-start.11) | collective-permute-done | bytes 655392 | tf_op jit(solution)/shard_map/ppermute | solution.py:48
  91.5 2.7 %collective-permute-start.13 = (bf16[2,528,128]{2,1,0:T(8,128)(2,1)S(1)}, bf16[2,528,128]{2,1,0:T(8,128)(2,1)}, u32[]{:S(2)}, u32[]{:S(2)}) collective-permute-start(bf16[2,528,128]{2,1,0:T(8,128)(2,1)S(1)} %collective-permute-done.9.refs_2_), channel_id=1, source_target_pairs={{32,0},{33,1},{34,2},{35,3},{36,4},{37,5},{38,6},{39,7},{40,8},{41... | collective-permute-start | bytes 811016 | tf_op jit(solution)/shard_map/ppermute | solution.py:48
  98.9 6.7 %query_first.1.refs_5_ = f32[512,512]{1,0:T(8,128)} custom-call(s32[2]{0:T(128)} %pad_add_fusion.1.refs_0_, bf16[1280,256]{1,0:T(8,128)(2,1)} %copy-done.7, bf16[768,256]{1,0:T(8,128)(2,1)} %copy-done.14, bf16[1280,256]{1,0:T(8,128)(2,1)} %copy-done.1, bf16[768,256]{1,0:T(8,128)(2,1)} %copy-done.6, bf16[1280,256]{1,0:T(8,128)(2,1)} %copy-done.2, ...), custom_call_target="tpu_custom_call" | custom-call | tf_op jit(solution)/shard_map/query_first/pallas_call | solution.py:277
  105.6 2.7 %collective-permute-start.17 = (bf16[2,528,128]{2,1,0:T(8,128)(2,1)}, bf16[2,528,128]{2,1,0:T(8,128)(2,1)S(1)}, u32[]{:S(2)}, u32[]{:S(2)}) collective-permute-start(bf16[2,528,128]{2,1,0:T(8,128)(2,1)} %collective-permute-done.13.refs_3_), channel_id=1, source_target_pairs={{32,0},{33,1},{34,2},{35,3},{36,4},{37,5},{38,6},{39,7},{40,8},{41... | collective-permute-start | bytes 811016 | tf_op jit(solution)/shard_map/ppermute | solution.py:48
  108.3 4.1 %collective-permute-done.17.refs_4_ = bf16[2,528,128]{2,1,0:T(8,128)(2,1)S(1)} collective-permute-done((bf16[2,528,128]{2,1,0:T(8,128)(2,1)}, bf16[2,528,128]{2,1,0:T(8,128)(2,1)S(1)}, u32[]{:S(2)}, u32[]{:S(2)}) %collective-permute-start.17) | collective-permute-done | bytes 270368 | tf_op jit(solution)/shard_map/ppermute | solution.py:48
  112.5 3.3 %collective-permute-done.18.refs_7_ = bf16[2,528,128]{2,1,0:T(8,128)(2,1)S(1)} collective-permute-done((bf16[2,528,128]{2,1,0:T(8,128)(2,1)}, bf16[2,528,128]{2,1,0:T(8,128)(2,1)S(1)}, u32[]{:S(2)}, u32[]{:S(2)}) %collective-permute-start.18) | collective-permute-done | bytes 270368 | tf_op jit(solution)/shard_map/ppermute | solution.py:48
  115.8 5.0 %query_last.1.refs_10_ = bf16[512,512]{1,0:T(8,128)(2,1)} custom-call(s32[2]{0:T(128)} %pad_add_fusion.1.refs_0_, bf16[1024,256]{1,0:T(8,128)(2,1)} %collective-permute-done.19.refs_1_, bf16[1024,256]{1,0:T(8,128)(2,1)} %collective-permute-done.20.refs_2_, bf16[256,4096]{1,0:T(8,128)(2,1)} %norm.2.refs_5_.refs_4_.refs_7_.refs_3_, ...), custom_call_target="tpu_custom_call" | custom-call | tf_op jit(solution)/shard_map/query_last/pallas_call | solution.py:277
  122.9 4.3 %collective-permute-done.21.refs_5_ = bf16[1,528,128]{2,1,0:T(8,128)(2,1)S(1)} collective-permute-done((bf16[1,528,128]{2,1,0:T(8,128)(2,1)S(1)}, bf16[1,528,128]{2,1,0:T(8,128)(2,1)S(1)}, u32[]{:S(2)}, u32[]{:S(2)}) %collective-permute-start.21) | collective-permute-done | bytes 135200 | tf_op jit(solution)/shard_map/ppermute | solution.py:48
  127.2 2.9 %collective-permute-done.22.refs_6_ = bf16[1,528,128]{2,1,0:T(8,128)(2,1)S(1)} collective-permute-done((bf16[1,528,128]{2,1,0:T(8,128)(2,1)S(1)}, bf16[1,528,128]{2,1,0:T(8,128)(2,1)S(1)}, u32[]{:S(2)}, u32[]{:S(2)}) %collective-permute-start.22) | collective-permute-done | bytes 135200 | tf_op jit(solution)/shard_map/ppermute | solution.py:48
  130.8 9.7 %attend.1.refs_0_ = bf16[512,512]{1,0:T(8,128)(2,1)} custom-call(s32[2]{0:T(128)} %pad_add_fusion.1.refs_0_, bf16[2,528,128]{2,1,0:T(8,128)(2,1)} %pair_last.1.refs_1_, bf16[2,528,128]{2,1,0:T(8,128)(2,1)} %copy-done.21, bf16[2,528,128]{2,1,0:T(8,128)(2,1)} %collective-permute-done.13.refs_3_, bf16[2,528,128]{2,1,0:T(8,128)(2,1)} %copy-done.12, ...), custom_call_target="tpu_custom_call" | custom-call | tf_op jit(solution)/shard_map/attend/pallas_call | solution.py:391
  140.6 11.8 %collective-permute-start.23 = (bf16[512,512]{1,0:T(8,128)(2,1)}, bf16[512,512]{1,0:T(8,128)(2,1)S(1)}, u32[]{:S(2)}, u32[]{:S(2)}) collective-permute-start(bf16[512,512]{1,0:T(8,128)(2,1)} %attend.1.refs_0_), channel_id=1, source_target_pairs={{8,0},{9,1},{10,2},{11,3},{12,4},{13,5},{14,6},{15,7},{0,8},{1,9},... | collective-permute-start | bytes 1572872 | tf_op jit(solution)/shard_map/ppermute | solution.py:48
  152.4 9.3 %collective-permute-start.25 = (bf16[512,512]{1,0:T(8,128)(2,1)S(1)}, bf16[512,512]{1,0:T(8,128)(2,1)S(1)}, u32[]{:S(2)}, u32[]{:S(2)}) collective-permute-start(bf16[512,512]{1,0:T(8,128)(2,1)S(1)} %collective-permute-done.24.refs_2_), channel_id=1, source_target_pairs={{8,0},{9,1},{10,2},{11,3},{12,4},{13,5},{14,6},{15,7},{0,8},{1,9},... | collective-permute-start | bytes 1572872 | tf_op jit(solution)/shard_map/ppermute | solution.py:48
  164.1 7.9 %blend.1 = (bf16[512,1024]{1,0:T(8,128)(2,1)}, f32[1,128]{1,0:T(1,128)}) custom-call(s32[4]{0:T(128)} %pad_add_fusion.owner_ref, bf16[512,512]{1,0:T(8,128)(2,1)} %attend.1.refs_0_, bf16[512,512]{1,0:T(8,128)(2,1)} %copy-done.16, bf16[512,512]{1,0:T(8,128)(2,1)} %copy-done.15, bf16[512,512]{1,0:T(8,128)(2,1)} %copy-done.17, ...), custom_call_target="tpu_custom_call" | custom-call | tf_op jit(solution)/shard_map/blend/pallas_call | solution.py:451
  172.7 29.3 %all_to_all.11 = f32[256,1,128]{2,1,0:T(1,128)S(1)} all-to-all(f32[256,1,128]{2,1,0:T(1,128)S(1)} %broadcast_in_dim.5), channel_id=1, replica_groups=mesh['ctx'=8,'tp'=4,'dp'=8] {'ctx','tp','dp'}, dimensions={0} | all-to-all | bytes 262144 | tf_op jit(solution)/shard_map/all_to_all | solution.py:631
  (142 shorter events, 45.8 us)
Async XLA Ops:
  7.2 156.1 %all-gather.2.cloned.1.call-start = ((), (), s32[]{:S(2)}) async-start(), calls=%async_computation.2 | async-start | bytes 4259840 | tf_op jit(solution)/shard_map/all_gather | solution.py:498
  11.8 7.8 %collective-permute-start = (bf16[64,512]{1,0:T(8,128)(2,1)S(1)}, bf16[64,512]{1,0:T(8,128)(2,1)S(1)}, u32[]{:S(2)}, u32[]{:S(2)}) collective-permute-start(bf16[64,512]{1,0:T(8,128)(2,1)S(1)} %add_convert_fusion), channel_id=1, source_target_pairs={{1,0},{0,1},{3,2},{2,3},{5,4},{4,5},{7,6},{6,7},{9,8},{8,9},{11,10... | collective-permute-start | bytes 196616 | tf_op jit(solution)/shard_map/ppermute | solution.py:48
  15.5 11.3 %all-to-all-start = ((bf16[8,64,256]{2,1,0:T(8,128)(2,1)}), bf16[8,64,256]{2,1,0:T(8,128)(2,1)S(1)}, u32[]{:S(2)}, u32[]{:S(2)}) async-start(bf16[8,64,256]{2,1,0:T(8,128)(2,1)} %broadcast_in_dim.4), calls=%async_computation | async-start | bytes 524288 | tf_op jit(solution)/shard_map/all_to_all | solution.py:510
  26.9 12.3 %collective-permute-start.1 = (bf16[768,256]{1,0:T(8,128)(2,1)S(1)}, bf16[768,256]{1,0:T(8,128)(2,1)S(1)}, u32[]{:S(2)}, u32[]{:S(2)}) collective-permute-start(bf16[768,256]{1,0:T(8,128)(2,1)S(1)} %pad_maximum_fusion.2.refs_2_), channel_id=1, source_target_pairs={{32,0},{33,1},{34,2},{35,3},{36,4},{37,5},{38,6},{39,7},{40,8},{41... | collective-permute-start | bytes 1179656 | tf_op jit(solution)/shard_map/ppermute | solution.py:48
  32.6 9.9 %collective-permute-start.2 = (bf16[768,256]{1,0:T(8,128)(2,1)S(1)}, bf16[768,256]{1,0:T(8,128)(2,1)S(1)}, u32[]{:S(2)}, u32[]{:S(2)}) collective-permute-start(bf16[768,256]{1,0:T(8,128)(2,1)S(1)} %pad_maximum_fusion.2.refs_2_), channel_id=1, source_target_pairs={{224,0},{225,1},{226,2},{227,3},{228,4},{229,5},{230,6},{231,7},{2... | collective-permute-start | bytes 1179656 | tf_op jit(solution)/shard_map/ppermute | solution.py:48
  42.5 8.8 %collective-permute-start.3 = (bf16[768,256]{1,0:T(8,128)(2,1)S(1)}, bf16[768,256]{1,0:T(8,128)(2,1)S(1)}, u32[]{:S(2)}, u32[]{:S(2)}) collective-permute-start(bf16[768,256]{1,0:T(8,128)(2,1)S(1)} %collective-permute-done.1.refs_3_), channel_id=1, source_target_pairs={{32,0},{33,1},{34,2},{35,3},{36,4},{37,5},{38,6},{39,7},{40,8},{41... | collective-permute-start | bytes 1179656 | tf_op jit(solution)/shard_map/ppermute | solution.py:48
  42.6 8.8 %collective-permute-start.4 = (bf16[768,256]{1,0:T(8,128)(2,1)S(1)}, bf16[768,256]{1,0:T(8,128)(2,1)S(1)}, u32[]{:S(2)}, u32[]{:S(2)}) collective-permute-start(bf16[768,256]{1,0:T(8,128)(2,1)S(1)} %collective-permute-done.2.refs_1_), channel_id=1, source_target_pairs={{224,0},{225,1},{226,2},{227,3},{228,4},{229,5},{230,6},{231,7},{2... | collective-permute-start | bytes 1179656 | tf_op jit(solution)/shard_map/ppermute | solution.py:48
  51.5 12.4 %collective-permute-start.6 = (bf16[768,256]{1,0:T(8,128)(2,1)S(1)}, bf16[768,256]{1,0:T(8,128)(2,1)S(1)}, u32[]{:S(2)}, u32[]{:S(2)}) collective-permute-start(bf16[768,256]{1,0:T(8,128)(2,1)S(1)} %collective-permute-done.4.refs_0_), channel_id=1, source_target_pairs={{224,0},{225,1},{226,2},{227,3},{228,4},{229,5},{230,6},{231,7},{2... | collective-permute-start | bytes 1179656 | tf_op jit(solution)/shard_map/ppermute | solution.py:48
  51.5 12.5 %collective-permute-start.5 = (bf16[768,256]{1,0:T(8,128)(2,1)S(1)}, bf16[768,256]{1,0:T(8,128)(2,1)S(1)}, u32[]{:S(2)}, u32[]{:S(2)}) collective-permute-start(bf16[768,256]{1,0:T(8,128)(2,1)S(1)} %collective-permute-done.3.refs_4_), channel_id=1, source_target_pairs={{32,0},{33,1},{34,2},{35,3},{36,4},{37,5},{38,6},{39,7},{40,8},{41... | collective-permute-start | bytes 1179656 | tf_op jit(solution)/shard_map/ppermute | solution.py:48
  65.6 18.1 %collective-permute-start.11 = (bf16[1280,256]{1,0:T(8,128)(2,1)S(1)}, bf16[1280,256]{1,0:T(8,128)(2,1)S(1)}, u32[]{:S(2)}, u32[]{:S(2)}) collective-permute-start(bf16[1280,256]{1,0:T(8,128)(2,1)S(1)} %slice_dynamic-update-slice_fusion.4.refs_1_), channel_id=1, source_target_pairs={{2,0},{3,1},{4,2},{5,3},{6,4},{7,5},{0,6},{1,7},{10,8},{11,9},{12,... | collective-permute-start | bytes 1966088 | tf_op jit(solution)/shard_map/ppermute | solution.py:48
  66.0 18.1 %collective-permute-start.12 = (bf16[1280,256]{1,0:T(8,128)(2,1)S(1)}, bf16[1280,256]{1,0:T(8,128)(2,1)S(1)}, u32[]{:S(2)}, u32[]{:S(2)}) collective-permute-start(bf16[1280,256]{1,0:T(8,128)(2,1)S(1)} %slice_dynamic-update-slice_fusion.4.refs_1_), channel_id=1, source_target_pairs={{6,0},{7,1},{0,2},{1,3},{2,4},{3,5},{4,6},{5,7},{14,8},{15,9},{8,1... | collective-permute-start | bytes 1966088 | tf_op jit(solution)/shard_map/ppermute | solution.py:48
  84.1 10.2 %collective-permute-start.16 = (bf16[768,256]{1,0:T(8,128)(2,1)S(1)}, bf16[768,256]{1,0:T(8,128)(2,1)S(1)}, u32[]{:S(2)}, u32[]{:S(2)}) collective-permute-start(bf16[768,256]{1,0:T(8,128)(2,1)S(1)} %constant_dynamic-update-slice_fusion.2.refs_2_), channel_id=1, source_target_pairs={{6,0},{7,1},{0,2},{1,3},{2,4},{3,5},{4,6},{5,7},{14,8},{15,9},{8,1... | collective-permute-start | bytes 1179656 | tf_op jit(solution)/shard_map/ppermute | solution.py:48
  84.1 7.5 %collective-permute-start.10 = (bf16[2,528,128]{2,1,0:T(8,128)(2,1)}, bf16[2,528,128]{2,1,0:T(8,128)(2,1)S(1)}, u32[]{:S(2)}, u32[]{:S(2)}) collective-permute-start(bf16[2,528,128]{2,1,0:T(8,128)(2,1)} %pair_last.1.refs_1_), channel_id=1, source_target_pairs={{224,0},{225,1},{226,2},{227,3},{228,4},{229,5},{230,6},{231,7},{2... | collective-permute-start | bytes 811016 | tf_op jit(solution)/shard_map/ppermute | solution.py:48
  87.1 9.4 %collective-permute-start.15 = (bf16[768,256]{1,0:T(8,128)(2,1)S(1)}, bf16[768,256]{1,0:T(8,128)(2,1)S(1)}, u32[]{:S(2)}, u32[]{:S(2)}) collective-permute-start(bf16[768,256]{1,0:T(8,128)(2,1)S(1)} %constant_dynamic-update-slice_fusion.2.refs_2_), channel_id=1, source_target_pairs={{2,0},{3,1},{4,2},{5,3},{6,4},{7,5},{0,6},{1,7},{10,8},{11,9},{12,... | collective-permute-start | bytes 1179656 | tf_op jit(solution)/shard_map/ppermute | solution.py:48
  91.5 14.0 %collective-permute-start.13 = (bf16[2,528,128]{2,1,0:T(8,128)(2,1)S(1)}, bf16[2,528,128]{2,1,0:T(8,128)(2,1)}, u32[]{:S(2)}, u32[]{:S(2)}) collective-permute-start(bf16[2,528,128]{2,1,0:T(8,128)(2,1)S(1)} %collective-permute-done.9.refs_2_), channel_id=1, source_target_pairs={{32,0},{33,1},{34,2},{35,3},{36,4},{37,5},{38,6},{39,7},{40,8},{41... | collective-permute-start | bytes 811016 | tf_op jit(solution)/shard_map/ppermute | solution.py:48
  94.3 11.3 %collective-permute-start.14 = (bf16[2,528,128]{2,1,0:T(8,128)(2,1)S(1)}, bf16[2,528,128]{2,1,0:T(8,128)(2,1)}, u32[]{:S(2)}, u32[]{:S(2)}) collective-permute-start(bf16[2,528,128]{2,1,0:T(8,128)(2,1)S(1)} %collective-permute-done.10.refs_9_), channel_id=1, source_target_pairs={{224,0},{225,1},{226,2},{227,3},{228,4},{229,5},{230,6},{231,7},{2... | collective-permute-start | bytes 811016 | tf_op jit(solution)/shard_map/ppermute | solution.py:48
  95.2 20.5 %collective-permute-start.20 = (bf16[1024,256]{1,0:T(8,128)(2,1)}, bf16[1024,256]{1,0:T(8,128)(2,1)}, u32[]{:S(2)}, u32[]{:S(2)}) collective-permute-start(bf16[1024,256]{1,0:T(8,128)(2,1)} %pad_maximum_fusion.1), channel_id=1, source_target_pairs={{6,0},{7,1},{0,2},{1,3},{2,4},{3,5},{4,6},{5,7},{14,8},{15,9},{8,1... | collective-permute-start | bytes 1572872 | tf_op jit(solution)/shard_map/ppermute | solution.py:48
  97.5 18.3 %collective-permute-start.19 = (bf16[1024,256]{1,0:T(8,128)(2,1)}, bf16[1024,256]{1,0:T(8,128)(2,1)}, u32[]{:S(2)}, u32[]{:S(2)}) collective-permute-start(bf16[1024,256]{1,0:T(8,128)(2,1)} %pad_maximum_fusion), channel_id=1, source_target_pairs={{2,0},{3,1},{4,2},{5,3},{6,4},{7,5},{0,6},{1,7},{10,8},{11,9},{12,... | collective-permute-start | bytes 1572872 | tf_op jit(solution)/shard_map/ppermute | solution.py:48
  105.6 6.9 %collective-permute-start.17 = (bf16[2,528,128]{2,1,0:T(8,128)(2,1)}, bf16[2,528,128]{2,1,0:T(8,128)(2,1)S(1)}, u32[]{:S(2)}, u32[]{:S(2)}) collective-permute-start(bf16[2,528,128]{2,1,0:T(8,128)(2,1)} %collective-permute-done.13.refs_3_), channel_id=1, source_target_pairs={{32,0},{33,1},{34,2},{35,3},{36,4},{37,5},{38,6},{39,7},{40,8},{41... | collective-permute-start | bytes 811016 | tf_op jit(solution)/shard_map/ppermute | solution.py:48
  108.3 7.4 %collective-permute-start.18 = (bf16[2,528,128]{2,1,0:T(8,128)(2,1)}, bf16[2,528,128]{2,1,0:T(8,128)(2,1)S(1)}, u32[]{:S(2)}, u32[]{:S(2)}) collective-permute-start(bf16[2,528,128]{2,1,0:T(8,128)(2,1)} %collective-permute-done.14.refs_8_), channel_id=1, source_target_pairs={{224,0},{225,1},{226,2},{227,3},{228,4},{229,5},{230,6},{231,7},{2... | collective-permute-start | bytes 811016 | tf_op jit(solution)/shard_map/ppermute | solution.py:48
  121.1 9.1 %collective-permute-start.22 = (bf16[1,528,128]{2,1,0:T(8,128)(2,1)S(1)}, bf16[1,528,128]{2,1,0:T(8,128)(2,1)S(1)}, u32[]{:S(2)}, u32[]{:S(2)}) collective-permute-start(bf16[1,528,128]{2,1,0:T(8,128)(2,1)S(1)} %slice.121), channel_id=1, source_target_pairs={{224,0},{225,1},{226,2},{227,3},{228,4},{229,5},{230,6},{231,7},{2... | collective-permute-start | bytes 405512 | tf_op jit(solution)/shard_map/ppermute | solution.py:48
  140.5 11.9 %collective-permute-start.24 = (bf16[512,512]{1,0:T(8,128)(2,1)}, bf16[512,512]{1,0:T(8,128)(2,1)S(1)}, u32[]{:S(2)}, u32[]{:S(2)}) collective-permute-start(bf16[512,512]{1,0:T(8,128)(2,1)} %attend.1.refs_0_), channel_id=1, source_target_pairs={{16,0},{17,1},{18,2},{19,3},{20,4},{21,5},{22,6},{23,7},{24,8},{25... | collective-permute-start | bytes 1572872 | tf_op jit(solution)/shard_map/ppermute | solution.py:48
  140.6 22.4 %collective-permute-start.23 = (bf16[512,512]{1,0:T(8,128)(2,1)}, bf16[512,512]{1,0:T(8,128)(2,1)S(1)}, u32[]{:S(2)}, u32[]{:S(2)}) collective-permute-start(bf16[512,512]{1,0:T(8,128)(2,1)} %attend.1.refs_0_), channel_id=1, source_target_pairs={{8,0},{9,1},{10,2},{11,3},{12,4},{13,5},{14,6},{15,7},{0,8},{1,9},... | collective-permute-start | bytes 1572872 | tf_op jit(solution)/shard_map/ppermute | solution.py:48
  152.4 10.8 %collective-permute-start.25 = (bf16[512,512]{1,0:T(8,128)(2,1)S(1)}, bf16[512,512]{1,0:T(8,128)(2,1)S(1)}, u32[]{:S(2)}, u32[]{:S(2)}) collective-permute-start(bf16[512,512]{1,0:T(8,128)(2,1)S(1)} %collective-permute-done.24.refs_2_), channel_id=1, source_target_pairs={{8,0},{9,1},{10,2},{11,3},{12,4},{13,5},{14,6},{15,7},{0,8},{1,9},... | collective-permute-start | bytes 1572872 | tf_op jit(solution)/shard_map/ppermute | solution.py:48
  (29 other events, 254.7 us)
Sparse Core Ops, SparseCore 0:
  11.5 130.6 all-gather.1

commit v6 on v4

--- a/solution.py
+++ b/solution.py
@@ -191,6 +191,26 @@
         ],
         name="pair_first" if tail is None else "pair_last",
     )(*pieces, *normed, *extra)
+
+
+def assemble_kernel(*refs, spans):
+    out_any, sems = refs[-2:]
+    pairs = []
+    for piece, start, target, size in spans:
+        pairs.append((refs[piece].at[pl.ds(start, size)], out_any.at[pl.ds(target, size)]))
+    run_copies(pairs, sems)
+
+
+def assemble(pieces, spans, rows):
+    any_spec = pl.BlockSpec(memory_space=pl.ANY)
+    return pl.pallas_call(
+        lambda *refs: assemble_kernel(*refs, spans=spans),
+        in_specs=[any_spec] * len(pieces),
+        out_specs=any_spec,
+        out_shape=jax.ShapeDtypeStruct((rows, pieces[0].shape[1]), pieces[0].dtype),
+        scratch_shapes=[pltpu.SemaphoreType.DMA((len(spans),))],
+        name="assemble",
+    )(*pieces)
 
 
 def column_parts(source, depth):
@@ -537,15 +557,17 @@
     )
     far_up = from_z(last_up, 1)
     far_down = from_z(last_down, -1)
-    column = jnp.concatenate(
-        [piece[depth : depth + fold] for piece in up]
-        + [far_up[depth // 2 :]]
-        + [piece[depth : depth + fold] for piece in down[:0:-1]]
-        + [piece[depth + fold :] for piece in up]
-        + [far_down[depth // 2 :]]
-        + [piece[depth + fold :] for piece in down[:0:-1]],
-        axis=0,
-    )
+    pieces = up + [far_up, far_down] + down[:0:-1]
+    spans = []
+    for half in range(2):
+        for entry in range(ctx_count):
+            target = (half * ctx_count + entry) * fold
+            if entry == ctx_count // 2:
+                spans.append((entry + half, depth // 2, target, fold))
+            else:
+                piece = entry if entry < ctx_count // 2 else entry + 1
+                spans.append((piece, depth + half * fold, target, fold))
+    column = assemble(pieces, spans, 2 * ctx_count * fold)
     next_x = from_x(column, 1)
     last_x = from_x(column, -1)
     parcel = project_pair(

time: 197 us -> 231 us (1.17)
  Pallas kernels: 48.6 us -> 87.8 us
  blocking collectives: 29.8 us -> 20.1 us
  waiting for transfers between devices: 30.3 us -> 38.9 us
  local copies, waits for them, and re-layouts: 12.9 us -> 5.79 us
  starting transfers between devices: 48.5 us -> 51.6 us
    pallas_call x0 -> x1, Pallas kernels: none -> 33 us  [assemble(): pl.pallas_call(lambda *refs: assemble_kernel(*refs, spans=spans), in_spec...]
    all_to_all x1, blocking collectives: 29.8 us -> 20.1 us  [shards(): lax.all_to_all(jnp.broadcast_to(squares * doc_weight[0], (everyone, LANES...]
    ppermute x24, waiting for transfers between devices: 24.3 us -> 31.7 us  [fetch(): return lax.ppermute(values, mesh_axes, pairs)]
    pallas_call x1, Pallas kernels: 10.8 us -> 17.4 us  [attend(): pl.pallas_call(lambda *refs: attend_kernel(*refs, half_rows=half_rows, he...]
    unnamed x59 -> x42, local copies, waits for them, and re-layouts: 8.15 us -> 2.8 us
    ppermute x24, starting transfers between devices: 44.4 us -> 47.6 us  [fetch(): return lax.ppermute(values, mesh_axes, pairs)]
  transfers between devices with their start and end apart: 26 -> 26, of which waited for: 12 -> 13; matrix products, arithmetic and copies ran while one was open for 7% -> 3% of each run, Pallas kernels for 21% -> 35%
where the time goes in v6:
time: 231 us; the launch traced here: 230 us
  Pallas kernels  87.8 us (38%)
  starting transfers between devices  51.6 us (22%)
  waiting for transfers between devices  38.9 us (17%)
  blocking collectives  20.1 us (9%)
  between operations  17.4 us (8%)
  other arithmetic  8.56 us (4%)
  local copies, waits for them, and re-layouts  5.79 us (3%)
    ppermute x24, starting transfers between devices, fetch(): return lax.ppermute(values, mesh_axes, pairs)  47.6 us
    pallas_call x1, Pallas kernels, assemble(): pl.pallas_call(lambda *refs: assemble_kernel(*refs, spans=spans), in_spec...  33 us
    ppermute x24, waiting for transfers between devices, fetch(): return lax.ppermute(values, mesh_axes, pairs)  31.7 us
    all_to_all x1, blocking collectives, shards(): lax.all_to_all(jnp.broadcast_to(squares * doc_weight[0], (everyone, LANES...  20.1 us
    pallas_call x1, Pallas kernels, attend(): pl.pallas_call(lambda *refs: attend_kernel(*refs, half_rows=half_rows, he...  17.4 us
    pallas_call x2, Pallas kernels, project_queries(): pl.pallas_call(lambda *refs: kernel(*refs, groups=groups, columns=columns...  11.5 us
    pallas_call x2, Pallas kernels, norm(): pl.pallas_call(lambda *refs: norm_kernel(*refs, groups=groups), grid_spec...  9.91 us
    pallas_call x2, Pallas kernels, project_pair(): pl.pallas_call(lambda *refs: kernel(*refs, count=count, ranges=ranges), i...  8.07 us
  transfers between devices with their start and end apart: 26, of which 13 were waited for; matrix products, arithmetic and copies ran while one was open for 3% of the time, Pallas kernels for 35%

profile of v6, /device:TPU:1, one launch (start us, length us, event | category | flops | bytes accessed | tf_op | source)
XLA Modules:
  0.0 230.2 jit_solution(15760689180386073252)
XLA Ops:
  11.8 3.8 %collective-permute-start = (bf16[64,512]{1,0:T(8,128)(2,1)S(1)}, bf16[64,512]{1,0:T(8,128)(2,1)S(1)}, u32[]{:S(2)}, u32[]{:S(2)}) collective-permute-start(bf16[64,512]{1,0:T(8,128)(2,1)S(1)} %add_convert_fusion.1), channel_id=1, source_target_pairs={{1,0},{0,1},{3,2},{2,3},{5,4},{4,5},{7,6},{6,7},{9,8},{8,9},{11,10... | collective-permute-start | bytes 196616 | tf_op jit(solution)/shard_map/ppermute | solution.py:48
  15.7 4.0 %all-to-all-start = ((bf16[8,64,256]{2,1,0:T(8,128)(2,1)}), bf16[8,64,256]{2,1,0:T(8,128)(2,1)S(1)}, u32[]{:S(2)}, u32[]{:S(2)}) async-start(bf16[8,64,256]{2,1,0:T(8,128)(2,1)} %broadcast_in_dim.4), calls=%async_computation | async-start | bytes 524288 | tf_op jit(solution)/shard_map/all_to_all | solution.py:509
  19.7 7.2 %all-to-all-done = bf16[8,64,256]{2,1,0:T(8,128)(2,1)S(1)} async-done(((bf16[8,64,256]{2,1,0:T(8,128)(2,1)}), bf16[8,64,256]{2,1,0:T(8,128)(2,1)S(1)}, u32[]{:S(2)}, u32[]{:S(2)}) %all-to-all-start) | async-done | bytes 262176 | tf_op jit(solution)/shard_map/all_to_all | solution.py:509
  27.0 5.7 %collective-permute-start.1 = (bf16[768,256]{1,0:T(8,128)(2,1)S(1)}, bf16[768,256]{1,0:T(8,128)(2,1)S(1)}, u32[]{:S(2)}, u32[]{:S(2)}) collective-permute-start(bf16[768,256]{1,0:T(8,128)(2,1)S(1)} %pad_maximum_fusion.refs_2_.refs_0_), channel_id=1, source_target_pairs={{32,0},{33,1},{34,2},{35,3},{36,4},{37,5},{38,6},{39,7},{40,8},{41... | collective-permute-start | bytes 1179656 | tf_op jit(solution)/shard_map/ppermute | solution.py:48
  33.3 4.9 %norm.2.refs_5_.refs_4_.refs_3_ = bf16[256,4096]{1,0:T(8,128)(2,1)} custom-call(s32[2]{0:T(128)} %pad_add_fusion.1.refs_0_, bf16[512,4096]{1,0:T(8,128)(2,1)} %bitcast.20, f32[1,4096]{1,0:T(1,128)} %bitcast.24), custom_call_target="tpu_custom_call" | custom-call | tf_op jit(solution)/shard_map/norm/pallas_call | solution.py:89
  39.2 3.3 %collective-permute-done.2.refs_1_.refs_8_ = bf16[768,256]{1,0:T(8,128)(2,1)S(1)} collective-permute-done((bf16[768,256]{1,0:T(8,128)(2,1)S(1)}, bf16[768,256]{1,0:T(8,128)(2,1)S(1)}, u32[]{:S(2)}, u32[]{:S(2)}) %collective-permute-start.2) | collective-permute-done | bytes 393248 | tf_op jit(solution)/shard_map/ppermute | solution.py:48
  44.7 5.0 %norm.3.refs_6_.refs_5_.refs_4_ = bf16[256,4096]{1,0:T(8,128)(2,1)} custom-call(s32[2]{0:T(128)} %pad_add_fusion.1.refs_0_, bf16[512,4096]{1,0:T(8,128)(2,1)} %bitcast.21, f32[1,4096]{1,0:T(1,128)} %bitcast.25), custom_call_target="tpu_custom_call" | custom-call | tf_op jit(solution)/shard_map/norm/pallas_call | solution.py:89
  51.5 2.7 %collective-permute-start.5 = (bf16[768,256]{1,0:T(8,128)(2,1)S(1)}, bf16[768,256]{1,0:T(8,128)(2,1)S(1)}, u32[]{:S(2)}, u32[]{:S(2)}) collective-permute-start(bf16[768,256]{1,0:T(8,128)(2,1)S(1)} %collective-permute-done.3.refs_4_.refs_2_), channel_id=1, source_target_pairs={{32,0},{33,1},{34,2},{35,3},{36,4},{37,5},{38,6},{39,7},{40,8},{41... | collective-permute-start | bytes 1179656 | tf_op jit(solution)/shard_map/ppermute | solution.py:48
  56.9 3.8 %pair_first.1.refs_6_ = f32[512,256]{1,0:T(8,128)} custom-call(bf16[768,256]{1,0:T(8,128)(2,1)} %copy-done.8, bf16[768,256]{1,0:T(8,128)(2,1)} %copy-done.6, bf16[768,256]{1,0:T(8,128)(2,1)} %copy-done, bf16[768,256]{1,0:T(8,128)(2,1)} %copy-done.5, bf16[768,256]{1,0:T(8,128)(2,1)} %copy-done.7, bf16[256,4096]{1,0:T(8,128)(2,1)} %norm.2.refs_5_.refs_4_.refs_3_, ...), custom_call_target="tpu_custom_call" | custom-call | tf_op jit(solution)/shard_map/pair_first/pallas_call | solution.py:182
  62.4 4.5 %collective-permute-done.7.refs_4_.refs_1_ = bf16[384,256]{1,0:T(8,128)(2,1)S(1)} collective-permute-done((bf16[384,256]{1,0:T(8,128)(2,1)S(1)}, bf16[384,256]{1,0:T(8,128)(2,1)S(1)}, u32[]{:S(2)}, u32[]{:S(2)}) %collective-permute-start.7) | collective-permute-done | bytes 196640 | tf_op jit(solution)/shard_map/ppermute | solution.py:48
  68.7 33.0 %assemble.1.refs_1_ = bf16[2048,256]{1,0:T(8,128)(2,1)} custom-call(bf16[768,256]{1,0:T(8,128)(2,1)} %copy-done, bf16[768,256]{1,0:T(8,128)(2,1)} %copy-done.5, bf16[768,256]{1,0:T(8,128)(2,1)} %copy-done.7, bf16[768,256]{1,0:T(8,128)(2,1)} %copy-done.2, bf16[384,256]{1,0:T(8,128)(2,1)} %copy-done.9, bf16[384,256]{1,0:T(8,128)(2,1)} %copy-done.10, ...), custom_call_target="tpu_custom_call" | custom-call | tf_op jit(solution)/shard_map/assemble/pallas_call | solution.py:206
  103.2 4.3 %pair_last.1.refs_1_ = bf16[2,528,128]{2,1,0:T(8,128)(2,1)} custom-call(bf16[768,256]{1,0:T(8,128)(2,1)} %copy-done.2, bf16[384,256]{1,0:T(8,128)(2,1)} %copy-done.9, bf16[384,256]{1,0:T(8,128)(2,1)} %copy-done.10, bf16[768,256]{1,0:T(8,128)(2,1)} %copy-done.1, bf16[256,4096]{1,0:T(8,128)(2,1)} %norm.2.refs_5_.refs_4_.refs_3_, ...), custom_call_target="tpu_custom_call" | custom-call | tf_op jit(solution)/shard_map/pair_last/pallas_call | solution.py:182
  109.8 4.2 %collective-permute-done.9.refs_2_ = bf16[2,528,128]{2,1,0:T(8,128)(2,1)S(1)} collective-permute-done((bf16[2,528,128]{2,1,0:T(8,128)(2,1)}, bf16[2,528,128]{2,1,0:T(8,128)(2,1)S(1)}, u32[]{:S(2)}, u32[]{:S(2)}) %collective-permute-start.9) | collective-permute-done | bytes 270368 | tf_op jit(solution)/shard_map/ppermute | solution.py:48
  114.0 3.4 %collective-permute-start.10 = (bf16[2,528,128]{2,1,0:T(8,128)(2,1)S(1)}, bf16[2,528,128]{2,1,0:T(8,128)(2,1)}, u32[]{:S(2)}, u32[]{:S(2)}) collective-permute-start(bf16[2,528,128]{2,1,0:T(8,128)(2,1)S(1)} %collective-permute-done.9.refs_2_), channel_id=1, source_target_pairs={{32,0},{33,1},{34,2},{35,3},{36,4},{37,5},{38,6},{39,7},{40,8},{41... | collective-permute-start | bytes 811016 | tf_op jit(solution)/shard_map/ppermute | solution.py:48
  117.5 13.4 %collective-permute-done.13.refs_2_ = bf16[2048,256]{1,0:T(8,128)(2,1)S(1)} collective-permute-done((bf16[2048,256]{1,0:T(8,128)(2,1)}, bf16[2048,256]{1,0:T(8,128)(2,1)S(1)}, u32[]{:S(2)}, u32[]{:S(2)}) %collective-permute-start.13) | collective-permute-done | bytes 1048608 | tf_op jit(solution)/shard_map/ppermute | solution.py:48
  134.9 6.1 %collective-permute-start.15 = (bf16[2,528,128]{2,1,0:T(8,128)(2,1)}, bf16[2,528,128]{2,1,0:T(8,128)(2,1)S(1)}, u32[]{:S(2)}, u32[]{:S(2)}) collective-permute-start(bf16[2,528,128]{2,1,0:T(8,128)(2,1)} %collective-permute-done.10.refs_3_), channel_id=1, source_target_pairs={{32,0},{33,1},{34,2},{35,3},{36,4},{37,5},{38,6},{39,7},{40,8},{41... | collective-permute-start | bytes 811016 | tf_op jit(solution)/shard_map/ppermute | solution.py:48
  141.0 6.6 %query_first.1.refs_5_ = f32[512,512]{1,0:T(8,128)} custom-call(s32[2]{0:T(128)} %pad_add_fusion.1.refs_0_, bf16[2048,256]{1,0:T(8,128)(2,1)} %assemble.1.refs_1_, bf16[2048,256]{1,0:T(8,128)(2,1)} %copy-done.3, bf16[2048,256]{1,0:T(8,128)(2,1)} %copy-done.4, bf16[256,4096]{1,0:T(8,128)(2,1)} %norm.2.refs_5_.refs_4_.refs_3_, ...), custom_call_target="tpu_custom_call" | custom-call | tf_op jit(solution)/shard_map/query_first/pallas_call | solution.py:279
  147.8 2.7 %collective-permute-start.17 = (bf16[1,528,128]{2,1,0:T(8,128)(2,1)S(1)}, bf16[1,528,128]{2,1,0:T(8,128)(2,1)S(1)}, u32[]{:S(2)}, u32[]{:S(2)}) collective-permute-start(bf16[1,528,128]{2,1,0:T(8,128)(2,1)S(1)} %slice.50), channel_id=1, source_target_pairs={{32,0},{33,1},{34,2},{35,3},{36,4},{37,5},{38,6},{39,7},{40,8},{41... | collective-permute-start | bytes 405512 | tf_op jit(solution)/shard_map/ppermute | solution.py:48
  151.1 4.9 %query_last.1.refs_10_ = bf16[512,512]{1,0:T(8,128)(2,1)} custom-call(s32[2]{0:T(128)} %pad_add_fusion.1.refs_0_, bf16[1024,256]{1,0:T(8,128)(2,1)} %collective-permute-done.19.refs_1_, bf16[1024,256]{1,0:T(8,128)(2,1)} %collective-permute-done.20.refs_2_, bf16[256,4096]{1,0:T(8,128)(2,1)} %norm.2.refs_5_.refs_4_.refs_3_, ...), custom_call_target="tpu_custom_call" | custom-call | tf_op jit(solution)/shard_map/query_last/pallas_call | solution.py:279
  157.3 17.4 %attend.1.refs_0_ = bf16[512,512]{1,0:T(8,128)(2,1)} custom-call(s32[2]{0:T(128)} %pad_add_fusion.1.refs_0_, bf16[2,528,128]{2,1,0:T(8,128)(2,1)} %pair_last.1.refs_1_, bf16[2,528,128]{2,1,0:T(8,128)(2,1)} %copy-done.16, bf16[2,528,128]{2,1,0:T(8,128)(2,1)} %collective-permute-done.10.refs_3_, bf16[2,528,128]{2,1,0:T(8,128)(2,1)} %copy-done.11, ...), custom_call_target="tpu_custom_call" | custom-call | tf_op jit(solution)/shard_map/attend/pallas_call | solution.py:393
  176.4 5.5 %collective-permute-start.21 = (bf16[512,512]{1,0:T(8,128)(2,1)}, bf16[512,512]{1,0:T(8,128)(2,1)S(1)}, u32[]{:S(2)}, u32[]{:S(2)}) collective-permute-start(bf16[512,512]{1,0:T(8,128)(2,1)} %attend.1.refs_0_), channel_id=1, source_target_pairs={{8,0},{9,1},{10,2},{11,3},{12,4},{13,5},{14,6},{15,7},{0,8},{1,9},... | collective-permute-start | bytes 1572872 | tf_op jit(solution)/shard_map/ppermute | solution.py:48
  183.1 6.7 %collective-permute-start.23 = (bf16[512,512]{1,0:T(8,128)(2,1)S(1)}, bf16[512,512]{1,0:T(8,128)(2,1)S(1)}, u32[]{:S(2)}, u32[]{:S(2)}) collective-permute-start(bf16[512,512]{1,0:T(8,128)(2,1)S(1)} %collective-permute-done.22.refs_2_), channel_id=1, source_target_pairs={{8,0},{9,1},{10,2},{11,3},{12,4},{13,5},{14,6},{15,7},{0,8},{1,9},... | collective-permute-start | bytes 1572872 | tf_op jit(solution)/shard_map/ppermute | solution.py:48
  192.2 7.9 %blend.1 = (bf16[512,1024]{1,0:T(8,128)(2,1)}, f32[1,128]{1,0:T(1,128)}) custom-call(s32[4]{0:T(128)} %pad_add_fusion.owner_ref, bf16[512,512]{1,0:T(8,128)(2,1)} %attend.1.refs_0_, bf16[512,512]{1,0:T(8,128)(2,1)} %copy-done.14, bf16[512,512]{1,0:T(8,128)(2,1)} %copy-done.13, bf16[512,512]{1,0:T(8,128)(2,1)} %copy-done.15, ...), custom_call_target="tpu_custom_call" | custom-call | tf_op jit(solution)/shard_map/blend/pallas_call | solution.py:453
  200.8 20.1 %all_to_all.11 = f32[256,1,128]{2,1,0:T(1,128)S(1)} all-to-all(f32[256,1,128]{2,1,0:T(1,128)S(1)} %broadcast_in_dim.5), channel_id=1, replica_groups=mesh['ctx'=8,'tp'=4,'dp'=8] {'ctx','tp','dp'}, dimensions={0} | all-to-all | bytes 262144 | tf_op jit(solution)/shard_map/all_to_all | solution.py:616
  (113 shorter events, 31.5 us)
Async XLA Ops:
  7.2 184.2 %all-gather.2.cloned.1.call-start = ((), (), s32[]{:S(2)}) async-start(), calls=%async_computation.2 | async-start | bytes 4259840 | tf_op jit(solution)/shard_map/all_gather | solution.py:511
  11.8 7.9 %collective-permute-start = (bf16[64,512]{1,0:T(8,128)(2,1)S(1)}, bf16[64,512]{1,0:T(8,128)(2,1)S(1)}, u32[]{:S(2)}, u32[]{:S(2)}) collective-permute-start(bf16[64,512]{1,0:T(8,128)(2,1)S(1)} %add_convert_fusion.1), channel_id=1, source_target_pairs={{1,0},{0,1},{3,2},{2,3},{5,4},{4,5},{7,6},{6,7},{9,8},{8,9},{11,10... | collective-permute-start | bytes 196616 | tf_op jit(solution)/shard_map/ppermute | solution.py:48
  15.7 11.3 %all-to-all-start = ((bf16[8,64,256]{2,1,0:T(8,128)(2,1)}), bf16[8,64,256]{2,1,0:T(8,128)(2,1)S(1)}, u32[]{:S(2)}, u32[]{:S(2)}) async-start(bf16[8,64,256]{2,1,0:T(8,128)(2,1)} %broadcast_in_dim.4), calls=%async_computation | async-start | bytes 524288 | tf_op jit(solution)/shard_map/all_to_all | solution.py:509
  27.0 12.2 %collective-permute-start.1 = (bf16[768,256]{1,0:T(8,128)(2,1)S(1)}, bf16[768,256]{1,0:T(8,128)(2,1)S(1)}, u32[]{:S(2)}, u32[]{:S(2)}) collective-permute-start(bf16[768,256]{1,0:T(8,128)(2,1)S(1)} %pad_maximum_fusion.refs_2_.refs_0_), channel_id=1, source_target_pairs={{32,0},{33,1},{34,2},{35,3},{36,4},{37,5},{38,6},{39,7},{40,8},{41... | collective-permute-start | bytes 1179656 | tf_op jit(solution)/shard_map/ppermute | solution.py:48
  32.7 9.9 %collective-permute-start.2 = (bf16[768,256]{1,0:T(8,128)(2,1)S(1)}, bf16[768,256]{1,0:T(8,128)(2,1)S(1)}, u32[]{:S(2)}, u32[]{:S(2)}) collective-permute-start(bf16[768,256]{1,0:T(8,128)(2,1)S(1)} %pad_maximum_fusion.refs_2_.refs_0_), channel_id=1, source_target_pairs={{224,0},{225,1},{226,2},{227,3},{228,4},{229,5},{230,6},{231,7},{2... | collective-permute-start | bytes 1179656 | tf_op jit(solution)/shard_map/ppermute | solution.py:48
  42.5 7.9 %collective-permute-start.3 = (bf16[768,256]{1,0:T(8,128)(2,1)S(1)}, bf16[768,256]{1,0:T(8,128)(2,1)S(1)}, u32[]{:S(2)}, u32[]{:S(2)}) collective-permute-start(bf16[768,256]{1,0:T(8,128)(2,1)S(1)} %collective-permute-done.1.refs_3_.refs_1_), channel_id=1, source_target_pairs={{32,0},{33,1},{34,2},{35,3},{36,4},{37,5},{38,6},{39,7},{40,8},{41... | collective-permute-start | bytes 1179656 | tf_op jit(solution)/shard_map/ppermute | solution.py:48
  42.7 8.8 %collective-permute-start.4 = (bf16[768,256]{1,0:T(8,128)(2,1)S(1)}, bf16[768,256]{1,0:T(8,128)(2,1)S(1)}, u32[]{:S(2)}, u32[]{:S(2)}) collective-permute-start(bf16[768,256]{1,0:T(8,128)(2,1)S(1)} %collective-permute-done.2.refs_1_.refs_8_), channel_id=1, source_target_pairs={{224,0},{225,1},{226,2},{227,3},{228,4},{229,5},{230,6},{231,7},{2... | collective-permute-start | bytes 1179656 | tf_op jit(solution)/shard_map/ppermute | solution.py:48
  51.5 9.2 %collective-permute-start.6 = (bf16[768,256]{1,0:T(8,128)(2,1)S(1)}, bf16[768,256]{1,0:T(8,128)(2,1)S(1)}, u32[]{:S(2)}, u32[]{:S(2)}) collective-permute-start(bf16[768,256]{1,0:T(8,128)(2,1)S(1)} %collective-permute-done.4.refs_0_.refs_7_), channel_id=1, source_target_pairs={{224,0},{225,1},{226,2},{227,3},{228,4},{229,5},{230,6},{231,7},{2... | collective-permute-start | bytes 1179656 | tf_op jit(solution)/shard_map/ppermute | solution.py:48
  51.5 9.2 %collective-permute-start.5 = (bf16[768,256]{1,0:T(8,128)(2,1)S(1)}, bf16[768,256]{1,0:T(8,128)(2,1)S(1)}, u32[]{:S(2)}, u32[]{:S(2)}) collective-permute-start(bf16[768,256]{1,0:T(8,128)(2,1)S(1)} %collective-permute-done.3.refs_4_.refs_2_), channel_id=1, source_target_pairs={{32,0},{33,1},{34,2},{35,3},{36,4},{37,5},{38,6},{39,7},{40,8},{41... | collective-permute-start | bytes 1179656 | tf_op jit(solution)/shard_map/ppermute | solution.py:48
  60.9 6.1 %collective-permute-start.7 = (bf16[384,256]{1,0:T(8,128)(2,1)S(1)}, bf16[384,256]{1,0:T(8,128)(2,1)S(1)}, u32[]{:S(2)}, u32[]{:S(2)}) collective-permute-start(bf16[384,256]{1,0:T(8,128)(2,1)S(1)} %pad_maximum_fusion.3), channel_id=1, source_target_pairs={{32,0},{33,1},{34,2},{35,3},{36,4},{37,5},{38,6},{39,7},{40,8},{41... | collective-permute-start | bytes 589832 | tf_op jit(solution)/shard_map/ppermute | solution.py:48
  101.7 29.1 %collective-permute-start.13 = (bf16[2048,256]{1,0:T(8,128)(2,1)}, bf16[2048,256]{1,0:T(8,128)(2,1)S(1)}, u32[]{:S(2)}, u32[]{:S(2)}) collective-permute-start(bf16[2048,256]{1,0:T(8,128)(2,1)} %assemble.1.refs_1_), channel_id=1, source_target_pairs={{2,0},{3,1},{4,2},{5,3},{6,4},{7,5},{0,6},{1,7},{10,8},{11,9},{12,... | collective-permute-start | bytes 3145736 | tf_op jit(solution)/shard_map/ppermute | solution.py:48
  102.1 29.4 %collective-permute-start.14 = (bf16[2048,256]{1,0:T(8,128)(2,1)}, bf16[2048,256]{1,0:T(8,128)(2,1)S(1)}, u32[]{:S(2)}, u32[]{:S(2)}) collective-permute-start(bf16[2048,256]{1,0:T(8,128)(2,1)} %assemble.1.refs_1_), channel_id=1, source_target_pairs={{6,0},{7,1},{0,2},{1,3},{2,4},{3,5},{4,6},{5,7},{14,8},{15,9},{8,1... | collective-permute-start | bytes 3145736 | tf_op jit(solution)/shard_map/ppermute | solution.py:48
  107.5 6.5 %collective-permute-start.9 = (bf16[2,528,128]{2,1,0:T(8,128)(2,1)}, bf16[2,528,128]{2,1,0:T(8,128)(2,1)S(1)}, u32[]{:S(2)}, u32[]{:S(2)}) collective-permute-start(bf16[2,528,128]{2,1,0:T(8,128)(2,1)} %pair_last.1.refs_1_), channel_id=1, source_target_pairs={{32,0},{33,1},{34,2},{35,3},{36,4},{37,5},{38,6},{39,7},{40,8},{41... | collective-permute-start | bytes 811016 | tf_op jit(solution)/shard_map/ppermute | solution.py:48
  109.8 7.7 %collective-permute-start.11 = (bf16[2,528,128]{2,1,0:T(8,128)(2,1)}, bf16[2,528,128]{2,1,0:T(8,128)(2,1)S(1)}, u32[]{:S(2)}, u32[]{:S(2)}) collective-permute-start(bf16[2,528,128]{2,1,0:T(8,128)(2,1)} %pair_last.1.refs_1_), channel_id=1, source_target_pairs={{224,0},{225,1},{226,2},{227,3},{228,4},{229,5},{230,6},{231,7},{2... | collective-permute-start | bytes 811016 | tf_op jit(solution)/shard_map/ppermute | solution.py:48
  114.0 20.8 %collective-permute-start.10 = (bf16[2,528,128]{2,1,0:T(8,128)(2,1)S(1)}, bf16[2,528,128]{2,1,0:T(8,128)(2,1)}, u32[]{:S(2)}, u32[]{:S(2)}) collective-permute-start(bf16[2,528,128]{2,1,0:T(8,128)(2,1)S(1)} %collective-permute-done.9.refs_2_), channel_id=1, source_target_pairs={{32,0},{33,1},{34,2},{35,3},{36,4},{37,5},{38,6},{39,7},{40,8},{41... | collective-permute-start | bytes 811016 | tf_op jit(solution)/shard_map/ppermute | solution.py:48
  117.5 17.4 %collective-permute-start.12 = (bf16[2,528,128]{2,1,0:T(8,128)(2,1)S(1)}, bf16[2,528,128]{2,1,0:T(8,128)(2,1)}, u32[]{:S(2)}, u32[]{:S(2)}) collective-permute-start(bf16[2,528,128]{2,1,0:T(8,128)(2,1)S(1)} %collective-permute-done.11.refs_9_), channel_id=1, source_target_pairs={{224,0},{225,1},{226,2},{227,3},{228,4},{229,5},{230,6},{231,7},{2... | collective-permute-start | bytes 811016 | tf_op jit(solution)/shard_map/ppermute | solution.py:48
  132.4 18.6 %collective-permute-start.19 = (bf16[1024,256]{1,0:T(8,128)(2,1)S(1)}, bf16[1024,256]{1,0:T(8,128)(2,1)}, u32[]{:S(2)}, u32[]{:S(2)}) collective-permute-start(bf16[1024,256]{1,0:T(8,128)(2,1)S(1)} %slice.52), channel_id=1, source_target_pairs={{2,0},{3,1},{4,2},{5,3},{6,4},{7,5},{0,6},{1,7},{10,8},{11,9},{12,... | collective-permute-start | bytes 1572872 | tf_op jit(solution)/shard_map/ppermute | solution.py:48
  134.8 16.2 %collective-permute-start.20 = (bf16[1024,256]{1,0:T(8,128)(2,1)}, bf16[1024,256]{1,0:T(8,128)(2,1)}, u32[]{:S(2)}, u32[]{:S(2)}) collective-permute-start(bf16[1024,256]{1,0:T(8,128)(2,1)} %slice.53), channel_id=1, source_target_pairs={{6,0},{7,1},{0,2},{1,3},{2,4},{3,5},{4,6},{5,7},{14,8},{15,9},{8,1... | collective-permute-start | bytes 1572872 | tf_op jit(solution)/shard_map/ppermute | solution.py:48
  134.9 12.8 %collective-permute-start.15 = (bf16[2,528,128]{2,1,0:T(8,128)(2,1)}, bf16[2,528,128]{2,1,0:T(8,128)(2,1)S(1)}, u32[]{:S(2)}, u32[]{:S(2)}) collective-permute-start(bf16[2,528,128]{2,1,0:T(8,128)(2,1)} %collective-permute-done.10.refs_3_), channel_id=1, source_target_pairs={{32,0},{33,1},{34,2},{35,3},{36,4},{37,5},{38,6},{39,7},{40,8},{41... | collective-permute-start | bytes 811016 | tf_op jit(solution)/shard_map/ppermute | solution.py:48
  141.0 6.7 %collective-permute-start.16 = (bf16[2,528,128]{2,1,0:T(8,128)(2,1)}, bf16[2,528,128]{2,1,0:T(8,128)(2,1)S(1)}, u32[]{:S(2)}, u32[]{:S(2)}) collective-permute-start(bf16[2,528,128]{2,1,0:T(8,128)(2,1)} %collective-permute-done.12.refs_8_), channel_id=1, source_target_pairs={{224,0},{225,1},{226,2},{227,3},{228,4},{229,5},{230,6},{231,7},{2... | collective-permute-start | bytes 811016 | tf_op jit(solution)/shard_map/ppermute | solution.py:48
  147.8 8.2 %collective-permute-start.17 = (bf16[1,528,128]{2,1,0:T(8,128)(2,1)S(1)}, bf16[1,528,128]{2,1,0:T(8,128)(2,1)S(1)}, u32[]{:S(2)}, u32[]{:S(2)}) collective-permute-start(bf16[1,528,128]{2,1,0:T(8,128)(2,1)S(1)} %slice.50), channel_id=1, source_target_pairs={{32,0},{33,1},{34,2},{35,3},{36,4},{37,5},{38,6},{39,7},{40,8},{41... | collective-permute-start | bytes 405512 | tf_op jit(solution)/shard_map/ppermute | solution.py:48
  174.7 8.4 %collective-permute-start.22 = (bf16[512,512]{1,0:T(8,128)(2,1)}, bf16[512,512]{1,0:T(8,128)(2,1)S(1)}, u32[]{:S(2)}, u32[]{:S(2)}) collective-permute-start(bf16[512,512]{1,0:T(8,128)(2,1)} %attend.1.refs_0_), channel_id=1, source_target_pairs={{16,0},{17,1},{18,2},{19,3},{20,4},{21,5},{22,6},{23,7},{24,8},{25... | collective-permute-start | bytes 1572872 | tf_op jit(solution)/shard_map/ppermute | solution.py:48
  176.4 14.8 %collective-permute-start.21 = (bf16[512,512]{1,0:T(8,128)(2,1)}, bf16[512,512]{1,0:T(8,128)(2,1)S(1)}, u32[]{:S(2)}, u32[]{:S(2)}) collective-permute-start(bf16[512,512]{1,0:T(8,128)(2,1)} %attend.1.refs_0_), channel_id=1, source_target_pairs={{8,0},{9,1},{10,2},{11,3},{12,4},{13,5},{14,6},{15,7},{0,8},{1,9},... | collective-permute-start | bytes 1572872 | tf_op jit(solution)/shard_map/ppermute | solution.py:48
  183.1 8.3 %collective-permute-start.23 = (bf16[512,512]{1,0:T(8,128)(2,1)S(1)}, bf16[512,512]{1,0:T(8,128)(2,1)S(1)}, u32[]{:S(2)}, u32[]{:S(2)}) collective-permute-start(bf16[512,512]{1,0:T(8,128)(2,1)S(1)} %collective-permute-done.22.refs_2_), channel_id=1, source_target_pairs={{8,0},{9,1},{10,2},{11,3},{12,4},{13,5},{14,6},{15,7},{0,8},{1,9},... | collective-permute-start | bytes 1572872 | tf_op jit(solution)/shard_map/ppermute | solution.py:48
  (23 other events, 234.5 us)
Sparse Core Ops, SparseCore 0:
  11.9 130.8 all-gather.1

commit v7 on v6

--- a/solution.py
+++ b/solution.py
@@ -206,7 +206,7 @@
     return pl.pallas_call(
         lambda *refs: assemble_kernel(*refs, spans=spans),
         in_specs=[any_spec] * len(pieces),
-        out_specs=any_spec,
+        out_specs=pl.BlockSpec(memory_space=pltpu.VMEM),
         out_shape=jax.ShapeDtypeStruct((rows, pieces[0].shape[1]), pieces[0].dtype),
         scratch_shapes=[pltpu.SemaphoreType.DMA((len(spans),))],
         name="assemble",

time: 231 us -> 194 us (0.84)
  Pallas kernels: 87.8 us -> 55.9 us
  waiting for transfers between devices: 38.9 us -> 32.2 us
  blocking collectives: 20.1 us -> 23.7 us
    pallas_call x1, Pallas kernels: 33 us -> 2.34 us  [assemble(): pl.pallas_call(lambda *refs: assemble_kernel(*refs, spans=spans), in_spec...]
    ppermute x24, waiting for transfers between devices: 31.7 us -> 24.9 us  [fetch(): return lax.ppermute(values, mesh_axes, pairs)]
    all_to_all x1, blocking collectives: 20.1 us -> 23.7 us  [shards(): lax.all_to_all(jnp.broadcast_to(squares * doc_weight[0], (everyone, LANES...]
  transfers between devices with their start and end apart: 26 -> 26, of which waited for: 13 -> 15; matrix products, arithmetic and copies ran while one was open for 3% -> 3% of each run, Pallas kernels for 35% -> 25%
where the time goes in v7:
time: 194 us
  Pallas kernels  55.9 us (29%)
  starting transfers between devices  50.7 us (26%)
  waiting for transfers between devices  32.2 us (17%)
  blocking collectives  23.7 us (12%)
  between operations  17.4 us (9%)
  other arithmetic  8.56 us (4%)
  local copies, waits for them, and re-layouts  5.62 us (3%)
    ppermute x24, starting transfers between devices, fetch(): return lax.ppermute(values, mesh_axes, pairs)  46.6 us
    ppermute x24, waiting for transfers between devices, fetch(): return lax.ppermute(values, mesh_axes, pairs)  24.9 us
    all_to_all x1, blocking collectives, shards(): lax.all_to_all(jnp.broadcast_to(squares * doc_weight[0], (everyone, LANES...  23.7 us
    pallas_call x1, Pallas kernels, attend(): pl.pallas_call(lambda *refs: attend_kernel(*refs, half_rows=half_rows, he...  15.9 us
    pallas_call x2, Pallas kernels, project_queries(): pl.pallas_call(lambda *refs: kernel(*refs, groups=groups, columns=columns...  11.9 us
    pallas_call x2, Pallas kernels, norm(): pl.pallas_call(lambda *refs: norm_kernel(*refs, groups=groups), grid_spec...  9.91 us
    pallas_call x2, Pallas kernels, project_pair(): pl.pallas_call(lambda *refs: kernel(*refs, count=count, ranges=ranges), i...  8 us
    pallas_call x1, Pallas kernels, blend(): pl.pallas_call(blend_kernel, in_specs=[pl.BlockSpec(memory_space=pltpu.SM...  7.9 us
  transfers between devices with their start and end apart: 26, of which 15 were waited for; matrix products, arithmetic and copies ran while one was open for 3% of the time, Pallas kernels for 25%

profile of v7, /device:TPU:1, one launch (start us, length us, event | category | flops | bytes accessed | tf_op | source)
XLA Modules:
  0.0 194.0 jit_solution(3259414438311489143)
XLA Ops:
  11.8 3.8 %collective-permute-start = (bf16[64,512]{1,0:T(8,128)(2,1)S(1)}, bf16[64,512]{1,0:T(8,128)(2,1)S(1)}, u32[]{:S(2)}, u32[]{:S(2)}) collective-permute-start(bf16[64,512]{1,0:T(8,128)(2,1)S(1)} %add_convert_fusion.1), channel_id=1, source_target_pairs={{1,0},{0,1},{3,2},{2,3},{5,4},{4,5},{7,6},{6,7},{9,8},{8,9},{11,10... | collective-permute-start | bytes 196616 | tf_op jit(solution)/shard_map/ppermute | solution.py:48
  15.7 4.0 %all-to-all-start = ((bf16[8,64,256]{2,1,0:T(8,128)(2,1)}), bf16[8,64,256]{2,1,0:T(8,128)(2,1)S(1)}, u32[]{:S(2)}, u32[]{:S(2)}) async-start(bf16[8,64,256]{2,1,0:T(8,128)(2,1)} %broadcast_in_dim.4), calls=%async_computation | async-start | bytes 524288 | tf_op jit(solution)/shard_map/all_to_all | solution.py:509
  19.7 7.2 %all-to-all-done = bf16[8,64,256]{2,1,0:T(8,128)(2,1)S(1)} async-done(((bf16[8,64,256]{2,1,0:T(8,128)(2,1)}), bf16[8,64,256]{2,1,0:T(8,128)(2,1)S(1)}, u32[]{:S(2)}, u32[]{:S(2)}) %all-to-all-start) | async-done | bytes 262176 | tf_op jit(solution)/shard_map/all_to_all | solution.py:509
  27.0 5.7 %collective-permute-start.1 = (bf16[768,256]{1,0:T(8,128)(2,1)S(1)}, bf16[768,256]{1,0:T(8,128)(2,1)S(1)}, u32[]{:S(2)}, u32[]{:S(2)}) collective-permute-start(bf16[768,256]{1,0:T(8,128)(2,1)S(1)} %pad_maximum_fusion.refs_2_.refs_0_), channel_id=1, source_target_pairs={{32,0},{33,1},{34,2},{35,3},{36,4},{37,5},{38,6},{39,7},{40,8},{41... | collective-permute-start | bytes 1179656 | tf_op jit(solution)/shard_map/ppermute | solution.py:48
  33.3 4.9 %norm.2.refs_5_.refs_4_.refs_3_ = bf16[256,4096]{1,0:T(8,128)(2,1)} custom-call(s32[2]{0:T(128)} %pad_add_fusion.1.refs_0_, bf16[512,4096]{1,0:T(8,128)(2,1)} %bitcast.20, f32[1,4096]{1,0:T(1,128)} %bitcast.24), custom_call_target="tpu_custom_call" | custom-call | tf_op jit(solution)/shard_map/norm/pallas_call | solution.py:89
  39.2 3.3 %collective-permute-done.2.refs_1_.refs_8_ = bf16[768,256]{1,0:T(8,128)(2,1)S(1)} collective-permute-done((bf16[768,256]{1,0:T(8,128)(2,1)S(1)}, bf16[768,256]{1,0:T(8,128)(2,1)S(1)}, u32[]{:S(2)}, u32[]{:S(2)}) %collective-permute-start.2) | collective-permute-done | bytes 393248 | tf_op jit(solution)/shard_map/ppermute | solution.py:48
  44.7 5.0 %norm.3.refs_6_.refs_5_.refs_4_ = bf16[256,4096]{1,0:T(8,128)(2,1)} custom-call(s32[2]{0:T(128)} %pad_add_fusion.1.refs_0_, bf16[512,4096]{1,0:T(8,128)(2,1)} %bitcast.21, f32[1,4096]{1,0:T(1,128)} %bitcast.25), custom_call_target="tpu_custom_call" | custom-call | tf_op jit(solution)/shard_map/norm/pallas_call | solution.py:89
  51.5 2.7 %collective-permute-start.5 = (bf16[768,256]{1,0:T(8,128)(2,1)S(1)}, bf16[768,256]{1,0:T(8,128)(2,1)S(1)}, u32[]{:S(2)}, u32[]{:S(2)}) collective-permute-start(bf16[768,256]{1,0:T(8,128)(2,1)S(1)} %collective-permute-done.3.refs_4_.refs_2_), channel_id=1, source_target_pairs={{32,0},{33,1},{34,2},{35,3},{36,4},{37,5},{38,6},{39,7},{40,8},{41... | collective-permute-start | bytes 1179656 | tf_op jit(solution)/shard_map/ppermute | solution.py:48
  56.9 3.8 %pair_first.1.refs_6_ = f32[512,256]{1,0:T(8,128)} custom-call(bf16[768,256]{1,0:T(8,128)(2,1)} %copy-done.8, bf16[768,256]{1,0:T(8,128)(2,1)} %copy-done.6, bf16[768,256]{1,0:T(8,128)(2,1)} %copy-done, bf16[768,256]{1,0:T(8,128)(2,1)} %copy-done.5, bf16[768,256]{1,0:T(8,128)(2,1)} %copy-done.7, bf16[256,4096]{1,0:T(8,128)(2,1)} %norm.2.refs_5_.refs_4_.refs_3_, ...), custom_call_target="tpu_custom_call" | custom-call | tf_op jit(solution)/shard_map/pair_first/pallas_call | solution.py:182
  62.4 4.5 %collective-permute-done.7.refs_4_.refs_1_ = bf16[384,256]{1,0:T(8,128)(2,1)S(1)} collective-permute-done((bf16[384,256]{1,0:T(8,128)(2,1)S(1)}, bf16[384,256]{1,0:T(8,128)(2,1)S(1)}, u32[]{:S(2)}, u32[]{:S(2)}) %collective-permute-start.7) | collective-permute-done | bytes 196640 | tf_op jit(solution)/shard_map/ppermute | solution.py:48
  68.7 2.3 %assemble.1.refs_1_ = bf16[2048,256]{1,0:T(8,128)(2,1)} custom-call(bf16[768,256]{1,0:T(8,128)(2,1)} %copy-done, bf16[768,256]{1,0:T(8,128)(2,1)} %copy-done.5, bf16[768,256]{1,0:T(8,128)(2,1)} %copy-done.7, bf16[768,256]{1,0:T(8,128)(2,1)} %copy-done.2, bf16[384,256]{1,0:T(8,128)(2,1)} %copy-done.9, bf16[384,256]{1,0:T(8,128)(2,1)} %copy-done.10, ...), custom_call_target="tpu_custom_call" | custom-call | tf_op jit(solution)/shard_map/assemble/pallas_call | solution.py:206
  72.6 4.2 %pair_last.1.refs_1_ = bf16[2,528,128]{2,1,0:T(8,128)(2,1)} custom-call(bf16[768,256]{1,0:T(8,128)(2,1)} %copy-done.2, bf16[384,256]{1,0:T(8,128)(2,1)} %copy-done.9, bf16[384,256]{1,0:T(8,128)(2,1)} %copy-done.10, bf16[768,256]{1,0:T(8,128)(2,1)} %copy-done.1, bf16[256,4096]{1,0:T(8,128)(2,1)} %norm.2.refs_5_.refs_4_.refs_3_, ...), custom_call_target="tpu_custom_call" | custom-call | tf_op jit(solution)/shard_map/pair_last/pallas_call | solution.py:182
  76.8 2.3 %collective-permute-start.9 = (bf16[2,528,128]{2,1,0:T(8,128)(2,1)}, bf16[2,528,128]{2,1,0:T(8,128)(2,1)S(1)}, u32[]{:S(2)}, u32[]{:S(2)}) collective-permute-start(bf16[2,528,128]{2,1,0:T(8,128)(2,1)} %pair_last.1.refs_1_), channel_id=1, source_target_pairs={{32,0},{33,1},{34,2},{35,3},{36,4},{37,5},{38,6},{39,7},{40,8},{41... | collective-permute-start | bytes 811016 | tf_op jit(solution)/shard_map/ppermute | solution.py:48
  79.1 4.3 %collective-permute-done.9.refs_2_ = bf16[2,528,128]{2,1,0:T(8,128)(2,1)S(1)} collective-permute-done((bf16[2,528,128]{2,1,0:T(8,128)(2,1)}, bf16[2,528,128]{2,1,0:T(8,128)(2,1)S(1)}, u32[]{:S(2)}, u32[]{:S(2)}) %collective-permute-start.9) | collective-permute-done | bytes 270368 | tf_op jit(solution)/shard_map/ppermute | solution.py:48
  83.5 3.2 %collective-permute-start.10 = (bf16[2,528,128]{2,1,0:T(8,128)(2,1)S(1)}, bf16[2,528,128]{2,1,0:T(8,128)(2,1)}, u32[]{:S(2)}, u32[]{:S(2)}) collective-permute-start(bf16[2,528,128]{2,1,0:T(8,128)(2,1)S(1)} %collective-permute-done.9.refs_2_), channel_id=1, source_target_pairs={{32,0},{33,1},{34,2},{35,3},{36,4},{37,5},{38,6},{39,7},{40,8},{41... | collective-permute-start | bytes 811016 | tf_op jit(solution)/shard_map/ppermute | solution.py:48
  86.8 6.3 %collective-permute-done.13.refs_2_ = bf16[2048,256]{1,0:T(8,128)(2,1)S(1)} collective-permute-done((bf16[2048,256]{1,0:T(8,128)(2,1)}, bf16[2048,256]{1,0:T(8,128)(2,1)S(1)}, u32[]{:S(2)}, u32[]{:S(2)}) %collective-permute-start.13) | collective-permute-done | bytes 1048608 | tf_op jit(solution)/shard_map/ppermute | solution.py:48
  95.9 5.1 %collective-permute-start.15 = (bf16[2,528,128]{2,1,0:T(8,128)(2,1)}, bf16[2,528,128]{2,1,0:T(8,128)(2,1)S(1)}, u32[]{:S(2)}, u32[]{:S(2)}) collective-permute-start(bf16[2,528,128]{2,1,0:T(8,128)(2,1)} %collective-permute-done.10.refs_3_), channel_id=1, source_target_pairs={{32,0},{33,1},{34,2},{35,3},{36,4},{37,5},{38,6},{39,7},{40,8},{41... | collective-permute-start | bytes 811016 | tf_op jit(solution)/shard_map/ppermute | solution.py:48
  101.0 7.0 %query_first.1.refs_5_ = f32[512,512]{1,0:T(8,128)} custom-call(s32[2]{0:T(128)} %pad_add_fusion.1.refs_0_, bf16[2048,256]{1,0:T(8,128)(2,1)} %assemble.1.refs_1_, bf16[2048,256]{1,0:T(8,128)(2,1)} %copy-done.3, bf16[2048,256]{1,0:T(8,128)(2,1)} %copy-done.4, bf16[256,4096]{1,0:T(8,128)(2,1)} %norm.2.refs_5_.refs_4_.refs_3_, ...), custom_call_target="tpu_custom_call" | custom-call | tf_op jit(solution)/shard_map/query_first/pallas_call | solution.py:279
  111.7 4.9 %query_last.1.refs_10_ = bf16[512,512]{1,0:T(8,128)(2,1)} custom-call(s32[2]{0:T(128)} %pad_add_fusion.1.refs_0_, bf16[1024,256]{1,0:T(8,128)(2,1)} %collective-permute-done.19.refs_1_, bf16[1024,256]{1,0:T(8,128)(2,1)} %collective-permute-done.20.refs_2_, bf16[256,4096]{1,0:T(8,128)(2,1)} %norm.2.refs_5_.refs_4_.refs_3_, ...), custom_call_target="tpu_custom_call" | custom-call | tf_op jit(solution)/shard_map/query_last/pallas_call | solution.py:279
  118.0 15.9 %attend.1.refs_0_ = bf16[512,512]{1,0:T(8,128)(2,1)} custom-call(s32[2]{0:T(128)} %pad_add_fusion.1.refs_0_, bf16[2,528,128]{2,1,0:T(8,128)(2,1)} %pair_last.1.refs_1_, bf16[2,528,128]{2,1,0:T(8,128)(2,1)} %copy-done.16, bf16[2,528,128]{2,1,0:T(8,128)(2,1)} %collective-permute-done.10.refs_3_, bf16[2,528,128]{2,1,0:T(8,128)(2,1)} %copy-done.11, ...), custom_call_target="tpu_custom_call" | custom-call | tf_op jit(solution)/shard_map/attend/pallas_call | solution.py:393
  134.3 8.1 %collective-permute-start.21 = (bf16[512,512]{1,0:T(8,128)(2,1)}, bf16[512,512]{1,0:T(8,128)(2,1)S(1)}, u32[]{:S(2)}, u32[]{:S(2)}) collective-permute-start(bf16[512,512]{1,0:T(8,128)(2,1)} %attend.1.refs_0_), channel_id=1, source_target_pairs={{8,0},{9,1},{10,2},{11,3},{12,4},{13,5},{14,6},{15,7},{0,8},{1,9},... | collective-permute-start | bytes 1572872 | tf_op jit(solution)/shard_map/ppermute | solution.py:48
  142.6 7.5 %collective-permute-start.23 = (bf16[512,512]{1,0:T(8,128)(2,1)S(1)}, bf16[512,512]{1,0:T(8,128)(2,1)S(1)}, u32[]{:S(2)}, u32[]{:S(2)}) collective-permute-start(bf16[512,512]{1,0:T(8,128)(2,1)S(1)} %collective-permute-done.22.refs_2_), channel_id=1, source_target_pairs={{8,0},{9,1},{10,2},{11,3},{12,4},{13,5},{14,6},{15,7},{0,8},{1,9},... | collective-permute-start | bytes 1572872 | tf_op jit(solution)/shard_map/ppermute | solution.py:48
  152.4 7.9 %blend.1 = (bf16[512,1024]{1,0:T(8,128)(2,1)}, f32[1,128]{1,0:T(1,128)}) custom-call(s32[4]{0:T(128)} %pad_add_fusion.owner_ref, bf16[512,512]{1,0:T(8,128)(2,1)} %attend.1.refs_0_, bf16[512,512]{1,0:T(8,128)(2,1)} %copy-done.14, bf16[512,512]{1,0:T(8,128)(2,1)} %copy-done.13, bf16[512,512]{1,0:T(8,128)(2,1)} %copy-done.15, ...), custom_call_target="tpu_custom_call" | custom-call | tf_op jit(solution)/shard_map/blend/pallas_call | solution.py:453
  161.1 23.7 %all_to_all.11 = f32[256,1,128]{2,1,0:T(1,128)S(1)} all-to-all(f32[256,1,128]{2,1,0:T(1,128)S(1)} %broadcast_in_dim.5), channel_id=1, replica_groups=mesh['ctx'=8,'tp'=4,'dp'=8] {'ctx','tp','dp'}, dimensions={0} | all-to-all | bytes 262144 | tf_op jit(solution)/shard_map/all_to_all | solution.py:616
  (113 shorter events, 28.7 us)
Async XLA Ops:
  7.2 144.5 %all-gather.2.cloned.1.call-start = ((), (), s32[]{:S(2)}) async-start(), calls=%async_computation.2 | async-start | bytes 4259840 | tf_op jit(solution)/shard_map/all_gather | solution.py:511
  11.8 7.9 %collective-permute-start = (bf16[64,512]{1,0:T(8,128)(2,1)S(1)}, bf16[64,512]{1,0:T(8,128)(2,1)S(1)}, u32[]{:S(2)}, u32[]{:S(2)}) collective-permute-start(bf16[64,512]{1,0:T(8,128)(2,1)S(1)} %add_convert_fusion.1), channel_id=1, source_target_pairs={{1,0},{0,1},{3,2},{2,3},{5,4},{4,5},{7,6},{6,7},{9,8},{8,9},{11,10... | collective-permute-start | bytes 196616 | tf_op jit(solution)/shard_map/ppermute | solution.py:48
  15.7 11.3 %all-to-all-start = ((bf16[8,64,256]{2,1,0:T(8,128)(2,1)}), bf16[8,64,256]{2,1,0:T(8,128)(2,1)S(1)}, u32[]{:S(2)}, u32[]{:S(2)}) async-start(bf16[8,64,256]{2,1,0:T(8,128)(2,1)} %broadcast_in_dim.4), calls=%async_computation | async-start | bytes 524288 | tf_op jit(solution)/shard_map/all_to_all | solution.py:509
  27.0 12.2 %collective-permute-start.1 = (bf16[768,256]{1,0:T(8,128)(2,1)S(1)}, bf16[768,256]{1,0:T(8,128)(2,1)S(1)}, u32[]{:S(2)}, u32[]{:S(2)}) collective-permute-start(bf16[768,256]{1,0:T(8,128)(2,1)S(1)} %pad_maximum_fusion.refs_2_.refs_0_), channel_id=1, source_target_pairs={{32,0},{33,1},{34,2},{35,3},{36,4},{37,5},{38,6},{39,7},{40,8},{41... | collective-permute-start | bytes 1179656 | tf_op jit(solution)/shard_map/ppermute | solution.py:48
  32.7 9.9 %collective-permute-start.2 = (bf16[768,256]{1,0:T(8,128)(2,1)S(1)}, bf16[768,256]{1,0:T(8,128)(2,1)S(1)}, u32[]{:S(2)}, u32[]{:S(2)}) collective-permute-start(bf16[768,256]{1,0:T(8,128)(2,1)S(1)} %pad_maximum_fusion.refs_2_.refs_0_), channel_id=1, source_target_pairs={{224,0},{225,1},{226,2},{227,3},{228,4},{229,5},{230,6},{231,7},{2... | collective-permute-start | bytes 1179656 | tf_op jit(solution)/shard_map/ppermute | solution.py:48
  42.5 7.9 %collective-permute-start.3 = (bf16[768,256]{1,0:T(8,128)(2,1)S(1)}, bf16[768,256]{1,0:T(8,128)(2,1)S(1)}, u32[]{:S(2)}, u32[]{:S(2)}) collective-permute-start(bf16[768,256]{1,0:T(8,128)(2,1)S(1)} %collective-permute-done.1.refs_3_.refs_1_), channel_id=1, source_target_pairs={{32,0},{33,1},{34,2},{35,3},{36,4},{37,5},{38,6},{39,7},{40,8},{41... | collective-permute-start | bytes 1179656 | tf_op jit(solution)/shard_map/ppermute | solution.py:48
  42.7 8.8 %collective-permute-start.4 = (bf16[768,256]{1,0:T(8,128)(2,1)S(1)}, bf16[768,256]{1,0:T(8,128)(2,1)S(1)}, u32[]{:S(2)}, u32[]{:S(2)}) collective-permute-start(bf16[768,256]{1,0:T(8,128)(2,1)S(1)} %collective-permute-done.2.refs_1_.refs_8_), channel_id=1, source_target_pairs={{224,0},{225,1},{226,2},{227,3},{228,4},{229,5},{230,6},{231,7},{2... | collective-permute-start | bytes 1179656 | tf_op jit(solution)/shard_map/ppermute | solution.py:48
  51.5 9.2 %collective-permute-start.6 = (bf16[768,256]{1,0:T(8,128)(2,1)S(1)}, bf16[768,256]{1,0:T(8,128)(2,1)S(1)}, u32[]{:S(2)}, u32[]{:S(2)}) collective-permute-start(bf16[768,256]{1,0:T(8,128)(2,1)S(1)} %collective-permute-done.4.refs_0_.refs_7_), channel_id=1, source_target_pairs={{224,0},{225,1},{226,2},{227,3},{228,4},{229,5},{230,6},{231,7},{2... | collective-permute-start | bytes 1179656 | tf_op jit(solution)/shard_map/ppermute | solution.py:48
  51.5 9.2 %collective-permute-start.5 = (bf16[768,256]{1,0:T(8,128)(2,1)S(1)}, bf16[768,256]{1,0:T(8,128)(2,1)S(1)}, u32[]{:S(2)}, u32[]{:S(2)}) collective-permute-start(bf16[768,256]{1,0:T(8,128)(2,1)S(1)} %collective-permute-done.3.refs_4_.refs_2_), channel_id=1, source_target_pairs={{32,0},{33,1},{34,2},{35,3},{36,4},{37,5},{38,6},{39,7},{40,8},{41... | collective-permute-start | bytes 1179656 | tf_op jit(solution)/shard_map/ppermute | solution.py:48
  71.0 22.1 %collective-permute-start.13 = (bf16[2048,256]{1,0:T(8,128)(2,1)}, bf16[2048,256]{1,0:T(8,128)(2,1)S(1)}, u32[]{:S(2)}, u32[]{:S(2)}) collective-permute-start(bf16[2048,256]{1,0:T(8,128)(2,1)} %assemble.1.refs_1_), channel_id=1, source_target_pairs={{2,0},{3,1},{4,2},{5,3},{6,4},{7,5},{0,6},{1,7},{10,8},{11,9},{12,... | collective-permute-start | bytes 3145736 | tf_op jit(solution)/shard_map/ppermute | solution.py:48
  71.5 21.9 %collective-permute-start.14 = (bf16[2048,256]{1,0:T(8,128)(2,1)}, bf16[2048,256]{1,0:T(8,128)(2,1)S(1)}, u32[]{:S(2)}, u32[]{:S(2)}) collective-permute-start(bf16[2048,256]{1,0:T(8,128)(2,1)} %assemble.1.refs_1_), channel_id=1, source_target_pairs={{6,0},{7,1},{0,2},{1,3},{2,4},{3,5},{4,6},{5,7},{14,8},{15,9},{8,1... | collective-permute-start | bytes 3145736 | tf_op jit(solution)/shard_map/ppermute | solution.py:48
  76.8 6.7 %collective-permute-start.9 = (bf16[2,528,128]{2,1,0:T(8,128)(2,1)}, bf16[2,528,128]{2,1,0:T(8,128)(2,1)S(1)}, u32[]{:S(2)}, u32[]{:S(2)}) collective-permute-start(bf16[2,528,128]{2,1,0:T(8,128)(2,1)} %pair_last.1.refs_1_), channel_id=1, source_target_pairs={{32,0},{33,1},{34,2},{35,3},{36,4},{37,5},{38,6},{39,7},{40,8},{41... | collective-permute-start | bytes 811016 | tf_op jit(solution)/shard_map/ppermute | solution.py:48
  79.1 7.7 %collective-permute-start.11 = (bf16[2,528,128]{2,1,0:T(8,128)(2,1)}, bf16[2,528,128]{2,1,0:T(8,128)(2,1)S(1)}, u32[]{:S(2)}, u32[]{:S(2)}) collective-permute-start(bf16[2,528,128]{2,1,0:T(8,128)(2,1)} %pair_last.1.refs_1_), channel_id=1, source_target_pairs={{224,0},{225,1},{226,2},{227,3},{228,4},{229,5},{230,6},{231,7},{2... | collective-permute-start | bytes 811016 | tf_op jit(solution)/shard_map/ppermute | solution.py:48
  83.5 12.5 %collective-permute-start.10 = (bf16[2,528,128]{2,1,0:T(8,128)(2,1)S(1)}, bf16[2,528,128]{2,1,0:T(8,128)(2,1)}, u32[]{:S(2)}, u32[]{:S(2)}) collective-permute-start(bf16[2,528,128]{2,1,0:T(8,128)(2,1)S(1)} %collective-permute-done.9.refs_2_), channel_id=1, source_target_pairs={{32,0},{33,1},{34,2},{35,3},{36,4},{37,5},{38,6},{39,7},{40,8},{41... | collective-permute-start | bytes 811016 | tf_op jit(solution)/shard_map/ppermute | solution.py:48
  86.8 9.1 %collective-permute-start.12 = (bf16[2,528,128]{2,1,0:T(8,128)(2,1)S(1)}, bf16[2,528,128]{2,1,0:T(8,128)(2,1)}, u32[]{:S(2)}, u32[]{:S(2)}) collective-permute-start(bf16[2,528,128]{2,1,0:T(8,128)(2,1)S(1)} %collective-permute-done.11.refs_9_), channel_id=1, source_target_pairs={{224,0},{225,1},{226,2},{227,3},{228,4},{229,5},{230,6},{231,7},{2... | collective-permute-start | bytes 811016 | tf_op jit(solution)/shard_map/ppermute | solution.py:48
  94.3 17.4 %collective-permute-start.19 = (bf16[1024,256]{1,0:T(8,128)(2,1)S(1)}, bf16[1024,256]{1,0:T(8,128)(2,1)}, u32[]{:S(2)}, u32[]{:S(2)}) collective-permute-start(bf16[1024,256]{1,0:T(8,128)(2,1)S(1)} %slice.52), channel_id=1, source_target_pairs={{2,0},{3,1},{4,2},{5,3},{6,4},{7,5},{0,6},{1,7},{10,8},{11,9},{12,... | collective-permute-start | bytes 1572872 | tf_op jit(solution)/shard_map/ppermute | solution.py:48
  95.9 15.8 %collective-permute-start.20 = (bf16[1024,256]{1,0:T(8,128)(2,1)}, bf16[1024,256]{1,0:T(8,128)(2,1)}, u32[]{:S(2)}, u32[]{:S(2)}) collective-permute-start(bf16[1024,256]{1,0:T(8,128)(2,1)} %slice.53), channel_id=1, source_target_pairs={{6,0},{7,1},{0,2},{1,3},{2,4},{3,5},{4,6},{5,7},{14,8},{15,9},{8,1... | collective-permute-start | bytes 1572872 | tf_op jit(solution)/shard_map/ppermute | solution.py:48
  95.9 12.1 %collective-permute-start.15 = (bf16[2,528,128]{2,1,0:T(8,128)(2,1)}, bf16[2,528,128]{2,1,0:T(8,128)(2,1)S(1)}, u32[]{:S(2)}, u32[]{:S(2)}) collective-permute-start(bf16[2,528,128]{2,1,0:T(8,128)(2,1)} %collective-permute-done.10.refs_3_), channel_id=1, source_target_pairs={{32,0},{33,1},{34,2},{35,3},{36,4},{37,5},{38,6},{39,7},{40,8},{41... | collective-permute-start | bytes 811016 | tf_op jit(solution)/shard_map/ppermute | solution.py:48
  101.0 8.6 %collective-permute-start.16 = (bf16[2,528,128]{2,1,0:T(8,128)(2,1)}, bf16[2,528,128]{2,1,0:T(8,128)(2,1)S(1)}, u32[]{:S(2)}, u32[]{:S(2)}) collective-permute-start(bf16[2,528,128]{2,1,0:T(8,128)(2,1)} %collective-permute-done.12.refs_8_), channel_id=1, source_target_pairs={{224,0},{225,1},{226,2},{227,3},{228,4},{229,5},{230,6},{231,7},{2... | collective-permute-start | bytes 811016 | tf_op jit(solution)/shard_map/ppermute | solution.py:48
  109.6 7.1 %collective-permute-start.17 = (bf16[1,528,128]{2,1,0:T(8,128)(2,1)S(1)}, bf16[1,528,128]{2,1,0:T(8,128)(2,1)S(1)}, u32[]{:S(2)}, u32[]{:S(2)}) collective-permute-start(bf16[1,528,128]{2,1,0:T(8,128)(2,1)S(1)} %slice.50), channel_id=1, source_target_pairs={{32,0},{33,1},{34,2},{35,3},{36,4},{37,5},{38,6},{39,7},{40,8},{41... | collective-permute-start | bytes 405512 | tf_op jit(solution)/shard_map/ppermute | solution.py:48
  110.8 6.2 %collective-permute-start.18 = (bf16[1,528,128]{2,1,0:T(8,128)(2,1)S(1)}, bf16[1,528,128]{2,1,0:T(8,128)(2,1)S(1)}, u32[]{:S(2)}, u32[]{:S(2)}) collective-permute-start(bf16[1,528,128]{2,1,0:T(8,128)(2,1)S(1)} %slice.51), channel_id=1, source_target_pairs={{224,0},{225,1},{226,2},{227,3},{228,4},{229,5},{230,6},{231,7},{2... | collective-permute-start | bytes 405512 | tf_op jit(solution)/shard_map/ppermute | solution.py:48
  133.8 8.7 %collective-permute-start.22 = (bf16[512,512]{1,0:T(8,128)(2,1)}, bf16[512,512]{1,0:T(8,128)(2,1)S(1)}, u32[]{:S(2)}, u32[]{:S(2)}) collective-permute-start(bf16[512,512]{1,0:T(8,128)(2,1)} %attend.1.refs_0_), channel_id=1, source_target_pairs={{16,0},{17,1},{18,2},{19,3},{20,4},{21,5},{22,6},{23,7},{24,8},{25... | collective-permute-start | bytes 1572872 | tf_op jit(solution)/shard_map/ppermute | solution.py:48
  134.3 17.1 %collective-permute-start.21 = (bf16[512,512]{1,0:T(8,128)(2,1)}, bf16[512,512]{1,0:T(8,128)(2,1)S(1)}, u32[]{:S(2)}, u32[]{:S(2)}) collective-permute-start(bf16[512,512]{1,0:T(8,128)(2,1)} %attend.1.refs_0_), channel_id=1, source_target_pairs={{8,0},{9,1},{10,2},{11,3},{12,4},{13,5},{14,6},{15,7},{0,8},{1,9},... | collective-permute-start | bytes 1572872 | tf_op jit(solution)/shard_map/ppermute | solution.py:48
  142.6 9.1 %collective-permute-start.23 = (bf16[512,512]{1,0:T(8,128)(2,1)S(1)}, bf16[512,512]{1,0:T(8,128)(2,1)S(1)}, u32[]{:S(2)}, u32[]{:S(2)}) collective-permute-start(bf16[512,512]{1,0:T(8,128)(2,1)S(1)} %collective-permute-done.22.refs_2_), channel_id=1, source_target_pairs={{8,0},{9,1},{10,2},{11,3},{12,4},{13,5},{14,6},{15,7},{0,8},{1,9},... | collective-permute-start | bytes 1572872 | tf_op jit(solution)/shard_map/ppermute | solution.py:48
  (23 other events, 214.7 us)
Sparse Core Ops, SparseCore 0:
  11.9 128.9 all-gather.1
